TPU v7x, 32 devices: a whole 2x2x4 slice. The times are simulated.
32 devices in a mesh: ctx: 8 (over z, y), fsdp: 4 (over x, core).
Axes of the slice: x: 2, y: 2, z: 4, core: 2. Of those that a mesh axis runs over, the one named last changes fastest.
Arguments:
- inputs: bfloat16 [16, 1024, 768], P('fsdp', 'ctx'), may hold values from -6 to 6
- query_weight: bfloat16 [768, 3072], P('fsdp'), may hold values from -0.21875 to 0.21875
- kv_weight: bfloat16 [768, 1536], P('fsdp'), may hold values from -0.21875 to 0.21875
- out_weight: bfloat16 [768, 768], P('fsdp'), may hold values from -3 to 3
- up_weight: bfloat16 [768, 3072], P('fsdp'), may hold values from -0.21875 to 0.21875
- down_weight: bfloat16 [3072, 768], P('fsdp'), may hold values from -0.109375 to 0.109375
- query_bias: bfloat16 [3072], P('fsdp'), may hold values from -4 to 4
- value_bias: bfloat16 [768], P('fsdp'), may hold values from -6 to 6
- out_bias: bfloat16 [768], P('fsdp'), may hold values from -4 to 4
- up_bias: bfloat16 [3072], P('fsdp'), may hold values from -4 to 4
- down_bias: bfloat16 [768], P('fsdp'), may hold values from -4 to 4
- norm1_gain: bfloat16 [768], P('fsdp'), may hold values from 0.5 to 1.5
- norm1_shift: bfloat16 [768], P('fsdp'), may hold values from -3 to 3
- norm2_gain: bfloat16 [768], P('fsdp'), may hold values from 0.5 to 1.5
- norm2_shift: bfloat16 [768], P('fsdp'), may hold values from -3 to 3
- types: int32 [16, 1024], P('fsdp'), may hold values 0 or 1
- lengths: int32 [16, 4], P('fsdp'), may hold values from 1 to 960, 1024 in all within a row
- cotangent: bfloat16 [16, 1024, 768], P('fsdp', 'ctx'), may hold values from -6 to 6
Outputs:
- output: bfloat16 [16, 1024, 768], P('fsdp', 'ctx')
- input_grad: bfloat16 [16, 1024, 768], P('fsdp', 'ctx')
- query_weight_grad: float32 [768, 3072], P('fsdp')
- kv_weight_grad: float32 [768, 1536], P('fsdp')
- out_weight_grad: float32 [768, 768], P('fsdp')
- up_weight_grad: float32 [768, 3072], P('fsdp')
- down_weight_grad: float32 [3072, 768], P('fsdp')
- query_bias_grad: float32 [3072], P('fsdp')
- value_bias_grad: float32 [768], P('fsdp')
- out_bias_grad: float32 [768], P('fsdp')
- up_bias_grad: float32 [3072], P('fsdp')
- down_bias_grad: float32 [768], P('fsdp')
- norm1_gain_grad: float32 [768], P('fsdp')
- norm1_shift_grad: float32 [768], P('fsdp')
- norm2_gain_grad: float32 [768], P('fsdp')
- norm2_shift_grad: float32 [768], P('fsdp')
Inputs may be any that keep to these rules, and one draw needn't show every extreme that they name: Each row holds the lengths of 4 documents packed in order into one sequence of 1024 tokens; they sum to 1024, and the largest is exactly 960.
All inputs are finite; a program needn't handle non-finite values. No bound on the sum of `types` on one device may be relied on, other than what follows from the above.
Results may differ from a plain program's by a relative error of at most 0.023.
Values may be sent and summed in bfloat16 or wider, within the bound.
No kernel may reach another device: no remote copies, remote signals or barrier semaphores. Data moves between devices by JAX's collectives and lax.ppermute only.
A program may use at most 256 MiB of HBM per device.

v0:
```python
import jax
import jax.numpy as jnp
from jax import lax
from jax.sharding import PartitionSpec as P

HEADS = 12
MB = 4


EPSILON = 1e-05
MASKED = -1e30


def matmul(left_mat, right_mat):
    return jnp.dot(left_mat, right_mat, preferred_element_type=jnp.float32)


def rows_inner(left_mat, right_mat):
    return lax.dot_general(
        left_mat, right_mat, (((0,), (0,)), ((), ())), preferred_element_type=jnp.float32
    )


def times_transposed(left_mat, right_mat):
    return lax.dot_general(
        left_mat, right_mat, (((1,), (1,)), ((), ())), preferred_element_type=jnp.float32
    )


def normalize(values, gain_vec, shift_vec):
    center = values - jnp.mean(values, axis=-1, keepdims=True)
    scale_inv = lax.rsqrt(jnp.mean(center * center, axis=-1, keepdims=True) + EPSILON)
    normed = center * scale_inv
    return (normed * gain_vec + shift_vec, normed, scale_inv)


def normalize_back(grad_in, normed, scale_inv, gain_vec):
    scaled = grad_in * gain_vec
    inner_part = (
        scaled
        - jnp.mean(scaled, axis=-1, keepdims=True)
        - normed * jnp.mean(scaled * normed, axis=-1, keepdims=True)
    )
    return (inner_part * scale_inv, jnp.sum(grad_in * normed, axis=0), jnp.sum(grad_in, axis=0))


def column_sum(values):
    return jnp.sum(values.astype(jnp.float32), axis=0)


def pair_slice(values, col_start, pair_width, head_dim):
    seq_count, length_here = values.shape[:2]
    part = lax.dynamic_slice_in_dim(values, col_start, pair_width, 2)
    return part.reshape(seq_count, length_here, pair_width // head_dim, head_dim)


def pair_scores(q_word, q_ent, all_keys, key_entity, same_doc, col_start, pair_width, head_dim):
    word_part = pair_slice(q_word, col_start, pair_width, head_dim)
    ent_part = pair_slice(q_ent, col_start, pair_width, head_dim)
    key_part = pair_slice(all_keys, col_start, pair_width, head_dim)
    word_score_matrix = jnp.einsum(
        "sqhd,skhd->shqk", word_part, key_part, preferred_element_type=jnp.float32
    )
    entity_score_matrix = jnp.einsum(
        "sqhd,skhd->shqk", ent_part, key_part, preferred_element_type=jnp.float32
    )
    scores = head_dim ** (-0.5) * jnp.where(
        key_entity[:, None, None, :], entity_score_matrix, word_score_matrix
    )
    return (jnp.where(same_doc[:, None], scores, MASKED), word_part, ent_part, key_part)


def attend(q_word, q_ent, all_keys, all_vals, key_entity, same_doc, head_dim):
    seq_count, own_span, model_width = q_word.shape
    pair_width = 2 * head_dim

    def one_pair(pair_index, loop_state):
        attended, log_total = loop_state
        col_start = pair_index * pair_width
        scores, word_part, ent_part, key_part = pair_scores(
            q_word, q_ent, all_keys, key_entity, same_doc, col_start, pair_width, head_dim
        )
        val_part = pair_slice(all_vals, col_start, pair_width, head_dim)
        row_top = jnp.max(scores, axis=-1, keepdims=True)
        weights = jnp.exp(scores - row_top)
        row_totals = jnp.sum(weights, axis=-1, keepdims=True)
        probs_low = (weights / row_totals).astype(jnp.bfloat16)
        mixed_heads = jnp.einsum(
            "shqk,skhd->sqhd", probs_low, val_part, preferred_element_type=jnp.float32
        )
        attended = lax.dynamic_update_slice_in_dim(
            attended,
            mixed_heads.reshape(seq_count, own_span, pair_width).astype(jnp.bfloat16),
            col_start,
            2,
        )
        log_total = lax.dynamic_update_slice_in_dim(
            log_total, (row_top + jnp.log(row_totals))[..., 0], pair_index * 2, 1
        )
        return (attended, log_total)

    start_state = (
        jnp.zeros((seq_count, own_span, model_width), jnp.bfloat16),
        jnp.zeros((seq_count, model_width // head_dim, own_span), jnp.float32),
    )
    return lax.fori_loop(0, model_width // pair_width, one_pair, start_state)


def attend_back(
    q_word, q_ent, all_keys, all_vals, key_entity, same_doc, log_total, grad_attended, head_dim
):
    seq_count, own_span, model_width = q_word.shape
    full_len = all_keys.shape[1]
    pair_width = 2 * head_dim
    score_scale = head_dim ** (-0.5)

    def one_pair(pair_index, loop_state):
        grad_word, grad_ent, grad_keys, grad_vals = loop_state
        col_start = pair_index * pair_width
        scores, word_part, ent_part, key_part = pair_scores(
            q_word, q_ent, all_keys, key_entity, same_doc, col_start, pair_width, head_dim
        )
        val_part = pair_slice(all_vals, col_start, pair_width, head_dim)
        out_part = pair_slice(grad_attended, col_start, pair_width, head_dim)
        lse_part = lax.dynamic_slice_in_dim(log_total, pair_index * 2, 2, 1)
        probs = jnp.exp(scores - lse_part[..., None])
        grad_probs = jnp.einsum(
            "sqhd,skhd->shqk", out_part, val_part, preferred_element_type=jnp.float32
        )
        row_delta = jnp.sum(probs * grad_probs, axis=-1, keepdims=True)
        grad_scores = (probs * (grad_probs - row_delta)).astype(jnp.bfloat16)
        zero_low = jnp.zeros((), jnp.bfloat16)
        key_mask = key_entity[:, None, None, :]
        to_word = jnp.where(key_mask, zero_low, grad_scores)
        to_ent = jnp.where(key_mask, grad_scores, zero_low)
        word_q = score_scale * jnp.einsum(
            "shqk,skhd->sqhd", to_word, key_part, preferred_element_type=jnp.float32
        )
        ent_q = score_scale * jnp.einsum(
            "shqk,skhd->sqhd", to_ent, key_part, preferred_element_type=jnp.float32
        )
        key_grad = score_scale * (
            jnp.einsum("shqk,sqhd->skhd", to_word, word_part, preferred_element_type=jnp.float32)
            + jnp.einsum("shqk,sqhd->skhd", to_ent, ent_part, preferred_element_type=jnp.float32)
        )
        val_grad = jnp.einsum(
            "shqk,sqhd->skhd",
            probs.astype(jnp.bfloat16),
            out_part,
            preferred_element_type=jnp.float32,
        )
        grad_word = lax.dynamic_update_slice_in_dim(
            grad_word, word_q.reshape(seq_count, own_span, pair_width), col_start, 2
        )
        grad_ent = lax.dynamic_update_slice_in_dim(
            grad_ent, ent_q.reshape(seq_count, own_span, pair_width), col_start, 2
        )
        grad_keys = lax.dynamic_update_slice_in_dim(
            grad_keys, key_grad.reshape(seq_count, full_len, pair_width), col_start, 2
        )
        grad_vals = lax.dynamic_update_slice_in_dim(
            grad_vals, val_grad.reshape(seq_count, full_len, pair_width), col_start, 2
        )
        return (grad_word, grad_ent, grad_keys, grad_vals)

    own_zeros = jnp.zeros((seq_count, own_span, model_width), jnp.float32)
    full_zeros = jnp.zeros((seq_count, full_len, model_width), jnp.float32)
    return lax.fori_loop(
        0, model_width // pair_width, one_pair, (own_zeros, own_zeros, full_zeros, full_zeros)
    )


def fetch_weights(parts):
    return (
        lax.all_gather(parts[0], "fsdp", axis=0, tiled=True),
        lax.all_gather(parts[1], "fsdp", axis=0, tiled=True),
        lax.all_gather(parts[2], "fsdp", axis=0, tiled=True),
        lax.all_gather(parts[3], "fsdp", axis=0, tiled=True),
        lax.all_gather(parts[4], "fsdp", axis=0, tiled=True),
        lax.all_gather(parts[5], "fsdp", axis=0, tiled=True),
        lax.all_gather(parts[6], "fsdp", axis=0, tiled=True),
        lax.all_gather(parts[7], "fsdp", axis=0, tiled=True),
        lax.all_gather(parts[8], "fsdp", axis=0, tiled=True),
        lax.all_gather(parts[9], "fsdp", axis=0, tiled=True),
        lax.all_gather(parts[10], "fsdp", axis=0, tiled=True),
        lax.all_gather(parts[11], "fsdp", axis=0, tiled=True),
        lax.all_gather(parts[12], "fsdp", axis=0, tiled=True),
        lax.all_gather(parts[13], "fsdp", axis=0, tiled=True),
    )


def scatter_parts(parts):
    return (
        lax.psum_scatter(
            parts[0].astype(jnp.bfloat16), "fsdp", scatter_dimension=0, tiled=True
        ).astype(jnp.float32),
        lax.psum_scatter(
            parts[1].astype(jnp.bfloat16), "fsdp", scatter_dimension=0, tiled=True
        ).astype(jnp.float32),
        lax.psum_scatter(
            parts[2].astype(jnp.bfloat16), "fsdp", scatter_dimension=0, tiled=True
        ).astype(jnp.float32),
        lax.psum_scatter(
            parts[3].astype(jnp.bfloat16), "fsdp", scatter_dimension=0, tiled=True
        ).astype(jnp.float32),
        lax.psum_scatter(
            parts[4].astype(jnp.bfloat16), "fsdp", scatter_dimension=0, tiled=True
        ).astype(jnp.float32),
        lax.psum_scatter(
            parts[5].astype(jnp.bfloat16), "fsdp", scatter_dimension=0, tiled=True
        ).astype(jnp.float32),
        lax.psum_scatter(
            parts[6].astype(jnp.bfloat16), "fsdp", scatter_dimension=0, tiled=True
        ).astype(jnp.float32),
        lax.psum_scatter(
            parts[7].astype(jnp.bfloat16), "fsdp", scatter_dimension=0, tiled=True
        ).astype(jnp.float32),
        lax.psum_scatter(
            parts[8].astype(jnp.bfloat16), "fsdp", scatter_dimension=0, tiled=True
        ).astype(jnp.float32),
        lax.psum_scatter(
            parts[9].astype(jnp.bfloat16), "fsdp", scatter_dimension=0, tiled=True
        ).astype(jnp.float32),
        lax.psum_scatter(
            parts[10].astype(jnp.bfloat16), "fsdp", scatter_dimension=0, tiled=True
        ).astype(jnp.float32),
        lax.psum_scatter(
            parts[11].astype(jnp.bfloat16), "fsdp", scatter_dimension=0, tiled=True
        ).astype(jnp.float32),
        lax.psum_scatter(
            parts[12].astype(jnp.bfloat16), "fsdp", scatter_dimension=0, tiled=True
        ).astype(jnp.float32),
        lax.psum_scatter(
            parts[13].astype(jnp.bfloat16), "fsdp", scatter_dimension=0, tiled=True
        ).astype(jnp.float32),
    )


def body(
    inputs,
    query_weight,
    kv_weight,
    out_weight,
    up_weight,
    down_weight,
    query_bias,
    value_bias,
    out_bias,
    up_bias,
    down_bias,
    norm1_gain,
    norm1_shift,
    norm2_gain,
    norm2_shift,
    types,
    lengths,
    cotangent,
):
    seq_count, own_span, model_width = inputs.shape
    head_dim = model_width // HEADS
    per_micro = seq_count // MB
    full_len = own_span * lax.axis_size("ctx")
    offset = lax.axis_index("ctx") * own_span
    doc_ends = jnp.cumsum(lengths, axis=1)
    positions = jnp.arange(full_len, dtype=jnp.int32)
    seg_all = jnp.sum((positions[None, :, None] >= doc_ends[:, None, :]).astype(jnp.int32), axis=-1)
    seg_own = lax.dynamic_slice_in_dim(seg_all, offset, own_span, 1)
    types_own = lax.dynamic_slice_in_dim(types, offset, own_span, 1)
    shards = (
        query_weight,
        kv_weight,
        out_weight,
        up_weight,
        down_weight,
        query_bias,
        value_bias,
        out_bias,
        up_bias,
        down_bias,
        norm1_gain,
        norm1_shift,
        norm2_gain,
        norm2_shift,
    )
    results = []
    input_grads = []
    shard_sums = None
    for micro_idx in range(MB):
        row_first = micro_idx * per_micro
        row_last = row_first + per_micro
        gathered = fetch_weights(shards)
        (
            w_query,
            w_kv,
            w_out,
            w_up,
            w_down,
            b_query,
            b_value,
            b_out,
            b_up,
            b_down,
            g_one,
            s_one,
            g_two,
            s_two,
        ) = gathered
        flat_rows = inputs[row_first:row_last].reshape(-1, model_width)
        entity_rows = (types_own[row_first:row_last] > 0).reshape(-1, 1)
        query_all = matmul(flat_rows, w_query) + b_query.astype(jnp.float32)
        q_word_flat = jnp.where(
            entity_rows, query_all[:, 2 * model_width : 3 * model_width], query_all[:, :model_width]
        ).astype(jnp.bfloat16)
        q_ent_flat = jnp.where(
            entity_rows,
            query_all[:, 3 * model_width :],
            query_all[:, model_width : 2 * model_width],
        ).astype(jnp.bfloat16)
        key_val = matmul(flat_rows, w_kv)
        key_rows = (
            key_val[:, :model_width].astype(jnp.bfloat16).reshape(per_micro, own_span, model_width)
        )
        val_rows = (
            (key_val[:, model_width:] + b_value.astype(jnp.float32))
            .astype(jnp.bfloat16)
            .reshape(per_micro, own_span, model_width)
        )
        all_keys, all_vals = (
            lax.all_gather(key_rows, "ctx", axis=1, tiled=True),
            lax.all_gather(val_rows, "ctx", axis=1, tiled=True),
        )
        key_entity = types[row_first:row_last] > 0
        same_doc = (
            seg_own[row_first:row_last][:, :, None] == seg_all[row_first:row_last][:, None, :]
        )
        q_word = q_word_flat.reshape(per_micro, own_span, model_width)
        q_ent = q_ent_flat.reshape(per_micro, own_span, model_width)
        attended, log_total = attend(
            q_word, q_ent, all_keys, all_vals, key_entity, same_doc, head_dim
        )
        attended_flat = attended.reshape(-1, model_width)
        attn_out = matmul(attended_flat, w_out) + b_out.astype(jnp.float32)
        gain_one = g_one.astype(jnp.float32)
        gain_two = g_two.astype(jnp.float32)
        hidden, normed_one, inv_one = normalize(
            flat_rows.astype(jnp.float32) + attn_out, gain_one, s_one.astype(jnp.float32)
        )
        hidden_low = hidden.astype(jnp.bfloat16)
        up_proj = matmul(hidden_low, w_up) + b_up.astype(jnp.float32)
        gelu_out, gelu_pull = jax.vjp(
            lambda value_in: jax.nn.gelu(value_in, approximate=False), up_proj
        )
        act_low = gelu_out.astype(jnp.bfloat16)
        ffn_out = matmul(act_low, w_down) + b_down.astype(jnp.float32)
        result, normed_two, inv_two = normalize(
            hidden + ffn_out, gain_two, s_two.astype(jnp.float32)
        )
        results.append(result.astype(jnp.bfloat16).reshape(per_micro, own_span, model_width))
        grad_result = cotangent[row_first:row_last].reshape(-1, model_width).astype(jnp.float32)
        grad_y2, grad_g2, grad_s2 = normalize_back(grad_result, normed_two, inv_two, gain_two)
        grad_ffn = grad_y2.astype(jnp.bfloat16)
        grad_w_down = rows_inner(act_low, grad_ffn)
        grad_b_down = column_sum(grad_ffn)
        grad_act = times_transposed(grad_ffn, w_down)
        grad_up = gelu_pull(grad_act)[0].astype(jnp.bfloat16)
        grad_w_up = rows_inner(hidden_low, grad_up)
        grad_b_up = column_sum(grad_up)
        grad_hidden = grad_y2 + times_transposed(grad_up, w_up)
        grad_y1, grad_g1, grad_s1 = normalize_back(grad_hidden, normed_one, inv_one, gain_one)
        grad_attn = grad_y1.astype(jnp.bfloat16)
        grad_w_out = rows_inner(attended_flat, grad_attn)
        grad_b_out = column_sum(grad_attn)
        grad_attended = (
            times_transposed(grad_attn, w_out)
            .astype(jnp.bfloat16)
            .reshape(per_micro, own_span, model_width)
        )
        grad_word, grad_ent, grad_keys, grad_vals = attend_back(
            q_word,
            q_ent,
            all_keys,
            all_vals,
            key_entity,
            same_doc,
            log_total,
            grad_attended,
            head_dim,
        )
        keys_own, vals_own = (
            lax.psum_scatter(
                grad_keys.astype(jnp.bfloat16), "ctx", scatter_dimension=1, tiled=True
            ).astype(jnp.float32),
            lax.psum_scatter(
                grad_vals.astype(jnp.bfloat16), "ctx", scatter_dimension=1, tiled=True
            ).astype(jnp.float32),
        )
        grad_kv = jnp.concatenate(
            [keys_own.reshape(-1, model_width), vals_own.reshape(-1, model_width)], axis=1
        ).astype(jnp.bfloat16)
        grad_w_kv = rows_inner(flat_rows, grad_kv)
        grad_b_value = column_sum(grad_kv[:, model_width:])
        word_low = grad_word.reshape(-1, model_width).astype(jnp.bfloat16)
        ent_low = grad_ent.reshape(-1, model_width).astype(jnp.bfloat16)
        zero_rows = jnp.zeros_like(word_low)
        grad_query = jnp.concatenate(
            [
                jnp.where(entity_rows, zero_rows, word_low),
                jnp.where(entity_rows, zero_rows, ent_low),
                jnp.where(entity_rows, word_low, zero_rows),
                jnp.where(entity_rows, ent_low, zero_rows),
            ],
            axis=1,
        )
        grad_w_query = rows_inner(flat_rows, grad_query)
        grad_b_query = column_sum(grad_query)
        grad_input = (
            grad_y1 + times_transposed(grad_query, w_query) + times_transposed(grad_kv, w_kv)
        )
        input_grads.append(
            grad_input.astype(jnp.bfloat16).reshape(per_micro, own_span, model_width)
        )
        grads_here = (
            grad_w_query,
            grad_w_kv,
            grad_w_out,
            grad_w_up,
            grad_w_down,
            grad_b_query,
            grad_b_value,
            grad_b_out,
            grad_b_up,
            grad_b_down,
            grad_g1,
            grad_s1,
            grad_g2,
            grad_s2,
        )
        scattered = scatter_parts(grads_here)
        shard_sums = (
            scattered if shard_sums is None else jax.tree.map(jnp.add, shard_sums, scattered)
        )
    totals = (
        lax.psum(shard_sums[0].astype(jnp.bfloat16), "ctx").astype(jnp.float32),
        lax.psum(shard_sums[1].astype(jnp.bfloat16), "ctx").astype(jnp.float32),
        lax.psum(shard_sums[2].astype(jnp.bfloat16), "ctx").astype(jnp.float32),
        lax.psum(shard_sums[3].astype(jnp.bfloat16), "ctx").astype(jnp.float32),
        lax.psum(shard_sums[4].astype(jnp.bfloat16), "ctx").astype(jnp.float32),
        lax.psum(shard_sums[5].astype(jnp.bfloat16), "ctx").astype(jnp.float32),
        lax.psum(shard_sums[6].astype(jnp.bfloat16), "ctx").astype(jnp.float32),
        lax.psum(shard_sums[7].astype(jnp.bfloat16), "ctx").astype(jnp.float32),
        lax.psum(shard_sums[8].astype(jnp.bfloat16), "ctx").astype(jnp.float32),
        lax.psum(shard_sums[9].astype(jnp.bfloat16), "ctx").astype(jnp.float32),
        lax.psum(shard_sums[10].astype(jnp.bfloat16), "ctx").astype(jnp.float32),
        lax.psum(shard_sums[11].astype(jnp.bfloat16), "ctx").astype(jnp.float32),
        lax.psum(shard_sums[12].astype(jnp.bfloat16), "ctx").astype(jnp.float32),
        lax.psum(shard_sums[13].astype(jnp.bfloat16), "ctx").astype(jnp.float32),
    )
    return (
        jnp.concatenate(results, axis=0),
        jnp.concatenate(input_grads, axis=0),
        totals[0],
        totals[1],
        totals[2],
        totals[3],
        totals[4],
        totals[5],
        totals[6],
        totals[7],
        totals[8],
        totals[9],
        totals[10],
        totals[11],
        totals[12],
        totals[13],
    )


def solution(mesh):
    in_specs = (
        P("fsdp", "ctx", None),
        P("fsdp", None),
        P("fsdp", None),
        P("fsdp", None),
        P("fsdp", None),
        P("fsdp", None),
        P("fsdp"),
        P("fsdp"),
        P("fsdp"),
        P("fsdp"),
        P("fsdp"),
        P("fsdp"),
        P("fsdp"),
        P("fsdp"),
        P("fsdp"),
        P("fsdp", None),
        P("fsdp", None),
        P("fsdp", "ctx", None),
    )
    out_specs = (
        P("fsdp", "ctx", None),
        P("fsdp", "ctx", None),
        P("fsdp", None),
        P("fsdp", None),
        P("fsdp", None),
        P("fsdp", None),
        P("fsdp", None),
        P("fsdp"),
        P("fsdp"),
        P("fsdp"),
        P("fsdp"),
        P("fsdp"),
        P("fsdp"),
        P("fsdp"),
        P("fsdp"),
        P("fsdp"),
    )
    return jax.shard_map(body, mesh=mesh, in_specs=in_specs, out_specs=out_specs, check_vma=False)
```

profile of v0, /device:TPU:0, one launch (start us, length us, event | category | flops | bytes accessed | tf_op | source)
XLA Modules:
  0.0 2694.9 jit_solution(3075766283982143089)
XLA Ops:
  15.0 13.1 all-reduce.46
  28.1 8.4 all-gather.24.cloned.1.call-done
  52.3 5.2 all-gather.8
  58.7 5.3 all-gather.9
  65.8 20.0 all-gather.46.cloned.1.call-done
  88.4 43.2 %all-gather.48.cloned.1.call-done = bf16[1024,768]{1,0:T(8,128)(2,1)} async-done(((bf16[128,768]{1,0:T(8,128)(2,1)}), bf16[1024,768]{1,0:T(8,128)(2,1)}) %all-gather.48.cloned.1.call-update) | async-done | bytes 1572880 | tf_op jit(solution)/shard_map/all_gather | solution.py:329
  134.2 43.1 %all-gather.38.cloned.1.call-done = bf16[1024,768]{1,0:T(8,128)(2,1)} async-done(((bf16[128,768]{1,0:T(8,128)(2,1)}), bf16[1024,768]{1,0:T(8,128)(2,1)}) %all-gather.38.cloned.1.call-update) | async-done | bytes 1572880 | tf_op jit(solution)/shard_map/all_gather | solution.py:330
  179.8 42.5 %all-gather.40.cloned.1.call-done = bf16[1024,768]{1,0:T(8,128)(2,1)} async-done(((bf16[128,768]{1,0:T(8,128)(2,1)}), bf16[1024,768]{1,0:T(8,128)(2,1)}) %all-gather.40.cloned.1.call-update) | async-done | bytes 1572880 | tf_op jit(solution)/shard_map/all_gather | solution.py:329
  224.9 43.0 %all-gather.42.cloned.1.call-done = bf16[1024,768]{1,0:T(8,128)(2,1)} async-done(((bf16[128,768]{1,0:T(8,128)(2,1)}), bf16[1024,768]{1,0:T(8,128)(2,1)}) %all-gather.42.cloned.1.call-update) | async-done | bytes 1572880 | tf_op jit(solution)/shard_map/all_gather | solution.py:330
  270.5 42.6 %all-gather.44.cloned.1.call-done = bf16[1024,768]{1,0:T(8,128)(2,1)} async-done(((bf16[128,768]{1,0:T(8,128)(2,1)}), bf16[1024,768]{1,0:T(8,128)(2,1)}) %all-gather.44.cloned.1.call-update) | async-done | bytes 1572880 | tf_op jit(solution)/shard_map/all_gather | solution.py:329
  315.7 43.2 %all-gather.34.cloned.1.call-done = bf16[1024,768]{1,0:T(8,128)(2,1)} async-done(((bf16[128,768]{1,0:T(8,128)(2,1)}), bf16[1024,768]{1,0:T(8,128)(2,1)}) %all-gather.34.cloned.1.call-update) | async-done | bytes 1572880 | tf_op jit(solution)/shard_map/all_gather | solution.py:330
  361.5 43.2 %all-gather.36.cloned.1.call-done = bf16[1024,768]{1,0:T(8,128)(2,1)} async-done(((bf16[128,768]{1,0:T(8,128)(2,1)}), bf16[1024,768]{1,0:T(8,128)(2,1)}) %all-gather.36.cloned.1.call-update) | async-done | bytes 1572880 | tf_op jit(solution)/shard_map/all_gather | solution.py:329
  407.3 35.1 %all-gather.26.cloned.1.call-done = bf16[768,3072]{1,0:T(8,128)(2,1)} async-done(((bf16[192,3072]{1,0:T(8,128)(2,1)}), bf16[768,3072]{1,0:T(8,128)(2,1)}) %all-gather.26.cloned.1.call-update) | async-done | bytes 4718608 | tf_op jit(solution)/shard_map/all_gather | solution.py:175
  448.6 60.2 %while.147 = (s32[]{:T(128)}, bf16[1,128,768]{1,2,0:T(8,128)(2,1)}, f32[1,12,128]{2,1,0:T(8,128)}, bf16[1,1024,768]{1,2,0:T(8,128)(2,1)}, pred[1,1024]{1,0:T(4,1...) while((s32[]{:T(128)}, bf16[1,128,768]{1,2,0:T(8,128)(2,1)}, ...), condition=%wide.region_29.30_spmd.clone, body=%wide.region_26.29_spmd.clone.sunk | while | flops 103169792 | bytes 7655206 | solution.py:106
  511.0 8.7 multiply_convert_fusion
  519.6 19.8 all-gather.32.cloned.1.call-done
  549.7 70.6 %while.145 = (s32[]{:T(128)}, bf16[1,128,768]{1,2,0:T(8,128)(2,1)}, f32[1,12,128]{2,1,0:T(8,128)}, bf16[1,1024,768]{1,2,0:T(8,128)(2,1)}, pred[1,1024]{1,0:T(4,1...) while((s32[]{:T(128)}, bf16[1,128,768]{1,2,0:T(8,128)(2,1)}, ...), condition=%wide.region_13.14_spmd.clone, body=%wide.region_10.13_spmd.clone.sunk | while | flops 103169792 | bytes 7655206 | solution.py:106
  622.2 9.5 multiply_convert_fusion.2
  638.4 70.3 %while.146 = (s32[]{:T(128)}, bf16[1,128,768]{1,2,0:T(8,128)(2,1)}, f32[1,12,128]{2,1,0:T(8,128)}, bf16[1,1024,768]{1,2,0:T(8,128)(2,1)}, pred[1,1024]{1,0:T(4,1...) while((s32[]{:T(128)}, bf16[1,128,768]{1,2,0:T(8,128)(2,1)}, ...), condition=%wide.region_21.22_spmd.clone, body=%wide.region_18.21_spmd.clone.sunk | while | flops 103169792 | bytes 7655206 | solution.py:106
  710.6 8.5 multiply_convert_fusion.1
  726.7 47.0 %while.144 = (s32[]{:T(128)}, bf16[1,128,768]{1,2,0:T(8,128)(2,1)}, f32[1,12,128]{2,1,0:T(8,128)}, bf16[1,1024,768]{1,2,0:T(8,128)(2,1)}, pred[1,1024]{1,0:T(4,1...) while((s32[]{:T(128)}, bf16[1,128,768]{1,2,0:T(8,128)(2,1)}, ...), condition=%wide.region_5.6_spmd.clone, body=%wide.region_2.5_spmd.clone.sunk | while | flops 103169792 | bytes 7651082 | solution.py:106
  775.9 6.0 multiply_convert_fusion.3
  815.4 146.1 %while.148 = (s32[]{:T(128)}, bf16[1,128,768]{2,1,0:T(8,128)(2,1)}, bf16[1,128,768]{2,1,0:T(8,128)(2,1)}, bf16[1,1024,768]{1,2,0:T(8,128)(2,1)}, bf16[1,1024,768...) while((s32[]{:T(128)}, bf16[1,128,768]{2,1,0:T(8,128)(2,1)}, ...), condition=%wide.region_40.41_spmd.clone, body=%wide.region_38.40_spmd.clone.sunk | while | flops 275584000 | bytes 19811184 | solution.py:168
  961.5 8.4 copy.174
  974.7 5.7 copy.172
  990.1 145.7 %while.149 = (s32[]{:T(128)}, bf16[1,128,768]{2,1,0:T(8,128)(2,1)}, bf16[1,128,768]{2,1,0:T(8,128)(2,1)}, bf16[1,1024,768]{1,2,0:T(8,128)(2,1)}, bf16[1,1024,768...) while((s32[]{:T(128)}, bf16[1,128,768]{2,1,0:T(8,128)(2,1)}, ...), condition=%wide.region_49.50_spmd.clone, body=%wide.region_47.49_spmd.clone.sunk | while | flops 275584000 | bytes 19811184 | solution.py:168
  1135.8 8.4 copy.178
  1149.0 5.7 copy.176
  1164.4 142.3 %while.150 = (s32[]{:T(128)}, bf16[1,128,768]{2,1,0:T(8,128)(2,1)}, bf16[1,128,768]{2,1,0:T(8,128)(2,1)}, bf16[1,1024,768]{1,2,0:T(8,128)(2,1)}, bf16[1,1024,768...) while((s32[]{:T(128)}, bf16[1,128,768]{2,1,0:T(8,128)(2,1)}, ...), condition=%wide.region_58.59_spmd.clone, body=%wide.region_56.58_spmd.clone.sunk | while | flops 275584000 | bytes 19807060 | solution.py:168
  1306.7 8.4 copy.182
  1319.8 5.7 copy.180
  1333.1 71.0 %while.151 = (s32[]{:T(128)}, bf16[1,128,768]{2,1,0:T(8,128)(2,1)S(1)}, bf16[1,128,768]{2,1,0:T(8,128)(2,1)S(1)}, bf16[1,1024,768]{1,2,0:T(8,128)(2,1)}, bf16[1,...) while((s32[]{:T(128)}, ...), condition=%wide.region_67.68_spmd.clone, body=%wide.region_65.67_spmd.clone.sunk | while | flops 275584000 | bytes 19675960 | solution.py:168
  1405.5 7.2 copy.186
  1414.2 7.2 copy.184
  1458.7 59.6 %reduce-scatter.99.cloned.1.call-done = bf16[128,768]{1,0:T(8,128)(2,1)} async-done(((bf16[1024,768]{1,0:T(8,128)(2,1)}), bf16[128,768]{1,0:T(8,128)(2,1)}) %reduce-scatter.99.cloned.1.call-update) | async-done | bytes 196624
  1521.3 65.1 %reduce-scatter.97.cloned.1.call-done = bf16[128,768]{1,0:T(8,128)(2,1)} async-done(((bf16[1024,768]{1,0:T(8,128)(2,1)}), bf16[128,768]{1,0:T(8,128)(2,1)}) %reduce-scatter.97.cloned.1.call-update) | async-done | bytes 196624
  1597.6 6.6 copy.188
  1609.0 6.6 copy.190
  1621.7 6.7 copy.192
  1634.5 6.7 copy.194
  1686.1 13.2 reduce-scatter.61.cloned.1.call-done
  1701.6 33.1 %reduce-scatter.109.cloned.1.call-done = bf16[192,1536]{1,0:T(8,128)(2,1)} async-done(((bf16[768,1536]{1,0:T(8,128)(2,1)}), bf16[192,1536]{1,0:T(8,128)(2,1)}) %reduce-scatter.109.cloned.1.call-update) | async-done | bytes 589840
  1736.1 34.9 %reduce-scatter.111.cloned.1.call-done = bf16[192,1536]{1,0:T(8,128)(2,1)} async-done(((bf16[768,1536]{1,0:T(8,128)(2,1)}), bf16[192,1536]{1,0:T(8,128)(2,1)}) %reduce-scatter.111.cloned.1.call-update) | async-done | bytes 589840
  1772.3 34.9 %reduce-scatter.113.cloned.1.call-done = bf16[192,1536]{1,0:T(8,128)(2,1)} async-done(((bf16[768,1536]{1,0:T(8,128)(2,1)}), bf16[192,1536]{1,0:T(8,128)(2,1)}) %reduce-scatter.113.cloned.1.call-update) | async-done | bytes 589840
  1808.5 35.0 %reduce-scatter.115.cloned.1.call-done = bf16[192,1536]{1,0:T(8,128)(2,1)} async-done(((bf16[768,1536]{1,0:T(8,128)(2,1)}), bf16[192,1536]{1,0:T(8,128)(2,1)}) %reduce-scatter.115.cloned.1.call-update) | async-done | bytes 589840
  1846.1 47.7 %reduce-scatter.101.cloned.1.call-done = bf16[192,3072]{1,0:T(8,128)(2,1)} async-done(((bf16[768,3072]{1,0:T(8,128)(2,1)}), bf16[192,3072]{1,0:T(8,128)(2,1)}) %reduce-scatter.101.cloned.1.call-update) | async-done | bytes 1179664
  1895.4 48.9 %reduce-scatter.103.cloned.1.call-done = bf16[192,3072]{1,0:T(8,128)(2,1)} async-done(((bf16[768,3072]{1,0:T(8,128)(2,1)}), bf16[192,3072]{1,0:T(8,128)(2,1)}) %reduce-scatter.103.cloned.1.call-update) | async-done | bytes 1179664
  1946.0 48.8 %reduce-scatter.105.cloned.1.call-done = bf16[192,3072]{1,0:T(8,128)(2,1)} async-done(((bf16[768,3072]{1,0:T(8,128)(2,1)}), bf16[192,3072]{1,0:T(8,128)(2,1)}) %reduce-scatter.105.cloned.1.call-update) | async-done | bytes 1179664
  1997.3 47.9 %reduce-scatter.107.cloned.1.call-done = bf16[192,3072]{1,0:T(8,128)(2,1)} async-done(((bf16[768,3072]{1,0:T(8,128)(2,1)}), bf16[192,3072]{1,0:T(8,128)(2,1)}) %reduce-scatter.107.cloned.1.call-update) | async-done | bytes 1179664
  2051.5 44.1 %reduce-scatter.71.cloned.1.call-done = bf16[192,3072]{1,0:T(8,128)(2,1)} async-done(((bf16[768,3072]{1,0:T(8,128)(2,1)}), bf16[192,3072]{1,0:T(8,128)(2,1)}) %reduce-scatter.71.cloned.1.call-update) | async-done | bytes 1179664 | tf_op jit(solution)/shard_map/reduce_scatter | solution.py:203
  2095.6 50.6 %reduce-scatter.73.cloned.1.call-done = bf16[192,3072]{1,0:T(8,128)(2,1)} async-done(((bf16[768,3072]{1,0:T(8,128)(2,1)}), bf16[192,3072]{1,0:T(8,128)(2,1)}) %reduce-scatter.73.cloned.1.call-update) | async-done | bytes 1179664 | tf_op jit(solution)/shard_map/reduce_scatter | solution.py:203
  2146.2 50.3 %reduce-scatter.75.cloned.1.call-done = bf16[192,3072]{1,0:T(8,128)(2,1)} async-done(((bf16[768,3072]{1,0:T(8,128)(2,1)}), bf16[192,3072]{1,0:T(8,128)(2,1)}) %reduce-scatter.75.cloned.1.call-update) | async-done | bytes 1179664 | tf_op jit(solution)/shard_map/reduce_scatter | solution.py:203
  2196.5 50.4 %reduce-scatter.69.cloned.1.call-done = bf16[192,3072]{1,0:T(8,128)(2,1)} async-done(((bf16[768,3072]{1,0:T(8,128)(2,1)}), bf16[192,3072]{1,0:T(8,128)(2,1)}) %reduce-scatter.69.cloned.1.call-update) | async-done | bytes 1179664 | tf_op jit(solution)/shard_map/reduce_scatter | solution.py:203
  2246.9 4.1 add_convert_fusion.2
  2251.0 46.3 %reduce-scatter.83.cloned.1.call-done = bf16[768,768]{1,0:T(8,128)(2,1)} async-done(((bf16[3072,768]{1,0:T(8,128)(2,1)}), bf16[768,768]{1,0:T(8,128)(2,1)}) %reduce-scatter.83.cloned.1.call-update) | async-done | bytes 1179664 | tf_op jit(solution)/shard_map/reduce_scatter | solution.py:206
  2297.3 50.4 %reduce-scatter.79.cloned.1.call-done = bf16[768,768]{1,0:T(8,128)(2,1)} async-done(((bf16[3072,768]{1,0:T(8,128)(2,1)}), bf16[768,768]{1,0:T(8,128)(2,1)}) %reduce-scatter.79.cloned.1.call-update) | async-done | bytes 1179664 | tf_op jit(solution)/shard_map/reduce_scatter | solution.py:206
  2347.7 50.4 %reduce-scatter.81.cloned.1.call-done = bf16[768,768]{1,0:T(8,128)(2,1)} async-done(((bf16[3072,768]{1,0:T(8,128)(2,1)}), bf16[768,768]{1,0:T(8,128)(2,1)}) %reduce-scatter.81.cloned.1.call-update) | async-done | bytes 1179664 | tf_op jit(solution)/shard_map/reduce_scatter | solution.py:206
  2398.1 50.6 %reduce-scatter.77.cloned.1.call-done = bf16[768,768]{1,0:T(8,128)(2,1)} async-done(((bf16[3072,768]{1,0:T(8,128)(2,1)}), bf16[768,768]{1,0:T(8,128)(2,1)}) %reduce-scatter.77.cloned.1.call-update) | async-done | bytes 1179664 | tf_op jit(solution)/shard_map/reduce_scatter | solution.py:206
  2448.7 3.9 add_convert_fusion.1
  2454.2 4.2 convolution_add_fusion.26
  2458.5 4.1 convolution_add_fusion.23
  2471.3 21.2 all-reduce.52.cloned.1.call-done
  2499.5 22.9 all-reduce.43
  2529.6 149.2 %all-reduce.50.cloned.1.call-done = (bf16[192,3072]{0,1:T(8,128)(2,1)}, bf16[192,1536]{0,1:T(8,128)(2,1)}, bf16[192,768]{1,0:T(8,128)(2,1)}, bf16[192,3072]{1,0:T(8,128)(2,1)}, bf16[768,768]{1,0:T(8,128)(2,1)}) async-done(((bf16[192,3072]{0,1:T(8,128)(2,1)}, bf16[192,1536]{0,1:T(8,128)(2,1)}, bf16[192,768]{1,0:T(8,128)(2,1)}, bf16[192,3072]{1,0:T(8,128)(2,1)}, bf16[768,768]{1,0:T(8,128)(2,1)}), ...) | async-done | bytes 4423696 | tf_op jit(solution)/shard_map/psum | solution.py:443
  (1644 shorter events, 1076.4 us)
Async XLA Ops:
  7.2 29.4 %all-gather.24.cloned.1.call-start = ((), (), s32[]{:S(2)}) async-start(), calls=%async_computation.28 | async-start | bytes 2949120 | tf_op jit(solution)/shard_map/all_gather | solution.py:176
  7.9 77.9 %all-gather.46.cloned.1.call-start = ((), (), s32[]{:S(2)}) async-start(), calls=%async_computation.51 | async-start | bytes 1769472 | tf_op jit(solution)/shard_map/all_gather | solution.py:330
  41.4 90.1 %all-gather.48.cloned.1.call-start = ((), (), s32[]{:S(2)}) async-start(), calls=%async_computation.52 | async-start | bytes 1769472 | tf_op jit(solution)/shard_map/all_gather | solution.py:329
  43.2 134.0 %all-gather.38.cloned.1.call-start = ((), (), s32[]{:S(2)}) async-start(), calls=%async_computation.47 | async-start | bytes 1769472 | tf_op jit(solution)/shard_map/all_gather | solution.py:330
  43.8 178.5 %all-gather.40.cloned.1.call-start = ((), (), s32[]{:S(2)}) async-start(), calls=%async_computation.48 | async-start | bytes 1769472 | tf_op jit(solution)/shard_map/all_gather | solution.py:329
  44.6 223.3 %all-gather.42.cloned.1.call-start = ((), (), s32[]{:S(2)}) async-start(), calls=%async_computation.49 | async-start | bytes 1769472 | tf_op jit(solution)/shard_map/all_gather | solution.py:330
  45.1 268.0 %all-gather.44.cloned.1.call-start = ((), (), s32[]{:S(2)}) async-start(), calls=%async_computation.50 | async-start | bytes 1769472 | tf_op jit(solution)/shard_map/all_gather | solution.py:329
  45.9 313.0 %all-gather.34.cloned.1.call-start = ((), (), s32[]{:S(2)}) async-start(), calls=%async_computation.45 | async-start | bytes 1769472 | tf_op jit(solution)/shard_map/all_gather | solution.py:330
  46.7 358.0 %all-gather.36.cloned.1.call-start = ((), (), s32[]{:S(2)}) async-start(), calls=%async_computation.46 | async-start | bytes 1769472 | tf_op jit(solution)/shard_map/all_gather | solution.py:329
  47.4 395.0 %all-gather.26.cloned.1.call-start = ((), (), s32[]{:S(2)}) async-start(), calls=%async_computation.29 | async-start | bytes 5898240 | tf_op jit(solution)/shard_map/all_gather | solution.py:175
  48.1 460.7 %all-gather.28.cloned.1.call-start = ((), (), s32[]{:S(2)}) async-start(), calls=%async_computation.30 | async-start | bytes 1474560 | tf_op jit(solution)/shard_map/all_gather | solution.py:177
  48.8 462.2 %all-gather.30.cloned.1.call-start = ((), (), s32[]{:S(2)}) async-start(), calls=%async_computation.31 | async-start | bytes 5898240 | tf_op jit(solution)/shard_map/all_gather | solution.py:178
  49.4 490.1 %all-gather.32.cloned.1.call-start = ((), (), s32[]{:S(2)}) async-start(), calls=%async_computation.32 | async-start | bytes 5898240 | tf_op jit(solution)/shard_map/all_gather | solution.py:179
  50.1 1380.0 %reduce-scatter.87.cloned.1.call-start = ((), (), s32[]{:S(2)}) async-start(), calls=%async_computation.54 | async-start | bytes 1769472
  52.3 393.3 %copy-start.199 = (pred[128]{0:T(512)(128)(4,1)}, pred[128]{0:T(512)(128)(4,1)S(1)}, u32[]{:S(2)}) copy-start(pred[128]{0:T(512)(128)(4,1)S(1)} %get-tuple-element.2519) | copy-start | bytes 388
  57.5 384.9 %copy-start.138 = (f32[4,1,768]{2,1,0:T(1,128)}, f32[4,1,768]{2,1,0:T(1,128)S(1)}, u32[]{:S(2)}) copy-start(f32[4,1,768]{2,1,0:T(1,128)S(1)} %convert_element_type.1139) | copy-start | bytes 36868
  58.7 723.2 %copy-start.74 = (f32[768]{0:T(1024)}, f32[768]{0:T(1024)S(1)}, u32[]{:S(2)}) copy-start(f32[768]{0:T(1024)S(1)} %convert_element_type.930) | copy-start | bytes 9220
  549.7 70.6 %copy-start.2 = (bf16[768,768]{1,0:T(8,128)(2,1)S(1)}, bf16[768,768]{1,0:T(8,128)(2,1)}, u32[]{:S(2)}) copy-start(bf16[768,768]{1,0:T(8,128)(2,1)} %all-gather.28.cloned.1.call-done) | copy-start | bytes 3538948
  710.4 97.7 %copy-start.162 = (f32[128]{0:T(128)}, f32[128]{0:T(128)S(1)}, u32[]{:S(2)}) copy-start(f32[128]{0:T(128)S(1)} %broadcast_multiply_fusion.19) | copy-start | bytes 1540
  710.6 97.5 %copy-start.173 = (f32[128]{0:T(128)}, f32[128]{0:T(128)S(1)}, u32[]{:S(2)}) copy-start(f32[128]{0:T(128)S(1)} %add_rsqrt_fusion.3) | copy-start | bytes 1540
  720.1 67.9 %copy-start.24 = (f32[128,768]{1,0:T(8,128)}, f32[128,768]{1,0:T(8,128)S(1)}, u32[]{:S(2)}) copy-start(f32[128,768]{1,0:T(8,128)S(1)} %get-tuple-element.2539) | copy-start | bytes 1179652
  720.1 67.9 %copy-start.186 = (f32[128]{0:T(128)}, f32[128]{0:T(128)S(1)}, u32[]{:S(2)}) copy-start(f32[128]{0:T(128)S(1)} %broadcast_multiply_fusion.18) | copy-start | bytes 1540
  720.3 67.7 %copy-start.195 = (f32[128]{0:T(128)}, f32[128]{0:T(128)S(1)}, u32[]{:S(2)}) copy-start(f32[128]{0:T(128)S(1)} %add_rsqrt_fusion.2) | copy-start | bytes 1540
  726.7 62.4 %slice-start.10 = ((s8[4718592]{0:T(1024)(128)(4,1)}), s8[524288]{0:T(1024)(128)(4,1)S(1)}, s32[]{:S(2)}) async-start(s8[4718592]{0:T(1024)(128)(4,1)} %bitcast.854), calls=%async_computation.81 | async-start | bytes 1048576
  973.3 459.9 %reduce-scatter.85.cloned.1.call-start = ((), (), s32[]{:S(2)}) async-start(), calls=%async_computation.53 | async-start | bytes 1769472
  984.7 455.2 %reduce-scatter.91.cloned.1.call-start = ((), (), s32[]{:S(2)}) async-start(), calls=%async_computation.56 | async-start | bytes 1769472
  1147.6 295.2 %reduce-scatter.89.cloned.1.call-start = ((), (), s32[]{:S(2)}) async-start(), calls=%async_computation.55 | async-start | bytes 1769472
  1158.1 291.2 %reduce-scatter.95.cloned.1.call-start = ((), (), s32[]{:S(2)}) async-start(), calls=%async_computation.58 | async-start | bytes 1769472
  1318.4 133.8 %reduce-scatter.93.cloned.1.call-start = ((), (), s32[]{:S(2)}) async-start(), calls=%async_computation.57 | async-start | bytes 1769472
  1328.9 189.5 %reduce-scatter.99.cloned.1.call-start = ((), (), s32[]{:S(2)}) async-start(), calls=%async_computation.60 | async-start | bytes 1769472
  1414.1 172.3 %reduce-scatter.97.cloned.1.call-start = ((), (), s32[]{:S(2)}) async-start(), calls=%async_computation.59 | async-start | bytes 1769472
  1422.8 263.2 %reduce-scatter.63.cloned.1.call-start = ((), (), s32[]{:S(2)}) async-start(), calls=%async_computation.34 | async-start | bytes 1474560 | tf_op jit(solution)/shard_map/reduce_scatter | solution.py:200
  1425.3 260.7 %reduce-scatter.65.cloned.1.call-start = ((), (), s32[]{:S(2)}) async-start(), calls=%async_computation.35 | async-start | bytes 1474560 | tf_op jit(solution)/shard_map/reduce_scatter | solution.py:200
  1427.0 259.1 %reduce-scatter.67.cloned.1.call-start = ((), (), s32[]{:S(2)}) async-start(), calls=%async_computation.36 | async-start | bytes 1474560 | tf_op jit(solution)/shard_map/reduce_scatter | solution.py:200
  1428.5 270.8 %reduce-scatter.61.cloned.1.call-start = ((), (), s32[]{:S(2)}) async-start(), calls=%async_computation.33 | async-start | bytes 1474560 | tf_op jit(solution)/shard_map/reduce_scatter | solution.py:200
  1430.1 304.7 %reduce-scatter.109.cloned.1.call-start = ((), (), s32[]{:S(2)}) async-start(), calls=%async_computation.65 | async-start | bytes 2949120
  1439.7 331.3 %reduce-scatter.111.cloned.1.call-start = ((), (), s32[]{:S(2)}) async-start(), calls=%async_computation.66 | async-start | bytes 2949120
  1449.2 357.9 %reduce-scatter.113.cloned.1.call-start = ((), (), s32[]{:S(2)}) async-start(), calls=%async_computation.67 | async-start | bytes 2949120
  1458.6 384.9 %reduce-scatter.115.cloned.1.call-start = ((), (), s32[]{:S(2)}) async-start(), calls=%async_computation.68 | async-start | bytes 2949120
  1592.8 301.0 %reduce-scatter.101.cloned.1.call-start = ((), (), s32[]{:S(2)}) async-start(), calls=%async_computation.61 | async-start | bytes 5898240
  1593.9 88.2 %copy-start.88 = (bf16[128,768]{1,0:T(8,128)(2,1)}, bf16[128,768]{1,0:T(8,128)(2,1)S(1)}, u32[]{:S(2)}) copy-start(bf16[128,768]{1,0:T(8,128)(2,1)S(1)} %get-tuple-element.2466) | copy-start | bytes 589828
  1593.9 88.2 %copy-start.90 = (bf16[128,768]{1,0:T(8,128)(2,1)}, bf16[128,768]{1,0:T(8,128)(2,1)S(1)}, u32[]{:S(2)}) copy-start(bf16[128,768]{1,0:T(8,128)(2,1)S(1)} %get-tuple-element.2467) | copy-start | bytes 589828
  1594.0 88.2 %copy-start.92 = (bf16[128,768]{1,0:T(8,128)(2,1)}, bf16[128,768]{1,0:T(8,128)(2,1)S(1)}, u32[]{:S(2)}) copy-start(bf16[128,768]{1,0:T(8,128)(2,1)S(1)} %get-tuple-element.2524) | copy-start | bytes 589828
  1594.0 88.2 %copy-start.94 = (bf16[128,768]{1,0:T(8,128)(2,1)}, bf16[128,768]{1,0:T(8,128)(2,1)S(1)}, u32[]{:S(2)}) copy-start(bf16[128,768]{1,0:T(8,128)(2,1)S(1)} %get-tuple-element.2525) | copy-start | bytes 589828
  1604.3 340.1 %reduce-scatter.103.cloned.1.call-start = ((), (), s32[]{:S(2)}) async-start(), calls=%async_computation.62 | async-start | bytes 5898240
  1605.4 77.5 %copy-start.96 = (bf16[128,768]{1,0:T(8,128)(2,1)}, bf16[128,768]{1,0:T(8,128)(2,1)S(1)}, u32[]{:S(2)}) copy-start(bf16[128,768]{1,0:T(8,128)(2,1)S(1)} %get-tuple-element.2470) | copy-start | bytes 589828
  1605.4 77.5 %copy-start.98 = (bf16[128,768]{1,0:T(8,128)(2,1)}, bf16[128,768]{1,0:T(8,128)(2,1)S(1)}, u32[]{:S(2)}) copy-start(bf16[128,768]{1,0:T(8,128)(2,1)S(1)} %get-tuple-element.2471) | copy-start | bytes 589828
  1605.4 77.5 %copy-start.100 = (bf16[128,768]{1,0:T(8,128)(2,1)}, bf16[128,768]{1,0:T(8,128)(2,1)S(1)}, u32[]{:S(2)}) copy-start(bf16[128,768]{1,0:T(8,128)(2,1)S(1)} %get-tuple-element.2526) | copy-start | bytes 589828
  1605.4 77.5 %copy-start.102 = (bf16[128,768]{1,0:T(8,128)(2,1)}, bf16[128,768]{1,0:T(8,128)(2,1)S(1)}, u32[]{:S(2)}) copy-start(bf16[128,768]{1,0:T(8,128)(2,1)S(1)} %get-tuple-element.2527) | copy-start | bytes 589828
  1615.6 379.2 %reduce-scatter.105.cloned.1.call-start = ((), (), s32[]{:S(2)}) async-start(), calls=%async_computation.63 | async-start | bytes 5898240
  1617.4 66.2 %copy-start.104 = (bf16[128,768]{1,0:T(8,128)(2,1)}, bf16[128,768]{1,0:T(8,128)(2,1)S(1)}, u32[]{:S(2)}) copy-start(bf16[128,768]{1,0:T(8,128)(2,1)S(1)} %get-tuple-element.2474) | copy-start | bytes 589828
  1628.4 416.8 %reduce-scatter.107.cloned.1.call-start = ((), (), s32[]{:S(2)}) async-start(), calls=%async_computation.64 | async-start | bytes 5898240
  1641.2 454.4 %reduce-scatter.71.cloned.1.call-start = ((), (), s32[]{:S(2)}) async-start(), calls=%async_computation.38 | async-start | bytes 5898240 | tf_op jit(solution)/shard_map/reduce_scatter | solution.py:203
  1646.2 500.0 %reduce-scatter.73.cloned.1.call-start = ((), (), s32[]{:S(2)}) async-start(), calls=%async_computation.39 | async-start | bytes 5898240 | tf_op jit(solution)/shard_map/reduce_scatter | solution.py:203
  1651.0 545.4 %reduce-scatter.75.cloned.1.call-start = ((), (), s32[]{:S(2)}) async-start(), calls=%async_computation.40 | async-start | bytes 5898240 | tf_op jit(solution)/shard_map/reduce_scatter | solution.py:203
  1656.1 590.8 %reduce-scatter.69.cloned.1.call-start = ((), (), s32[]{:S(2)}) async-start(), calls=%async_computation.37 | async-start | bytes 5898240 | tf_op jit(solution)/shard_map/reduce_scatter | solution.py:203
  1661.1 636.2 %reduce-scatter.83.cloned.1.call-start = ((), (), s32[]{:S(2)}) async-start(), calls=%async_computation.44 | async-start | bytes 5898240 | tf_op jit(solution)/shard_map/reduce_scatter | solution.py:206
  1665.9 681.8 %reduce-scatter.79.cloned.1.call-start = ((), (), s32[]{:S(2)}) async-start(), calls=%async_computation.42 | async-start | bytes 5898240 | tf_op jit(solution)/shard_map/reduce_scatter | solution.py:206
  1670.6 727.5 %reduce-scatter.81.cloned.1.call-start = ((), (), s32[]{:S(2)}) async-start(), calls=%async_computation.43 | async-start | bytes 5898240 | tf_op jit(solution)/shard_map/reduce_scatter | solution.py:206
  1675.4 773.3 %reduce-scatter.77.cloned.1.call-start = ((), (), s32[]{:S(2)}) async-start(), calls=%async_computation.41 | async-start | bytes 5898240 | tf_op jit(solution)/shard_map/reduce_scatter | solution.py:206
  1680.2 812.3 %all-reduce.52.cloned.1.call-start = ((), (), s32[]{:S(2)}) async-start(), calls=%async_computation.70 | async-start | bytes 217088
  1701.4 977.4 %all-reduce.50.cloned.1.call-start = ((), (), s32[]{:S(2)}) async-start(), calls=%async_computation.69 | async-start | bytes 10027008 | tf_op jit(solution)/shard_map/psum | solution.py:443
  2470.2 58.0 %copy-start.20 = (f32[128,768]{1,0:T(8,128)S(1)}, f32[128,768]{1,0:T(8,128)}, u32[]{:S(2)}) copy-start(f32[128,768]{1,0:T(8,128)} %copy-done.18) | copy-start | bytes 1179652
  2470.2 58.0 %copy-start.23 = (f32[128,768]{1,0:T(8,128)S(1)}, f32[128,768]{1,0:T(8,128)}, u32[]{:S(2)}) copy-start(f32[128,768]{1,0:T(8,128)} %copy-done.21) | copy-start | bytes 1179652
  (250 other events, 1575.3 us)
Sparse Core Ops, SparseCore 0:
  9.6 26.9 all-gather.23
  41.6 44.1 all-gather.45
  88.6 42.9 all-gather.47
  134.2 42.9 all-gather.37
  179.2 42.9 all-gather.39
  224.9 42.9 all-gather.41
  270.1 42.9 all-gather.43
  315.9 42.9 all-gather.33
  361.7 42.9 all-gather.35
  406.1 36.2 all-gather.25
  444.0 17.4 all-gather.27
  462.9 37.4 all-gather.29
  502.0 37.4 all-gather.31
  973.4 64.9 reduce-scatter.86
  1042.1 63.7 reduce-scatter.84
  1147.7 64.9 reduce-scatter.90
  1216.4 63.8 reduce-scatter.88
  1318.5 65.1 reduce-scatter.94
  1387.5 63.6 reduce-scatter.92
  1454.5 63.7 reduce-scatter.98
  1522.7 63.6 reduce-scatter.96
  1589.0 24.6 reduce-scatter.62
  1616.4 25.6 reduce-scatter.64
  1645.1 25.6 reduce-scatter.66
  1673.5 25.7 reduce-scatter.60
  1701.7 33.0 reduce-scatter.108
  1737.9 33.0 reduce-scatter.110
  1774.1 33.0 reduce-scatter.112
  1810.4 33.0 reduce-scatter.114
  1845.9 47.8 reduce-scatter.100
  1896.5 47.8 reduce-scatter.102
  1946.9 47.8 reduce-scatter.104
  1997.3 47.8 reduce-scatter.106
  2047.7 47.8 reduce-scatter.70
  2098.3 47.8 reduce-scatter.72
  2148.6 47.8 reduce-scatter.74
  2199.0 47.8 reduce-scatter.68
  2249.4 47.8 reduce-scatter.82
  2299.8 47.8 reduce-scatter.78
  2350.3 47.8 reduce-scatter.80
  2400.8 47.8 reduce-scatter.76
  2455.1 37.4 all-reduce.51
  2497.8 180.9 all-reduce.49
where the time goes:
time: 2720 us; the launch traced here: 2690 us
  waiting for transfers between devices  1420 us (52%)
  local copies, waits for them, and re-layouts  577 us (21%)
  matrix products  431 us (16%)
  other arithmetic  193 us (7%)
  blocking collectives  46.5 us (2%)
    unnamed x60, waiting for transfers between devices  483 us
    unnamed x525, local copies, waits for them, and re-layouts  204 us
    reduce_scatter x4, waiting for transfers between devices, scatter_parts(): lax.psum_scatter(parts[4].astype(jnp.bfloat16), 'fsdp', scatter_dimension...  198 us
    reduce_scatter x4, waiting for transfers between devices, scatter_parts(): lax.psum_scatter(parts[3].astype(jnp.bfloat16), 'fsdp', scatter_dimension...  195 us
    dynamic_slice x192, local copies, waits for them, and re-layouts, pair_slice(): part = lax.dynamic_slice_in_dim(values, col_start, pair_width, 2)  190 us
    all_gather x4, waiting for transfers between devices, body(): lax.all_gather(key_rows, 'ctx', axis=1, tiled=True)  171 us
    all_gather x4, waiting for transfers between devices, body(): lax.all_gather(val_rows, 'ctx', axis=1, tiled=True)  149 us
    psum x1, waiting for transfers between devices, body(): lax.psum(shard_sums[0].astype(jnp.bfloat16), 'ctx').astype(jnp.float32)  149 us
  transfers between devices with their start and end apart: 43, of which 32 were waited for; matrix products, arithmetic and copies ran while one was open for 27% of the time, Pallas kernels for 0%

commit v1 on v0

v1 whole, which is shorter than its diff:
```python
import functools

import jax
import jax.numpy as jnp
from jax import lax
from jax.experimental import pallas as pl
from jax.experimental.pallas import tpu as pltpu
from jax.sharding import Mesh
from jax.sharding import PartitionSpec as P

HEADS = 12
EPSILON = 1e-05
BLOCKED = -1e30
BF = jnp.bfloat16
F32 = jnp.float32
LANES = 128
CHUNK = 16


def matmul(left_mat, right_mat):
    return jnp.dot(left_mat, right_mat, preferred_element_type=F32)


def rows_inner(left_mat, right_mat):
    return lax.dot_general(left_mat, right_mat, (((0,), (0,)), ((), ())), preferred_element_type=F32)


def times_transposed(left_mat, right_mat):
    return lax.dot_general(left_mat, right_mat, (((1,), (1,)), ((), ())), preferred_element_type=F32)


def normalize(values, gain_vec, shift_vec):
    center = values - jnp.mean(values, axis=-1, keepdims=True)
    scale_inv = lax.rsqrt(jnp.mean(center * center, axis=-1, keepdims=True) + EPSILON)
    normed = center * scale_inv
    return (normed * gain_vec + shift_vec, normed, scale_inv)


def normalize_back(grad_in, normed, scale_inv, gain_vec):
    scaled = grad_in * gain_vec
    inner_part = (
        scaled
        - jnp.mean(scaled, axis=-1, keepdims=True)
        - normed * jnp.mean(scaled * normed, axis=-1, keepdims=True)
    )
    return (inner_part * scale_inv, jnp.sum(grad_in * normed, axis=0), jnp.sum(grad_in, axis=0))


def column_sum(values):
    return jnp.sum(values.astype(F32), axis=0)


def forward_kernel(
    heads, hd, rows_ref, w_ref, bias_ref, ent_ref, qseg_ref, kseg_ref,
    att_ref, wts_ref, inv_ref, qcat_ref, kcat_ref, vneg_ref,
    kaug_s, vaug_s, score_s,
):
    step = pl.program_id(0)
    span = heads * hd
    full = rows_ref.shape[0]
    block = att_ref.shape[0]
    scale = hd ** (-0.5)

    @pl.when(step == 0)
    def _():
        kaug_s[:, :, LANES:] = jnp.broadcast_to(kseg_ref[...][None], (heads, full, LANES))
        lane = lax.broadcasted_iota(jnp.int32, (block, LANES - hd), 1)
        one_col = jnp.where(lane == 0, 1.0, 0.0).astype(BF)
        neg_col = jnp.where(lane < 2, -1.0, 0.0).astype(BF)

        def project(piece, carry):
            at = pl.ds(pl.multiple_of(piece * block, block), block)
            rows = rows_ref[at, :]
            ent = ent_ref[at, :hd]
            wide = ent_ref[at, :1] > 0
            word = (1 - ent).astype(BF)

            def part(index):
                cols = slice(index * span, (index + 1) * span)
                return jnp.dot(rows, w_ref[:, cols], preferred_element_type=F32) + bias_ref[:, cols]

            q_word = (jnp.where(wide, part(2), part(0))).astype(BF) * BF(scale)
            q_ent = (jnp.where(wide, part(3), part(1))).astype(BF) * BF(scale)
            keys = part(4).astype(BF)
            vals = part(5).astype(BF)
            for h in range(heads):
                cut = slice(h * hd, (h + 1) * hd)
                qcat_ref[h, at, :] = jnp.concatenate([q_word[:, cut], q_ent[:, cut]], axis=1)
                k_pair = jnp.concatenate([keys[:, cut] * word, keys[:, cut] * ent], axis=1)
                kcat_ref[h, at, :] = k_pair
                kaug_s[h, at, :LANES] = k_pair
                vneg_ref[h, at, :] = jnp.concatenate([vals[:, cut], neg_col], axis=1)
                vaug_s[h, at, :] = jnp.concatenate([vals[:, cut], one_col], axis=1)
            return carry

        lax.fori_loop(0, full // block, project, 0)

    here = pl.ds(pl.multiple_of(step * block, block), block)
    q_seg = qseg_ref[here, :]
    lane = lax.broadcasted_iota(jnp.int32, (block, LANES), 1)
    inv_all = jnp.zeros((block, LANES), F32)
    mixed = []
    for h in range(heads):
        q_aug = jnp.concatenate([qcat_ref[h, here, :], q_seg], axis=1)
        score_s[h % 2] = lax.dot_general(
            q_aug, kaug_s[h], (((1,), (1,)), ((), ())), preferred_element_type=F32
        )
        for r in range(0, block, CHUNK):
            s = score_s[h % 2, r : r + CHUNK, :]
            top = jnp.max(s, axis=1, keepdims=True)
            wts_ref[h, r : r + CHUNK, :] = jnp.exp(s - top).astype(BF)
        out = jnp.dot(wts_ref[h], vaug_s[h], preferred_element_type=F32)
        inv = 1.0 / out[:, hd : hd + 1]
        inv_all = jnp.where(lane == h, inv, inv_all)
        mixed.append((out[:, :hd] * inv).astype(BF))
    att_ref[...] = jnp.concatenate(mixed, axis=1)
    inv_ref[...] = inv_all


def attention_forward(rows, w_sel, bias_sel, ent, qseg, kseg, heads, hd):
    full, width = rows.shape
    block = min(256, full)
    span = heads * hd
    steps = full // block
    whole = lambda *dims: pl.BlockSpec(dims, lambda i: (0,) * len(dims))
    return pl.pallas_call(
        functools.partial(forward_kernel, heads, hd),
        grid=(steps,),
        in_specs=[
            whole(full, width),
            whole(width, 6 * span),
            whole(1, 6 * span),
            whole(full, LANES),
            whole(full, LANES),
            whole(full, LANES),
        ],
        out_specs=[
            pl.BlockSpec((block, span), lambda i: (i, 0)),
            pl.BlockSpec((heads, block, full), lambda i: (0, i, 0)),
            pl.BlockSpec((block, LANES), lambda i: (i, 0)),
            whole(heads, full, 2 * hd),
            whole(heads, full, 2 * hd),
            whole(heads, full, LANES),
        ],
        out_shape=[
            jax.ShapeDtypeStruct((full, span), BF),
            jax.ShapeDtypeStruct((heads, full, full), BF),
            jax.ShapeDtypeStruct((full, LANES), F32),
            jax.ShapeDtypeStruct((heads, full, 2 * hd), BF),
            jax.ShapeDtypeStruct((heads, full, 2 * hd), BF),
            jax.ShapeDtypeStruct((heads, full, LANES), BF),
        ],
        scratch_shapes=[
            pltpu.VMEM((heads, full, 2 * LANES), BF),
            pltpu.VMEM((heads, full, LANES), BF),
            pltpu.VMEM((2, block, full), F32),
        ],
        compiler_params=pltpu.CompilerParams(vmem_limit_bytes=60 << 20),
        cost_estimate=pl.CostEstimate(
            flops=2 * full * width * 6 * span + 8 * heads * full * full * LANES,
            bytes_accessed=2 * heads * full * full + 10 * full * width,
            transcendentals=heads * full * full,
        ),
        name="attention_forward",
    )(rows, w_sel, bias_sel, ent, qseg, kseg)


def backward_kernel(
    heads, hd, go_ref, att_ref, inv_ref, wts_ref, qcat_ref, kcat_ref, vneg_ref, ent_ref, entb_ref,
    gq_ref, gkv_ref, gscore_s, low_s, gk_s, gv_s,
):
    step = pl.program_id(0)
    span = heads * hd
    block = go_ref.shape[0]
    full = kcat_ref.shape[1]
    scale = hd ** (-0.5)
    lane = lax.broadcasted_iota(jnp.int32, (block, LANES - hd), 1)
    is_ent = entb_ref[:, :1] > 0
    g_word, g_ent = [], []
    for h in range(heads):
        cut = slice(h * hd, (h + 1) * hd)
        g_low = (go_ref[:, cut].astype(F32) * inv_ref[:, h : h + 1]).astype(BF)
        delta = jnp.sum(g_low.astype(F32) * att_ref[:, cut].astype(F32), axis=1, keepdims=True)
        d_hi = delta.astype(BF)
        d_lo = (delta - d_hi.astype(F32)).astype(BF)
        extra = jnp.where(
            lane == 0, d_hi.astype(F32), jnp.where(lane == 1, d_lo.astype(F32), 0.0)
        ).astype(BF)
        g_aug = jnp.concatenate([g_low, extra], axis=1)
        gscore_s[h % 2] = lax.dot_general(
            g_aug, vneg_ref[h], (((1,), (1,)), ((), ())), preferred_element_type=F32
        )
        for r in range(0, block, CHUNK):
            low_s[h % 2, r : r + CHUNK, :] = (
                wts_ref[h, r : r + CHUNK, :].astype(F32) * gscore_s[h % 2, r : r + CHUNK, :]
            ).astype(BF)
        g_q = jnp.dot(low_s[h % 2], kcat_ref[h], preferred_element_type=F32) * scale
        g_word.append(g_q[:, :hd])
        g_ent.append(g_q[:, hd:])
        g_k = lax.dot_general(
            qcat_ref[h], low_s[h % 2], (((0,), (0,)), ((), ())), preferred_element_type=F32
        )
        g_v = lax.dot_general(
            g_low, wts_ref[h], (((0,), (0,)), ((), ())), preferred_element_type=F32
        )

        @pl.when(step == 0)
        def _(h=h, g_k=g_k, g_v=g_v):
            gk_s[h] = g_k
            gv_s[h] = g_v

        @pl.when(step > 0)
        def _(h=h, g_k=g_k, g_v=g_v):
            gk_s[h] += g_k
            gv_s[h] += g_v

    g_word = jnp.concatenate(g_word, axis=1)
    g_ent = jnp.concatenate(g_ent, axis=1)
    gq_ref[:, :span] = jnp.where(is_ent, 0.0, g_word).astype(BF)
    gq_ref[:, span : 2 * span] = jnp.where(is_ent, 0.0, g_ent).astype(BF)
    gq_ref[:, 2 * span : 3 * span] = jnp.where(is_ent, g_word, 0.0).astype(BF)
    gq_ref[:, 3 * span :] = jnp.where(is_ent, g_ent, 0.0).astype(BF)

    @pl.when(step == pl.num_programs(0) - 1)
    def _():
        def close(piece, carry):
            at = pl.ds(pl.multiple_of(piece * block, block), block)
            pick = ent_ref[at, :1] > 0
            g_keys, g_vals = [], []
            for h in range(heads):
                both = gk_s[h, :, at].T
                g_keys.append(jnp.where(pick, both[:, hd:], both[:, :hd]))
                g_vals.append(gv_s[h, :, at].T)
            gkv_ref[at, :span] = jnp.concatenate(g_keys, axis=1).astype(BF)
            gkv_ref[at, span:] = jnp.concatenate(g_vals, axis=1).astype(BF)
            return carry

        lax.fori_loop(0, full // block, close, 0)


def attention_backward(g_out, att, inv, wts, qcat, kcat, vneg, ent, heads, hd):
    full, span = att.shape
    block = min(256, full)
    whole = lambda *dims: pl.BlockSpec(dims, lambda i: (0,) * len(dims))
    by_rows = lambda width: pl.BlockSpec((block, width), lambda i: (i, 0))
    by_head = lambda width: pl.BlockSpec((heads, block, width), lambda i: (0, i, 0))
    return pl.pallas_call(
        functools.partial(backward_kernel, heads, hd),
        grid=(full // block,),
        in_specs=[
            by_rows(span),
            by_rows(span),
            by_rows(LANES),
            by_head(full),
            by_head(2 * hd),
            whole(heads, full, 2 * hd),
            whole(heads, full, LANES),
            whole(full, LANES),
            by_rows(LANES),
        ],
        out_specs=[by_rows(4 * span), whole(full, 2 * span)],
        out_shape=[
            jax.ShapeDtypeStruct((full, 4 * span), BF),
            jax.ShapeDtypeStruct((full, 2 * span), BF),
        ],
        scratch_shapes=[
            pltpu.VMEM((2, block, full), F32),
            pltpu.VMEM((2, block, full), BF),
            pltpu.VMEM((heads, 2 * hd, full), F32),
            pltpu.VMEM((heads, hd, full), F32),
        ],
        compiler_params=pltpu.CompilerParams(vmem_limit_bytes=60 << 20),
        cost_estimate=pl.CostEstimate(
            flops=16 * heads * full * full * LANES,
            bytes_accessed=2 * heads * full * full + 20 * full * span,
            transcendentals=0,
        ),
        name="attention_backward",
    )(g_out, att, inv, wts, qcat, kcat, vneg, ent, ent)


def layer(
    half, per_row, inputs, query_weight, kv_weight, out_weight, up_weight, down_weight,
    query_bias, value_bias, out_bias, up_bias, down_bias,
    norm1_gain, norm1_shift, norm2_gain, norm2_shift, types, lengths, cotangent,
):
    rows_here, span, width = inputs.shape
    head_dim = width // HEADS
    full = types.shape[1]
    members = 2 * per_row
    heads = HEADS // members
    cols = heads * head_dim
    row_count = lax.axis_size("row")
    outer = lax.axis_size("outer")
    core = lax.axis_index("core")
    group = lax.axis_index("group")
    member = group * 2 + core
    row_id = lax.axis_index("row")
    own = row_count * (span // 2)

    def swap(values):
        return lax.ppermute(values, "core", [(0, 1), (1, 0)])

    def in_order(index, mine, other):
        return jnp.stack([jnp.where(index == 0, mine, other), jnp.where(index == 0, other, mine)])

    def gather_outer(values):
        if outer == 2:
            other = lax.ppermute(values, "outer", [(0, 1), (1, 0)])
            return in_order(lax.axis_index("outer"), values, other)
        return lax.all_gather(values, "outer", axis=0, tiled=False)

    def gather_members(values):
        pair = in_order(core, values, swap(values))
        if per_row == 1:
            return pair
        spread = lax.all_gather(pair, "group", axis=0, tiled=False)
        return spread.reshape((members,) + values.shape)

    def exchange_members(values):
        if per_row == 1:
            mine = lax.dynamic_index_in_dim(values, core, 0, keepdims=False)
            away = lax.dynamic_index_in_dim(values, 1 - core, 0, keepdims=False)
            return in_order(core, mine, swap(away))
        return lax.all_to_all(values, ("group", "core"), 0, 0, tiled=True)

    def take(values, index, axis):
        return lax.dynamic_index_in_dim(values, index, axis, keepdims=False)

    def to_row(values):
        pieces = values.reshape(rows_here, 2, span // 2, width)
        other = swap(take(pieces, 1 - core, 1))
        both = in_order(core, take(pieces, core, 1), other).reshape(row_count, span // 2, width)
        return lax.all_to_all(both, "row", 0, 0, tiled=True).reshape(own, width)

    def from_row(values):
        back = lax.all_to_all(values.reshape(row_count, span // 2, width), "row", 0, 0, tiled=True)
        back = back.reshape(2, rows_here, span // 2, width)
        other = swap(take(back, 1 - core, 0))
        both = in_order(core, take(back, core, 0), other)
        return both.transpose(1, 0, 2, 3).reshape(rows_here, span, width)

    own_rows = to_row(inputs)
    all_rows = gather_members(own_rows).reshape(full, width)

    tags = jnp.concatenate([types, lengths], axis=1)
    tags = in_order(core, tags, swap(tags)).reshape(row_count, -1)
    tags = take(tags, row_id, 0)
    types_row, lengths_row = tags[:full], tags[full:]

    def by_member(values):
        return values.reshape(row_count, per_row, 2, span // 2).transpose(1, 2, 0, 3).reshape(full)

    entity = by_member(types_row) > 0
    positions = by_member(lax.iota(jnp.int32, full))
    docs = lengths_row.shape[0]
    ends = [jnp.sum(lengths_row[: d + 1]) for d in range(docs)]
    seg = sum((positions >= end).astype(jnp.int32) for end in ends)
    lanes = lax.broadcasted_iota(jnp.int32, (full, LANES), 1)
    same = lanes == seg[:, None]
    qseg = jnp.where(same, 1.0, 0.0).astype(BF)
    kseg = jnp.where(same | (lanes >= docs), 0.0, BLOCKED).astype(BF)
    ent = jnp.broadcast_to(jnp.where(entity, 1.0, 0.0).astype(BF)[:, None], (full, LANES))

    shard = query_weight.shape[0]
    cut = jnp.concatenate([query_weight, kv_weight], axis=1).reshape(shard, 6, members, cols)
    away = take(cut, group * 2 + 1 - core, 2).reshape(shard, 6 * cols)
    mine = take(cut, member, 2).reshape(shard, 6 * cols)
    w_sel = gather_outer(in_order(core, mine, swap(away))).reshape(width, 6 * cols)

    vectors = (
        query_bias, value_bias, out_bias, up_bias, down_bias,
        norm1_gain, norm1_shift, norm2_gain, norm2_shift,
    )
    sizes = [v.shape[0] for v in vectors]
    packed = jnp.concatenate(vectors)
    packed = lax.all_gather(packed, ("outer", "core"), axis=0, tiled=False)
    offsets = [sum(sizes[:i]) for i in range(len(sizes) + 1)]
    (b_query, b_value, b_out, b_up, b_down, g_one, s_one, g_two, s_two) = (
        packed[:, a:b].reshape(-1).astype(F32) for a, b in zip(offsets[:-1], offsets[1:])
    )
    b_six = jnp.concatenate([b_query, jnp.zeros((width,), F32), b_value])
    b_sel = take(b_six.reshape(6, members, cols), member, 1).reshape(1, 6 * cols)

    att, inv_stored, wts = None, None, None
    att, wts, inv_stored, qcat, kcat, vneg = attention_forward(
        all_rows, w_sel, b_sel, ent, qseg, kseg, heads, head_dim
    )

    def fetch(values):
        return gather_outer(in_order(core, values, swap(values))).reshape(-1, values.shape[1])

    w_out, w_up, w_down = fetch(out_weight), fetch(up_weight), fetch(down_weight)

    def heads_to_tokens(values):
        got = exchange_members(values.reshape(members, own, cols))
        return got.transpose(1, 0, 2).reshape(own, width)

    def tokens_to_heads(values):
        parts = values.reshape(own, members, cols).transpose(1, 0, 2)
        return exchange_members(parts).reshape(full, cols)

    attended = heads_to_tokens(att)
    attn_out = matmul(attended, w_out) + b_out
    hidden, normed_one, inv_one = normalize(own_rows.astype(F32) + attn_out, g_one, s_one)
    hidden_low = hidden.astype(BF)
    up_proj = matmul(hidden_low, w_up) + b_up
    gelu_out, gelu_pull = jax.vjp(lambda v: jax.nn.gelu(v, approximate=False), up_proj)
    act_low = gelu_out.astype(BF)
    ffn_out = matmul(act_low, w_down) + b_down
    result, normed_two, inv_two = normalize(hidden + ffn_out, g_two, s_two)
    output = from_row(result.astype(BF))

    cot = to_row(cotangent).astype(F32)
    grad_y2, grad_g2, grad_s2 = normalize_back(cot, normed_two, inv_two, g_two)
    grad_ffn = grad_y2.astype(BF)
    grad_act = times_transposed(grad_ffn, w_down)
    grad_up = gelu_pull(grad_act)[0].astype(BF)
    grad_hidden = grad_y2 + times_transposed(grad_up, w_up)
    grad_y1, grad_g1, grad_s1 = normalize_back(grad_hidden, normed_one, inv_one, g_one)
    grad_attn = grad_y1.astype(BF)
    grad_attended = times_transposed(grad_attn, w_out).astype(BF)

    def pick_rows(left, core_index, outer_index):
        parts = left.reshape(left.shape[0], outer, 2, -1)
        if outer_index is None:
            return take(parts, core_index, 2).reshape(left.shape[0], -1)
        return take(take(parts, core_index, 2), outer_index, 1)

    def reduce_outer(partial):
        if outer == 2:
            me = lax.axis_index("outer")
            other = lax.ppermute(take(partial, 1 - me, 0).astype(BF), "outer", [(0, 1), (1, 0)])
            return take(partial, me, 0).astype(F32) + other.astype(F32)
        return lax.psum_scatter(partial.astype(BF), "outer", scatter_dimension=0, tiled=False).astype(F32)

    def shard_grad(left, right):
        away = rows_inner(pick_rows(left, 1 - core, None), right).astype(BF)
        mine = rows_inner(pick_rows(left, core, None), right)
        pair = mine + swap(away).astype(F32)
        part = reduce_outer(pair.reshape(outer, -1, right.shape[1]))
        return lax.psum(part.astype(BF), ("row", "group")).astype(F32)

    g_w_down = shard_grad(act_low, grad_ffn)
    g_w_up = shard_grad(hidden_low, grad_up)
    g_w_out = shard_grad(attended, grad_attn)

    gq, gkv = attention_backward(
        tokens_to_heads(grad_attended), att, inv_stored, wts, qcat, kcat, vneg, ent, heads, head_dim
    )
    g_six = jnp.concatenate([gq, gkv], axis=1)
    g_sel = reduce_outer(rows_inner(all_rows, g_six).reshape(outer, -1, 6 * cols))
    g_sel = lax.psum(g_sel.astype(BF), "row").reshape(2, shard, 6, cols)
    got = in_order(core, take(g_sel, core, 0), swap(take(g_sel, 1 - core, 0)))
    if per_row > 1:
        got = lax.all_gather(got, "group", axis=0, tiled=False)
    got = got.reshape(members, shard, 6, cols).transpose(1, 2, 0, 3).reshape(shard, 6 * width)
    g_w_query = got[:, : 4 * width].astype(F32)
    g_w_kv = got[:, 4 * width :].astype(F32)

    part_in = times_transposed(g_six, w_sel)
    got_in = exchange_members(part_in.astype(BF).reshape(members, own, width))
    grad_in = grad_y1 + jnp.sum(got_in.astype(F32), axis=0)
    input_grad = from_row(grad_in.astype(BF))

    six_sum = column_sum(g_six).reshape(6, 1, cols)
    spot = lax.broadcasted_iota(jnp.int32, (1, members, 1), 1) == member
    six_sum = jnp.where(spot, six_sum, 0.0).reshape(6, width)
    small = [
        six_sum[:4].reshape(-1), six_sum[5], column_sum(grad_attn), column_sum(grad_up),
        column_sum(grad_ffn), grad_g1, grad_s1, grad_g2, grad_s2,
    ]
    total = lax.psum(jnp.concatenate(small), ("row", "group", "outer", "core"))
    me = lax.axis_index("outer") * 2 + core
    pieces, at = [], 0
    for size in sizes:
        whole_size = size * outer * 2
        pieces.append(lax.dynamic_slice_in_dim(total[at : at + whole_size], me * size, size))
        at += whole_size
    return (output, input_grad, g_w_query, g_w_kv, g_w_out, g_w_up, g_w_down, *pieces)


def solution(mesh):
    def step(*args):
        ctx, fsdp = mesh.shape["ctx"], mesh.shape["fsdp"]
        row_count = args[0].shape[0] // (fsdp // 2)
        per_row = ctx // row_count
        fine = Mesh(
            mesh.devices.reshape(row_count, per_row, fsdp // 2, 2), ("row", "group", "outer", "core")
        )
        tokens = P(("outer", "core"), ("row", "group"), None)
        mat, vec = P(("outer", "core"), None), P(("outer", "core"))
        in_specs = (tokens, *[mat] * 5, *[vec] * 9, mat, mat, tokens)
        out_specs = (tokens, tokens, *[mat] * 5, *[vec] * 9)
        body = functools.partial(layer, None, per_row)
        return jax.shard_map(
            body, mesh=fine, in_specs=in_specs, out_specs=out_specs, check_vma=False
        )(*args)

    return step
```

time: 2720 us -> 688 us (0.25)
  waiting for transfers between devices: 1420 us -> 252 us
  local copies, waits for them, and re-layouts: 577 us -> 115 us
  matrix products: 431 us -> 64.4 us
  other arithmetic: 193 us -> 67.7 us
  Pallas kernels: 0 us -> 69.8 us
  starting transfers between devices: 2.52 us -> 30.8 us
    unnamed x60 -> x1, waiting for transfers between devices: 483 us -> 0.02 us
    reduce_scatter x12 -> x0, waiting for transfers between devices: 406 us -> none  [the longest x4 198 us: scatter_parts(): lax.psum_scatter(parts[4].astype(jnp.bfloat16), 'fsdp', scatter_dimension...]
    all_gather x13 -> x0, waiting for transfers between devices: 384 us -> none  [the longest x4 171 us: body(): lax.all_gather(key_rows, 'ctx', axis=1, tiled=True)]
    dot_general x284 -> x3, matrix products: 337 us -> 23.6 us  [matmul(): return jnp.dot(left_mat, right_mat, preferred_element_type=F32)]
    unnamed x525 -> x163, local copies, waits for them, and re-layouts: 204 us -> 35.2 us
    dynamic_slice x193 -> x18, local copies, waits for them, and re-layouts: 190 us -> 36.2 us  [the longest x6 25.6 us: take(): return lax.dynamic_index_in_dim(values, index, axis, keepdims=False)]
    dynamic_update_slice x120 -> x0, local copies, waits for them, and re-layouts: 121 us -> none  [the longest x48 41.8 us: one_pair(): lax.dynamic_update_slice_in_dim(grad_ent, ent_q.reshape(seq_count, own_sp...]
    ppermute x0 -> x25, waiting for transfers between devices: none -> 113 us  [the longest x4 72.8 us: reduce_outer(): lax.ppermute(take(partial, 1 - me, 0).astype(BF), 'outer', [(0, 1), (1, 0)])]
  transfers between devices with their start and end apart: 43 -> 30, of which waited for: 32 -> 10; matrix products, arithmetic and copies ran while one was open for 27% -> 24% of each run, Pallas kernels for 0% -> 10%
where the time goes in v1:
time: 688 us; the launch traced here: 683 us
  waiting for transfers between devices  252 us (37%)
  local copies, waits for them, and re-layouts  115 us (17%)
  Pallas kernels  69.8 us (10%)
  other arithmetic  67.7 us (10%)
  blocking collectives  67.4 us (10%)
  matrix products  64.4 us (9%)
  starting transfers between devices  30.8 us (4%)
  between operations  16.2 us (2%)
    psum x1, waiting for transfers between devices, layer(): g_sel = lax.psum(g_sel.astype(BF), 'row').reshape(2, shard, 6, cols)  96.2 us
    ppermute x4, waiting for transfers between devices, reduce_outer(): lax.ppermute(take(partial, 1 - me, 0).astype(BF), 'outer', [(0, 1), (1, 0)])  72.8 us
    psum x1, blocking collectives, layer(): total = lax.psum(jnp.concatenate(small), ('row', 'group', 'outer', 'core'))  54.7 us
    pallas_call x1, Pallas kernels, attention_backward(): pl.pallas_call(functools.partial(backward_kernel, heads, hd), grid=(full...  44.4 us
    ppermute x4, waiting for transfers between devices, gather_outer(): other = lax.ppermute(values, 'outer', [(0, 1), (1, 0)])  39.7 us
    all_to_all x2, waiting for transfers between devices, from_row(): lax.all_to_all(values.reshape(row_count, span // 2, width), 'row', 0, 0,...  35.4 us
    unnamed x163, local copies, waits for them, and re-layouts  35.2 us
    another operation x33, other arithmetic, in_order(): jnp.stack([jnp.where(index == 0, mine, other), jnp.where(index == 0, othe...  33.7 us
  transfers between devices with their start and end apart: 30, of which 10 were waited for; matrix products, arithmetic and copies ran while one was open for 24% of the time, Pallas kernels for 10%

profile of v1, /device:TPU:0, one launch (start us, length us, event | category | flops | bytes accessed | tf_op | source)
XLA Modules:
  0.0 682.7 jit_solution(18033487587904651030)
XLA Ops:
  9.2 11.5 %dynamic-slice_reduce_fusion.1 = (bf16[192,6,384]{2,1,0:T(8,128)(2,1)S(1)}, bf16[192,6,384]{2,1,0:T(8,128)(2,1)}) fusion(bf16[192,6,2,384]{3,2,1,0:T(2,128)(2,1)S(1)} %reshape.445, s32[]{:T(128)S(6)} %select_n.292, s32[]{:T(128)S(6)} %select_n.293), kind=kLoop, calls=%fused_computation.51 | loop fusion | bytes 3538952 | tf_op jit(solution)/shard_map/jit(dynamic_index_in_dim)/dynamic_slice | solution.py:328
  20.9 2.4 copy.84
  23.8 1.8 dynamic-slice_bitcast_fusion.4
  28.7 12.7 %all-reduce = bf16[11520]{0:T(1024)(128)(2,1)S(1)} all-reduce(bf16[11520]{0:T(1024)(128)(2,1)S(1)} %dynamic-update-slice), channel_id=2, replica_groups=mesh['row'=8,'group'=1,'outer'=2,'core'=2] {'outer','core'}, use_global_device_ids=true, to_apply=%add | all-reduce | flops 11520 | bytes 46080
  48.9 2.6 add_bitcast_fusion
  57.4 6.0 all-to-all-start
  69.7 2.6 collective-permute-done.7
  74.6 1.8 select_bitcast_fusion.9
  76.4 7.2 %all-to-all-done = bf16[8,64,768]{2,1,0:T(8,128)(2,1)} async-done(((bf16[8,64,768]{2,1,0:T(8,128)(2,1)}), bf16[8,64,768]{2,1,0:T(8,128)(2,1)}, u32[]{:S(2)}, u32[]{:S(2)}) %all-to-all-start) | async-done | bytes 786464 | tf_op jit(solution)/shard_map/all_to_all | solution.py:334
  83.6 3.6 all-to-all-start.2
  91.8 1.8 pad_maximum_fusion.4
  97.2 13.1 %collective-permute-done.3 = bf16[2,192,2304]{2,1,0:T(8,128)(2,1)} collective-permute-done((bf16[2,192,2304]{2,1,0:T(8,128)(2,1)}, bf16[2,192,2304]{2,1,0:T(8,128)(2,1)}, u32[]{:S(2)}, u32[]{:S(2)}) %collective-permute-start.3) | collective-permute-done | bytes 1769504 | tf_op jit(solution)/shard_map/ppermute | solution.py:309
  110.3 1.7 select_bitcast_fusion.5
  112.0 2.1 pad_maximum_fusion.2
  114.9 25.4 %attention_forward.1 = (bf16[1024,384]{1,0:T(8,128)(2,1)}, bf16[6,1024,1024]{2,1,0:T(8,128)(2,1)}, f32[1024,128]{1,0:T(8,128)}, bf16[6,1024,128]{2,1,0:T(8,128)(...) custom-call(bf16[1024,768]{1,0:T(8,128)(2,1)} %bitcast.281, bf16[768,2304]{1,0:T(8,128)(2,1)} %bitcast.293, ...), custom_call_target="tpu_custom_call" | custom-call | flops 10066329600 | bytes 20447232 | tf_op jit(solution)/shard_map/attention_forward/pallas_call | solution.py:126
  140.3 1.9 constant_dynamic-slice_fusion.12
  142.3 1.9 copy.58
  145.7 2.6 copy.74
  150.8 2.2 fusion.49
  155.7 2.4 constant_dynamic-slice_fusion.3
  158.1 2.7 collective-permute-done.9
  160.8 2.0 select_bitcast_fusion.3
  163.5 18.5 %multiply_convert_fusion = (bf16[512,3072]{1,0:T(8,128)(2,1)}, f32[512,3072]{1,0:T(8,128)}, f32[512,3072]{1,0:T(8,128)}) fusion(f32[3072]{0:T(1024)S(1)} %copy-done.53, bf16[512,768]{1,0:T(8,128)(2,1)S(1)} %fusion.19, bf16[768,3072]{1,0:T(8,128)(2,1)S(1)} %bitcast.283), kind=kOutput, calls=%fused_computation.5 | convolution fusion | flops 2519728128 | bytes 21245952 | tf_op jit(solution)/shard_map/dot_general | solution.py:21
  182.0 7.2 %reshape.483 = bf16[512,2,2,768]{3,2,1,0:T(2,128)(2,1)S(1)} reshape(bf16[512,3072]{1,0:T(8,128)(2,1)} %get-tuple-element.54) | data formatting | bytes 6291456 | tf_op jit(solution)/shard_map/reshape | solution.py:425
  189.2 21.3 %collective-permute-done.11 = bf16[2,768,768]{2,1,0:T(8,128)(2,1)} collective-permute-done((bf16[2,768,768]{2,1,0:T(8,128)(2,1)}, bf16[2,768,768]{2,1,0:T(8,128)(2,1)}, u32[]{:S(2)}, u32[]{:S(2)}) %collective-permute-start.11) | collective-permute-done | bytes 2359328 | tf_op jit(solution)/shard_map/ppermute | solution.py:309
  210.6 2.6 select_bitcast_fusion.1
  215.6 2.8 fusion.50
  220.0 2.8 convert_reduce_fusion.4
  222.8 8.8 %convert_reduce_fusion.1 = (f32[3072]{0:T(1024)}, bf16[512,3072]{1,0:T(8,128)(2,1)S(1)}) fusion(f32[512,3072]{1,0:T(8,128)} %get-tuple-element.55, f32[512,3072]{1,0:T(8,128)} %get-tuple-element.127, f32[3072]{0:T(1024)S(1)} %copy-done.54, bf16[512,768]{1,0:T(8,128)(2,1)S(1)} %get-tuple-element.47, bf16[3072,768]{1,0:T(8,128)(2,1)S(1)} %bitcast.288), kind=kOutput, calls=%fused_computation.3 | convolution fusion | flops 2442654720 | bytes 21258240 | tf_op jit(solution)/shard_map/dot_general | solution.py:29
  231.7 6.2 multiply_reduce_fusion
  240.5 1.7 convolution_convert_fusion.3
  242.2 2.7 reshape.468
  244.9 4.2 constant_dynamic-slice_fusion.10
  249.1 2.9 copy.82
  252.0 3.2 copy.81
  255.2 9.1 %constant_dynamic-slice_fusion.1 = (bf16[512,2,1,768]{3,2,1,0:T(2,128)(2,1)}, bf16[512,2,1,768]{3,2,1,0:T(2,128)(2,1)}) fusion(bf16[512,2,2,768]{3,2,1,0:T(2,128)(2,1)S(1)} %reshape.483, s32[]{:T(128)S(6)} %select_n.293, s32[]{:T(128)S(6)} %select_n.292), kind=kLoop, calls=%fused_computation.167 | loop fusion | bytes 6291464 | tf_op jit(solution)/shard_map/jit(dynamic_index_in_dim)/dynamic_slice | solution.py:328
  264.2 6.8 %copy.80 = bf16[512,2,1,768]{0,3,1,2:T(8,128)(2,1)S(1)} copy(bf16[512,2,1,768]{3,2,1,0:T(2,128)(2,1)} %get-tuple-element.62) | data formatting | bytes 3145728
  271.1 2.8 convolution_convert_fusion.1
  274.4 2.8 convolution_convert_fusion
  277.2 6.2 copy.79
  283.4 2.4 convolution_convert_fusion.4
  288.7 44.4 %attention_backward.1 = (bf16[1024,1536]{1,0:T(8,128)(2,1)}, bf16[1024,768]{1,0:T(8,128)(2,1)}) custom-call(bf16[1024,384]{1,0:T(8,128)(2,1)} %bitcast.317, bf16[1024,384]{1,0:T(8,128)(2,1)} %get-tuple-element.24.att_ref, f32[1024,128]{1,0:T(8,128)} %get-tuple-element.25.inv_ref, bf16[6,1024,1024]{2,1,0:T(8,128)(2,1)} %get-tuple-element.26.wts_ref, ...), custom_call_target="tpu_custom_call" | custom-call | flops 12884901888 | bytes 20447232 | tf_op jit(solution)/shard_map/attention_backward/pallas_call | solution.py:247
  333.1 2.2 constant_dynamic-update-slice_fusion.3
  335.6 1.7 copy-done.28
  337.3 3.8 fusion.6
  345.2 3.2 convert_add_fusion
  348.4 2.2 copy-done
  354.1 2.2 copy-done.1
  358.6 30.7 %collective-permute-done.20 = bf16[192,768]{1,0:T(8,128)(2,1)S(1)} collective-permute-done((bf16[192,768]{1,0:T(8,128)(2,1)S(1)}, bf16[192,768]{1,0:T(8,128)(2,1)S(1)}, u32[]{:S(2)}, u32[]{:S(2)}) %collective-permute-start.20) | collective-permute-done | bytes 294944 | tf_op jit(solution)/shard_map/ppermute | solution.py:433
  390.4 3.0 reshape.474
  393.4 21.2 %collective-permute-done.24 = bf16[768,768]{1,0:T(8,128)(2,1)} collective-permute-done((bf16[768,768]{1,0:T(8,128)(2,1)}, bf16[768,768]{1,0:T(8,128)(2,1)}, u32[]{:S(2)}, u32[]{:S(2)}) %collective-permute-start.24) | collective-permute-done | bytes 1179680 | tf_op jit(solution)/shard_map/ppermute | solution.py:433
  414.7 3.3 fusion.9
  418.0 20.8 %collective-permute-done.22 = bf16[192,3072]{1,0:T(8,128)(2,1)S(1)} collective-permute-done((bf16[192,3072]{1,0:T(8,128)(2,1)}, bf16[192,3072]{1,0:T(8,128)(2,1)S(1)}, u32[]{:S(2)}, u32[]{:S(2)}) %collective-permute-start.22) | collective-permute-done | bytes 1179680 | tf_op jit(solution)/shard_map/ppermute | solution.py:433
  438.8 2.9 fusion.10
  441.7 2.0 copy-done.19
  443.7 6.2 convolution_convert_fusion.2
  451.2 6.1 all-to-all-start.1
  457.3 3.2 convert_reduce_fusion
  464.2 35.4 %all-to-all-done.1 = bf16[8,64,768]{2,1,0:T(8,128)(2,1)S(1)} async-done(((bf16[8,64,768]{2,1,0:T(8,128)(2,1)}), bf16[8,64,768]{2,1,0:T(8,128)(2,1)S(1)}, u32[]{:S(2)}, u32[]{:S(2)}) %all-to-all-start.1) | async-done | bytes 786464 | tf_op jit(solution)/shard_map/all_to_all | solution.py:337
  499.7 3.5 all-to-all-start.3
  503.5 54.7 %psum.39 = f32[11520]{0:T(1024)S(1)} all-reduce(f32[11520]{0:T(1024)S(1)} %constant_dynamic-update-slice_fusion.5), channel_id=1, replica_groups=mesh['row'=8,'group'=1,'outer'=2,'core'=2] {'row','group','outer','core'}, use_global_device_ids=true, to_apply=%region_24.25 | all-reduce | flops 11520 | bytes 92160 | tf_op jit(solution)/shard_map/psum | solution.py:473
  559.0 96.2 %all-reduce.4.cloned.1.call-done = (bf16[2,192,6,384]{3,2,1,0:T(8,128)(2,1)}, bf16[192,768]{1,0:T(8,128)(2,1)}, bf16[192,3072]{1,0:T(8,128)(2,1)}, bf16[768,768]{1,0:T(8,128)(2,1)}) async-done(((bf16[2,192,6,384]{3,2,1,0:T(8,128)(2,1)}, bf16[192,768]{1,0:T(8,128)(2,1)}, bf16[192,3072]{1,0:T(8,128)(2,1)}, bf16[768,768]{1,0:T(8,128)(2,1)}), (bf16[2,192,6,384]{3,2,1,0:T(8,128)(2,1)}, ...) | async-done | bytes 4423696 | tf_op jit(solution)/shard_map/psum | solution.py:453
  655.2 1.9 constant_dynamic-slice_fusion.8
  669.8 1.8 copy.70
  (324 shorter events, 86.6 us)
Async XLA Ops:
  20.8 4.8 copy-start.62
  20.8 5.4 copy-start.44
  20.8 5.9 copy-start.70
  20.8 7.1 %copy-start.60 = (bf16[768]{0:T(1024)(128)(2,1)S(1)}, bf16[768]{0:T(1024)(128)(2,1)}, u32[]{:S(2)}) copy-start(bf16[768]{0:T(1024)(128)(2,1)} %param.24) | copy-start | bytes 4612
  20.8 7.1 %copy-start.61 = (bf16[768]{0:T(1024)(128)(2,1)S(1)}, bf16[768]{0:T(1024)(128)(2,1)}, u32[]{:S(2)}) copy-start(bf16[768]{0:T(1024)(128)(2,1)} %param.27) | copy-start | bytes 4612
  20.8 7.1 %copy-start.63 = (bf16[192]{0:T(256)(128)(2,1)S(1)}, bf16[192]{0:T(256)(128)(2,1)}, u32[]{:S(2)}) copy-start(bf16[192]{0:T(256)(128)(2,1)} %param.25) | copy-start | bytes 1156
  20.8 7.1 %copy-start.64 = (bf16[192]{0:T(256)(128)(2,1)S(1)}, bf16[192]{0:T(256)(128)(2,1)}, u32[]{:S(2)}) copy-start(bf16[192]{0:T(256)(128)(2,1)} %param.26) | copy-start | bytes 1156
  20.8 7.1 %copy-start.65 = (bf16[192]{0:T(256)(128)(2,1)S(1)}, bf16[192]{0:T(256)(128)(2,1)}, u32[]{:S(2)}) copy-start(bf16[192]{0:T(256)(128)(2,1)} %param.28) | copy-start | bytes 1156
  20.8 7.1 %copy-start.66 = (bf16[192]{0:T(256)(128)(2,1)S(1)}, bf16[192]{0:T(256)(128)(2,1)}, u32[]{:S(2)}) copy-start(bf16[192]{0:T(256)(128)(2,1)} %param.29) | copy-start | bytes 1156
  20.8 7.1 %copy-start.67 = (bf16[192]{0:T(256)(128)(2,1)S(1)}, bf16[192]{0:T(256)(128)(2,1)}, u32[]{:S(2)}) copy-start(bf16[192]{0:T(256)(128)(2,1)} %param.30) | copy-start | bytes 1156
  20.8 7.1 %copy-start.68 = (bf16[192]{0:T(256)(128)(2,1)S(1)}, bf16[192]{0:T(256)(128)(2,1)}, u32[]{:S(2)}) copy-start(bf16[192]{0:T(256)(128)(2,1)} %param.31) | copy-start | bytes 1156
  20.9 7.1 %copy-start.69 = (bf16[192]{0:T(256)(128)(2,1)S(1)}, bf16[192]{0:T(256)(128)(2,1)}, u32[]{:S(2)}) copy-start(bf16[192]{0:T(256)(128)(2,1)} %param.32) | copy-start | bytes 1156
  20.9 21.5 %copy-start.40 = (bf16[4,128,768]{2,1,0:T(8,128)(2,1)S(1)}, bf16[4,128,768]{2,1,0:T(8,128)(2,1)}, u32[]{:S(2)}) copy-start(bf16[4,128,768]{2,1,0:T(8,128)(2,1)} %param.35) | copy-start | bytes 2359300
  23.3 42.1 %collective-permute-start.2 = (bf16[192,2304]{1,0:T(8,128)(2,1)}, bf16[192,2304]{1,0:T(8,128)(2,1)}, u32[]{:S(2)}, u32[]{:S(2)}) collective-permute-start(bf16[192,2304]{1,0:T(8,128)(2,1)} %bitcast.115), channel_id=1, source_target_pairs={{0,1},{1,0},{2,3},{3,2},{4,5},{5,4},{6,7},{7,6},{8,9},{9,8},{10,11... | collective-permute-start | bytes 2654216 | tf_op jit(solution)/shard_map/ppermute | solution.py:302
  25.5 30.4 %collective-permute-start = (bf16[4,64,768]{2,1,0:T(8,128)(2,1)}, bf16[4,64,768]{2,1,0:T(8,128)(2,1)S(1)}, u32[]{:S(2)}, u32[]{:S(2)}) collective-permute-start(bf16[4,64,768]{2,1,0:T(8,128)(2,1)} %dynamic-slice_bitcast_fusion.4), channel_id=1, source_target_pairs={{0,1},{1,0},{2,3},{3,2},{4,5},{5,4},{6,7},{7,6},{8,9},{9,8},{10,11... | collective-permute-start | bytes 1179656 | tf_op jit(solution)/shard_map/ppermute | solution.py:302
  25.6 20.5 %collective-permute-start.4 = (s32[4,1028]{1,0:T(4,128)S(1)}, s32[4,1028]{1,0:T(4,128)S(1)}, u32[]{:S(2)}, u32[]{:S(2)}) collective-permute-start(s32[4,1028]{1,0:T(4,128)S(1)} %constant_dynamic-update-slice_fusion), channel_id=1, source_target_pairs={{0,1},{1,0},{2,3},{3,2},{4,5},{5,4},{6,7},{7,6},{8,9},{9,8},{10,11... | collective-permute-start | bytes 49352 | tf_op jit(solution)/shard_map/ppermute | solution.py:302
  26.1 26.6 %collective-permute-start.6 = (bf16[192,768]{1,0:T(8,128)(2,1)S(1)}, bf16[192,768]{1,0:T(8,128)(2,1)S(1)}, u32[]{:S(2)}, u32[]{:S(2)}) collective-permute-start(bf16[192,768]{1,0:T(8,128)(2,1)S(1)} %copy-done.44), channel_id=1, source_target_pairs={{0,1},{1,0},{2,3},{3,2},{4,5},{5,4},{6,7},{7,6},{8,9},{9,8},{10,11... | collective-permute-start | bytes 884744 | tf_op jit(solution)/shard_map/ppermute | solution.py:302
  26.2 48.4 %collective-permute-start.8 = (bf16[192,3072]{1,0:T(8,128)(2,1)}, bf16[192,3072]{1,0:T(8,128)(2,1)}, u32[]{:S(2)}, u32[]{:S(2)}) collective-permute-start(bf16[192,3072]{1,0:T(8,128)(2,1)} %param.22), channel_id=1, source_target_pairs={{0,1},{1,0},{2,3},{3,2},{4,5},{5,4},{6,7},{7,6},{8,9},{9,8},{10,11... | collective-permute-start | bytes 3538952 | tf_op jit(solution)/shard_map/ppermute | solution.py:302
  43.3 13.1 %copy-start.39 = (bf16[4,128,768]{2,1,0:T(8,128)(2,1)S(1)}, bf16[4,128,768]{2,1,0:T(8,128)(2,1)}, u32[]{:S(2)}) copy-start(bf16[4,128,768]{2,1,0:T(8,128)(2,1)} %param.18) | copy-start | bytes 2359300
  46.1 44.3 %collective-permute-start.10 = (bf16[768,768]{1,0:T(8,128)(2,1)}, bf16[768,768]{1,0:T(8,128)(2,1)}, u32[]{:S(2)}, u32[]{:S(2)}) collective-permute-start(bf16[768,768]{1,0:T(8,128)(2,1)} %param.23), channel_id=1, source_target_pairs={{0,1},{1,0},{2,3},{3,2},{4,5},{5,4},{6,7},{7,6},{8,9},{9,8},{10,11... | collective-permute-start | bytes 3538952 | tf_op jit(solution)/shard_map/ppermute | solution.py:302
  53.5 9.9 %collective-permute-start.13 = (bf16[4,64,768]{2,1,0:T(8,128)(2,1)}, bf16[4,64,768]{2,1,0:T(8,128)(2,1)}, u32[]{:S(2)}, u32[]{:S(2)}) collective-permute-start(bf16[4,64,768]{2,1,0:T(8,128)(2,1)} %dynamic-slice_bitcast_fusion.2), channel_id=1, source_target_pairs={{0,1},{1,0},{2,3},{3,2},{4,5},{5,4},{6,7},{7,6},{8,9},{9,8},{10,11... | collective-permute-start | bytes 1179656 | tf_op jit(solution)/shard_map/ppermute | solution.py:302
  56.0 7.4 %copy-start.41 = (bf16[4,128,768]{2,1,0:T(8,128)(2,1)S(1)}, bf16[4,128,768]{2,1,0:T(8,128)(2,1)}, u32[]{:S(2)}) copy-start(bf16[4,128,768]{2,1,0:T(8,128)(2,1)} %param.35) | copy-start | bytes 2359300
  56.0 16.4 %collective-permute-start.7 = (bf16[2,192,768]{2,1,0:T(8,128)(2,1)}, bf16[2,192,768]{2,1,0:T(8,128)(2,1)}, u32[]{:S(2)}, u32[]{:S(2)}) collective-permute-start(bf16[2,192,768]{2,1,0:T(8,128)(2,1)} %pad_maximum_fusion.14), channel_id=1, source_target_pairs={{0,2},{2,0},{1,3},{3,1},{4,6},{6,4},{5,7},{7,5},{8,10},{10,8},{9,1... | collective-permute-start | bytes 1769480 | tf_op jit(solution)/shard_map/ppermute | solution.py:309
  57.4 26.3 %all-to-all-start = ((bf16[8,64,768]{2,1,0:T(8,128)(2,1)}), bf16[8,64,768]{2,1,0:T(8,128)(2,1)}, u32[]{:S(2)}, u32[]{:S(2)}) async-start(bf16[8,64,768]{2,1,0:T(8,128)(2,1)} %bitcast.5), calls=%async_computation | async-start | bytes 1572864 | tf_op jit(solution)/shard_map/all_to_all | solution.py:334
  66.7 6.8 copy-start.11
  66.7 6.8 copy-start.13
  68.2 42.1 %collective-permute-start.3 = (bf16[2,192,2304]{2,1,0:T(8,128)(2,1)}, bf16[2,192,2304]{2,1,0:T(8,128)(2,1)}, u32[]{:S(2)}, u32[]{:S(2)}) collective-permute-start(bf16[2,192,2304]{2,1,0:T(8,128)(2,1)} %pad_maximum_fusion.6), channel_id=1, source_target_pairs={{0,2},{2,0},{1,3},{3,1},{4,6},{6,4},{5,7},{7,5},{8,10},{10,8},{9,1... | collective-permute-start | bytes 5308424 | tf_op jit(solution)/shard_map/ppermute | solution.py:309
  83.6 60.5 %all-to-all-start.2 = ((bf16[8,64,768]{2,1,0:T(8,128)(2,1)}), bf16[8,64,768]{2,1,0:T(8,128)(2,1)S(1)}, u32[]{:S(2)}, u32[]{:S(2)}) async-start(bf16[8,64,768]{2,1,0:T(8,128)(2,1)} %bitcast.297), calls=%async_computation.2 | async-start | bytes 1572864 | tf_op jit(solution)/shard_map/all_to_all | solution.py:334
  87.2 568.0 %all-reduce.4.cloned.1.call-start = ((), (), s32[]{:S(2)}) async-start(), calls=%async_computation.4 | async-start | bytes 10027008 | tf_op jit(solution)/shard_map/psum | solution.py:453
  87.2 7.3 %collective-permute-start.1 = (bf16[512,768]{1,0:T(8,128)(2,1)}, bf16[512,768]{1,0:T(8,128)(2,1)S(1)}, u32[]{:S(2)}, u32[]{:S(2)}) collective-permute-start(bf16[512,768]{1,0:T(8,128)(2,1)} %bitcast.6), channel_id=1, source_target_pairs={{0,1},{1,0},{2,3},{3,2},{4,5},{5,4},{6,7},{7,6},{8,9},{9,8},{10,11... | collective-permute-start | bytes 2359304 | tf_op jit(solution)/shard_map/ppermute | solution.py:302
  89.0 71.9 %collective-permute-start.9 = (bf16[2,192,3072]{2,1,0:T(8,128)(2,1)}, bf16[2,192,3072]{2,1,0:T(8,128)(2,1)}, u32[]{:S(2)}, u32[]{:S(2)}) collective-permute-start(bf16[2,192,3072]{2,1,0:T(8,128)(2,1)} %pad_maximum_fusion.3), channel_id=1, source_target_pairs={{0,2},{2,0},{1,3},{3,1},{4,6},{6,4},{5,7},{7,5},{8,10},{10,8},{9,1... | collective-permute-start | bytes 7077896 | tf_op jit(solution)/shard_map/ppermute | solution.py:309
  93.9 116.6 %collective-permute-start.11 = (bf16[2,768,768]{2,1,0:T(8,128)(2,1)}, bf16[2,768,768]{2,1,0:T(8,128)(2,1)}, u32[]{:S(2)}, u32[]{:S(2)}) collective-permute-start(bf16[2,768,768]{2,1,0:T(8,128)(2,1)} %pad_maximum_fusion.4), channel_id=1, source_target_pairs={{0,2},{2,0},{1,3},{3,1},{4,6},{6,4},{5,7},{7,5},{8,10},{10,8},{9,1... | collective-permute-start | bytes 7077896 | tf_op jit(solution)/shard_map/ppermute | solution.py:309
  95.9 14.4 %copy-start.12 = (bf16[1,192,2304]{2,1,0:T(8,128)(2,1)S(1)}, bf16[1,192,2304]{2,1,0:T(8,128)(2,1)}, u32[]{:S(2)}) copy-start(bf16[1,192,2304]{2,1,0:T(8,128)(2,1)} %copy-done.11) | copy-start | bytes 2654212
  95.9 14.4 %copy-start.14 = (bf16[1,192,2304]{2,1,0:T(8,128)(2,1)S(1)}, bf16[1,192,2304]{2,1,0:T(8,128)(2,1)}, u32[]{:S(2)}) copy-start(bf16[1,192,2304]{2,1,0:T(8,128)(2,1)} %copy-done.13) | copy-start | bytes 2654212
  144.2 5.1 collective-permute-start.5
  144.2 5.1 copy-start.5
  163.2 18.8 %copy-start.18 = (bf16[2,2,192,3072]{3,2,1,0:T(8,128)(2,1)}, bf16[2,2,192,3072]{3,2,1,0:T(8,128)(2,1)S(1)}, u32[]{:S(2)}) copy-start(bf16[2,2,192,3072]{3,2,1,0:T(8,128)(2,1)S(1)} %pad_maximum_fusion) | copy-start | bytes 14155780
  220.0 11.6 %slice-start = ((s8[4718592]{0:T(1024)(128)(4,1)}), s8[524288]{0:T(1024)(128)(4,1)S(1)}, s32[]{:S(2)}) async-start(s8[4718592]{0:T(1024)(128)(4,1)} %bitcast.284), calls=%async_computation.5 | async-start | bytes 1048576
  222.8 8.8 %copy-start.25 = (bf16[512,768]{1,0:T(8,128)(2,1)}, bf16[512,768]{1,0:T(8,128)(2,1)S(1)}, u32[]{:S(2)}) copy-start(bf16[512,768]{1,0:T(8,128)(2,1)S(1)} %get-tuple-element.47) | copy-start | bytes 2359300
  222.8 8.8 %slice-start.1 = ((s8[4718592]{0:T(1024)(128)(4,1)}), s8[4194304]{0:T(1024)(128)(4,1)S(1)}, s32[]{:S(2)}) async-start(s8[4718592]{0:T(1024)(128)(4,1)} %bitcast.284), calls=%async_computation.6 | async-start | bytes 8388608
  231.6 6.3 copy-start.22
  252.0 34.3 %collective-permute-start.14 = (bf16[512,384]{0,1:T(8,128)(2,1)}, bf16[512,384]{0,1:T(8,128)(2,1)}, u32[]{:S(2)}, u32[]{:S(2)}) collective-permute-start(bf16[512,384]{0,1:T(8,128)(2,1)} %bitcast.324), channel_id=1, source_target_pairs={{0,1},{1,0},{2,3},{3,2},{4,5},{5,4},{6,7},{7,6},{8,9},{9,8},{10,11... | collective-permute-start | bytes 1179656 | tf_op jit(solution)/shard_map/ppermute | solution.py:302
  264.2 6.9 %copy-start.26 = (bf16[512,768]{1,0:T(8,128)(2,1)S(1)}, bf16[512,768]{1,0:T(8,128)(2,1)}, u32[]{:S(2)}) copy-start(bf16[512,768]{1,0:T(8,128)(2,1)} %copy-done.25) | copy-start | bytes 2359300
  273.9 71.3 %collective-permute-start.23 = (bf16[1536,768]{1,0:T(8,128)(2,1)}, bf16[1536,768]{1,0:T(8,128)(2,1)}, u32[]{:S(2)}, u32[]{:S(2)}) collective-permute-start(bf16[1536,768]{1,0:T(8,128)(2,1)} %convolution_convert_fusion.1), channel_id=1, source_target_pairs={{0,1},{1,0},{2,3},{3,2},{4,5},{5,4},{6,7},{7,6},{8,9},{9,8},{10,11... | collective-permute-start | bytes 7077896 | tf_op jit(solution)/shard_map/ppermute | solution.py:302
  283.4 69.3 %collective-permute-start.21 = (bf16[384,3072]{1,0:T(8,128)(2,1)}, bf16[384,3072]{1,0:T(8,128)(2,1)S(1)}, u32[]{:S(2)}, u32[]{:S(2)}) collective-permute-start(bf16[384,3072]{1,0:T(8,128)(2,1)} %convolution_convert_fusion), channel_id=1, source_target_pairs={{0,1},{1,0},{2,3},{3,2},{4,5},{5,4},{6,7},{7,6},{8,9},{9,8},{10,11... | collective-permute-start | bytes 7077896 | tf_op jit(solution)/shard_map/ppermute | solution.py:302
  285.8 56.2 %collective-permute-start.19 = (bf16[384,768]{1,0:T(8,128)(2,1)}, bf16[384,768]{1,0:T(8,128)(2,1)}, u32[]{:S(2)}, u32[]{:S(2)}) collective-permute-start(bf16[384,768]{1,0:T(8,128)(2,1)} %convolution_convert_fusion.4), channel_id=1, source_target_pairs={{0,1},{1,0},{2,3},{3,2},{4,5},{5,4},{6,7},{7,6},{8,9},{9,8},{10,11... | collective-permute-start | bytes 1769480 | tf_op jit(solution)/shard_map/ppermute | solution.py:302
  335.6 5.6 copy-start.4
  341.4 48.6 %collective-permute-start.17 = (bf16[384,2304]{1,0:T(8,128)(2,1)S(1)}, bf16[384,2304]{1,0:T(8,128)(2,1)S(1)}, u32[]{:S(2)}, u32[]{:S(2)}) collective-permute-start(bf16[384,2304]{1,0:T(8,128)(2,1)S(1)} %fusion.11), channel_id=1, source_target_pairs={{0,2},{2,0},{1,3},{3,1},{4,6},{6,4},{5,7},{7,5},{8,10},{10,8},{9,1... | collective-permute-start | bytes 5308424 | tf_op jit(solution)/shard_map/ppermute | solution.py:433
  344.0 45.3 %collective-permute-start.20 = (bf16[192,768]{1,0:T(8,128)(2,1)S(1)}, bf16[192,768]{1,0:T(8,128)(2,1)S(1)}, u32[]{:S(2)}, u32[]{:S(2)}) collective-permute-start(bf16[192,768]{1,0:T(8,128)(2,1)S(1)} %fusion.40), channel_id=1, source_target_pairs={{0,2},{2,0},{1,3},{3,1},{4,6},{6,4},{5,7},{7,5},{8,10},{10,8},{9,1... | collective-permute-start | bytes 884744 | tf_op jit(solution)/shard_map/ppermute | solution.py:433
  345.2 7.5 %copy-start.24 = (bf16[512,3072]{1,0:T(8,128)(2,1)S(1)}, bf16[512,3072]{1,0:T(8,128)(2,1)}, u32[]{:S(2)}) copy-start(bf16[512,3072]{1,0:T(8,128)(2,1)} %copy-done.22) | copy-start | bytes 9437188
  351.7 62.9 %collective-permute-start.24 = (bf16[768,768]{1,0:T(8,128)(2,1)}, bf16[768,768]{1,0:T(8,128)(2,1)}, u32[]{:S(2)}, u32[]{:S(2)}) collective-permute-start(bf16[768,768]{1,0:T(8,128)(2,1)} %fusion.21), channel_id=1, source_target_pairs={{0,2},{2,0},{1,3},{3,1},{4,6},{6,4},{5,7},{7,5},{8,10},{10,8},{9,1... | collective-permute-start | bytes 3538952 | tf_op jit(solution)/shard_map/ppermute | solution.py:433
  357.5 81.3 %collective-permute-start.22 = (bf16[192,3072]{1,0:T(8,128)(2,1)}, bf16[192,3072]{1,0:T(8,128)(2,1)S(1)}, u32[]{:S(2)}, u32[]{:S(2)}) collective-permute-start(bf16[192,3072]{1,0:T(8,128)(2,1)} %fusion.20), channel_id=1, source_target_pairs={{0,2},{2,0},{1,3},{3,1},{4,6},{6,4},{5,7},{7,5},{8,10},{10,8},{9,1... | collective-permute-start | bytes 3538952 | tf_op jit(solution)/shard_map/ppermute | solution.py:433
  451.1 9.4 %collective-permute-start.15 = (bf16[512,768]{1,0:T(8,128)(2,1)S(1)}, bf16[512,768]{1,0:T(8,128)(2,1)}, u32[]{:S(2)}, u32[]{:S(2)}) collective-permute-start(bf16[512,768]{1,0:T(8,128)(2,1)S(1)} %dynamic-slice_bitcast_fusion), channel_id=1, source_target_pairs={{0,1},{1,0},{2,3},{3,2},{4,5},{5,4},{6,7},{7,6},{8,9},{9,8},{10,11... | collective-permute-start | bytes 2359304 | tf_op jit(solution)/shard_map/ppermute | solution.py:302
  451.2 48.5 %all-to-all-start.1 = ((bf16[8,64,768]{2,1,0:T(8,128)(2,1)}), bf16[8,64,768]{2,1,0:T(8,128)(2,1)S(1)}, u32[]{:S(2)}, u32[]{:S(2)}) async-start(bf16[8,64,768]{2,1,0:T(8,128)(2,1)} %bitcast.296), calls=%async_computation.1 | async-start | bytes 1572864 | tf_op jit(solution)/shard_map/all_to_all | solution.py:337
  463.2 40.2 %copy-start.55 = (f32[3072]{0:T(1024)S(1)}, f32[3072]{0:T(1024)}, u32[]{:S(2)}) copy-start(f32[3072]{0:T(1024)} %get-tuple-element.49) | copy-start | bytes 36868
  463.2 40.2 %copy-start.51 = (f32[768]{0:T(1024)S(1)}, f32[768]{0:T(1024)}, u32[]{:S(2)}) copy-start(f32[768]{0:T(1024)} %get-tuple-element.46) | copy-start | bytes 9220
  463.2 40.3 %copy-start.59 = (f32[768]{0:T(1024)S(1)}, f32[768]{0:T(1024)}, u32[]{:S(2)}) copy-start(f32[768]{0:T(1024)} %get-tuple-element.32) | copy-start | bytes 9220
  463.2 40.3 %copy-start.58 = (f32[768]{0:T(1024)S(1)}, f32[768]{0:T(1024)}, u32[]{:S(2)}) copy-start(f32[768]{0:T(1024)} %get-tuple-element.39) | copy-start | bytes 9220
  463.2 40.3 %copy-start.48 = (f32[768]{0:T(1024)S(1)}, f32[768]{0:T(1024)}, u32[]{:S(2)}) copy-start(f32[768]{0:T(1024)} %get-tuple-element.34) | copy-start | bytes 9220
  463.2 40.3 %copy-start.46 = (f32[768]{0:T(1024)S(1)}, f32[768]{0:T(1024)}, u32[]{:S(2)}) copy-start(f32[768]{0:T(1024)} %get-tuple-element.40) | copy-start | bytes 9220
  499.7 58.7 %all-to-all-start.3 = ((bf16[8,64,768]{2,1,0:T(8,128)(2,1)}), bf16[8,64,768]{2,1,0:T(8,128)(2,1)S(1)}, u32[]{:S(2)}, u32[]{:S(2)}) async-start(bf16[8,64,768]{2,1,0:T(8,128)(2,1)} %bitcast.69), calls=%async_computation.3 | async-start | bytes 1572864 | tf_op jit(solution)/shard_map/all_to_all | solution.py:337
  558.3 104.8 %collective-permute-start.12 = (bf16[4,64,768]{2,1,0:T(8,128)(2,1)S(1)}, bf16[4,64,768]{2,1,0:T(8,128)(2,1)S(1)}, u32[]{:S(2)}, u32[]{:S(2)}) collective-permute-start(bf16[4,64,768]{2,1,0:T(8,128)(2,1)S(1)} %dynamic-slice_bitcast_fusion.3), channel_id=1, source_target_pairs={{0,1},{1,0},{2,3},{3,2},{4,5},{5,4},{6,7},{7,6},{8,9},{9,8},{10,11... | collective-permute-start | bytes 1179656 | tf_op jit(solution)/shard_map/ppermute | solution.py:302
  558.4 105.7 %collective-permute-start.16 = (bf16[4,64,768]{2,1,0:T(8,128)(2,1)S(1)}, bf16[4,64,768]{2,1,0:T(8,128)(2,1)S(1)}, u32[]{:S(2)}, u32[]{:S(2)}) collective-permute-start(bf16[4,64,768]{2,1,0:T(8,128)(2,1)S(1)} %dynamic-slice_bitcast_fusion.1), channel_id=1, source_target_pairs={{0,1},{1,0},{2,3},{3,2},{4,5},{5,4},{6,7},{7,6},{8,9},{9,8},{10,11... | collective-permute-start | bytes 1179656 | tf_op jit(solution)/shard_map/ppermute | solution.py:302
  657.2 12.1 %collective-permute-start.18 = (bf16[192,6,384]{2,0,1:T(8,128)(2,1)S(1)}, bf16[192,6,384]{2,0,1:T(8,128)(2,1)S(1)}, u32[]{:S(2)}, u32[]{:S(2)}) collective-permute-start(bf16[192,6,384]{2,0,1:T(8,128)(2,1)S(1)} %bitcast.314), channel_id=1, source_target_pairs={{0,1},{1,0},{2,3},{3,2},{4,5},{5,4},{6,7},{7,6},{8,9},{9,8},{10,11... | collective-permute-start | bytes 2654216 | tf_op jit(solution)/shard_map/ppermute | solution.py:302
  (39 other events, 89.1 us)
Sparse Core Ops, SparseCore 0:
  441.9 213.2 all-reduce.3

commit v2 on v1

--- a/solution.py
+++ b/solution.py
@@ -480,6 +480,884 @@
     return (output, input_grad, g_w_query, g_w_kv, g_w_out, g_w_up, g_w_down, *pieces)
 
 
+def project_kernel(
+    heads, hd, query_rows, kv_rows, at_ref, own_ref, other_ref, bias_ref, ent_ref, *refs
+):
+    n_query, n_kv = len(query_rows), len(kv_rows)
+    query_refs, kv_refs = refs[:n_query], refs[n_query : n_query + n_kv]
+    qcat_ref, kcat_ref, vaug_ref, w_ref, sems = refs[n_query + n_kv :]
+    span = heads * hd
+    half, width = own_ref.shape
+    block = min(256, half)
+    scale = hd ** (-0.5)
+    core = at_ref[0]
+    made = []
+    for i, (ref, rows) in enumerate(zip(query_refs + kv_refs, query_rows + kv_rows)):
+        first, blocks = (0, 4) if i < n_query else (4, 2)
+        to = pl.ds(pl.multiple_of(at_ref[1 + i], 16), rows)
+        for b in range(blocks):
+            here = pl.ds(pl.multiple_of(b * width + core * span, LANES), span)
+            cols = slice((first + b) * span, (first + b + 1) * span)
+            copy = pltpu.make_async_copy(ref.at[:, here], w_ref.at[to, cols], sems.at[len(made)])
+            copy.start()
+            made.append(copy)
+    lane = lax.broadcasted_iota(jnp.int32, (block, LANES - hd), 1)
+    tail = jnp.where(lane < 2, -1.0, jnp.where(lane == 2, 1.0, 0.0)).astype(BF)
+    for copy in made:
+        copy.wait()
+    for side, rows_ref in enumerate((own_ref, other_ref)):
+
+        def project(piece, carry, side=side, rows_ref=rows_ref):
+            rows = rows_ref[pl.ds(pl.multiple_of(piece * block, block), block), :]
+            at = pl.ds(pl.multiple_of(side * half + piece * block, block), block)
+            ent = ent_ref[at, :hd]
+            wide = ent_ref[at, :1] > 0
+            word = (1 - ent).astype(BF)
+
+            def part(index):
+                cols = slice(index * span, (index + 1) * span)
+                return jnp.dot(rows, w_ref[:, cols], preferred_element_type=F32) + bias_ref[:, cols]
+
+            q_word = (jnp.where(wide, part(2), part(0))).astype(BF) * BF(scale)
+            q_ent = (jnp.where(wide, part(3), part(1))).astype(BF) * BF(scale)
+            keys = part(4).astype(BF)
+            vals = part(5).astype(BF)
+            for h in range(heads):
+                cut = slice(h * hd, (h + 1) * hd)
+                qcat_ref[h, at, :] = jnp.concatenate([q_word[:, cut], q_ent[:, cut]], axis=1)
+                kcat_ref[h, at, :] = jnp.concatenate([keys[:, cut] * word, keys[:, cut] * ent], axis=1)
+                vaug_ref[h, at, :] = jnp.concatenate([vals[:, cut], tail], axis=1)
+            return carry
+
+        lax.fori_loop(0, half // block, project, 0)
+
+
+def row_project(at, own, other, bias, ent, query_pieces, kv_pieces, heads, hd):
+    half, width = own.shape
+    full = 2 * half
+    span = heads * hd
+    vmem = pl.BlockSpec(memory_space=pltpu.VMEM)
+    anywhere = pl.BlockSpec(memory_space=pl.ANY)
+    query_rows = tuple(p.shape[0] for p in query_pieces)
+    kv_rows = tuple(p.shape[0] for p in kv_pieces)
+    return pl.pallas_call(
+        functools.partial(project_kernel, heads, hd, query_rows, kv_rows),
+        in_specs=[pl.BlockSpec(memory_space=pltpu.SMEM)]
+        + [vmem] * 4
+        + [anywhere] * (len(query_pieces) + len(kv_pieces)),
+        out_specs=[vmem] * 4,
+        out_shape=[
+            jax.ShapeDtypeStruct((heads, full, 2 * hd), BF),
+            jax.ShapeDtypeStruct((heads, full, 2 * hd), BF),
+            jax.ShapeDtypeStruct((heads, full, LANES), BF),
+            jax.ShapeDtypeStruct((width, 6 * span), BF),
+        ],
+        scratch_shapes=[pltpu.SemaphoreType.DMA((4 * len(query_pieces) + 2 * len(kv_pieces),))],
+        compiler_params=pltpu.CompilerParams(vmem_limit_bytes=60 << 20),
+        cost_estimate=pl.CostEstimate(
+            flops=2 * full * width * 6 * span, bytes_accessed=18 * full * width, transcendentals=0
+        ),
+        name="row_project",
+    )(at, own, other, bias, ent, *query_pieces, *kv_pieces)
+
+
+def attend_kernel(
+    heads, hd, qcat_ref, qseg_ref, kcat_ref, kseg_ref, vaug_ref, keep_ref, send_ref, wts_ref, inv_ref, score_s
+):
+    step = pl.program_id(0)
+    block = keep_ref.shape[0]
+    q_seg = qseg_ref[...]
+    lane = lax.broadcasted_iota(jnp.int32, (block, LANES), 1)
+    inv_all = jnp.zeros((block, LANES), F32)
+    mixed = []
+    for h in range(heads):
+        q_aug = jnp.concatenate([qcat_ref[h], q_seg], axis=1)
+        k_aug = jnp.concatenate([kcat_ref[h], kseg_ref[...]], axis=1)
+        score_s[h % 2] = lax.dot_general(
+            q_aug, k_aug, (((1,), (1,)), ((), ())), preferred_element_type=F32
+        )
+        for r in range(0, block, CHUNK):
+            s = score_s[h % 2, r : r + CHUNK, :]
+            top = jnp.max(s, axis=1, keepdims=True)
+            wts_ref[h, r : r + CHUNK, :] = jnp.exp(s - top).astype(BF)
+        out = jnp.dot(wts_ref[h], vaug_ref[h], preferred_element_type=F32)
+        inv = 1.0 / out[:, hd + 2 : hd + 3]
+        inv_all = jnp.where(lane == h, inv, inv_all)
+        mixed.append((out[:, :hd] * inv).astype(BF))
+    mixed = jnp.concatenate(mixed, axis=1)
+    inv_ref[...] = inv_all
+    late = pl.num_programs(0) // 2
+
+    @pl.when(step < late)
+    def _():
+        send_ref[...] = mixed
+
+    @pl.when(step >= late)
+    def _():
+        keep_ref[...] = mixed
+
+
+def row_attend(qcat, kcat, vaug, qseg, kseg, heads, hd):
+    full = qcat.shape[1]
+    half = full // 2
+    block = min(256, half)
+    span = heads * hd
+    first = half // block
+    whole = lambda *dims: pl.BlockSpec(dims, lambda i: (0,) * len(dims))
+    turn = lambda i: jnp.where(i < first, i + first, i - first)
+    return pl.pallas_call(
+        functools.partial(attend_kernel, heads, hd),
+        grid=(full // block,),
+        in_specs=[
+            pl.BlockSpec((heads, block, 2 * hd), lambda i: (0, turn(i), 0)),
+            pl.BlockSpec((block, LANES), lambda i: (turn(i), 0)),
+            whole(heads, full, 2 * hd),
+            whole(full, LANES),
+            whole(heads, full, LANES),
+        ],
+        out_specs=[
+            pl.BlockSpec((block, span), lambda i: (jnp.maximum(i - first, 0), 0)),
+            pl.BlockSpec((block, span), lambda i: (jnp.minimum(i, first - 1), 0)),
+            pl.BlockSpec((heads, block, full), lambda i: (0, turn(i), 0)),
+            pl.BlockSpec((block, LANES), lambda i: (turn(i), 0)),
+        ],
+        out_shape=[
+            jax.ShapeDtypeStruct((half, span), BF),
+            jax.ShapeDtypeStruct((half, span), BF),
+            jax.ShapeDtypeStruct((heads, full, full), BF),
+            jax.ShapeDtypeStruct((full, LANES), F32),
+        ],
+        scratch_shapes=[pltpu.VMEM((2, block, full), F32)],
+        compiler_params=pltpu.CompilerParams(vmem_limit_bytes=60 << 20),
+        cost_estimate=pl.CostEstimate(
+            flops=8 * heads * full * full * LANES,
+            bytes_accessed=2 * heads * full * full + 4 * full * LANES * heads,
+            transcendentals=heads * full * full,
+        ),
+        name="row_attend",
+    )(qcat, qseg, kcat, kseg, vaug)
+
+
+def token_kernel(
+    out_rows, up_rows, down_rows, at_ref, own_ref, mine_ref, theirs_ref, cot_ref, vec_ref, *refs
+):
+    groups = (out_rows, up_rows, down_rows)
+    sets, at = [], 0
+    for rows in groups:
+        sets.append(refs[at : at + len(rows)])
+        at += len(rows)
+    (
+        result_ref, gy1_ref, gmine_ref, gtheirs_ref, act_ref, hlow_ref, gffn_ref, gup_ref, gattn_ref,
+        small_ref, wout_s, wup_s, wdown_s, acc_s, hid_s, norm_s, inv_s, slope_s, gy2_s, tmp_s, sum_s, sems,
+    ) = refs[at:]
+    total, width = own_ref.shape
+    ff = wup_s.shape[1]
+    parts = ff // width
+    span = mine_ref.shape[1]
+    core = at_ref[0]
+    made, slot = [], 0
+    for rows, piece_refs, dst in zip(groups, sets, (wout_s, wup_s, wdown_s)):
+        batch = []
+        for n, ref in zip(rows, piece_refs):
+            to = pl.ds(pl.multiple_of(at_ref[1 + slot], 16), n)
+            copy = pltpu.make_async_copy(ref, dst.at[to, :], sems.at[slot])
+            copy.start()
+            batch.append(copy)
+            slot += 1
+        made.append(batch)
+
+    def wait(index):
+        for copy in made[index]:
+            copy.wait()
+
+    def row(index):
+        return vec_ref[index : index + 1, :]
+
+    rows_at = lambda i, n: pl.ds(pl.multiple_of(i * n, n), n)
+    chunk = 16
+    mine_rows = pl.ds(pl.multiple_of(core * span, LANES), span)
+    other_rows = pl.ds(pl.multiple_of((1 - core) * span, LANES), span)
+    sum_s[...] = jnp.zeros_like(sum_s)
+    wait(0)
+    acc_s[...] = jnp.dot(mine_ref[...], wout_s[mine_rows, :], preferred_element_type=F32)
+    acc_s[...] += jnp.dot(theirs_ref[...], wout_s[other_rows, :], preferred_element_type=F32)
+
+    def first_norm(i, carry):
+        at = rows_at(i, chunk)
+        y = own_ref[at, :].astype(F32) + (acc_s[at, :] + row(4))
+        center = y - jnp.mean(y, axis=1, keepdims=True)
+        inv = lax.rsqrt(jnp.mean(center * center, axis=1, keepdims=True) + EPSILON)
+        normed = center * inv
+        hidden = normed * row(6) + row(7)
+        norm_s[at, :] = normed
+        inv_s[at, :] = jnp.broadcast_to(inv, (chunk, LANES))
+        hid_s[at, :] = hidden
+        hlow_ref[at, :] = hidden.astype(BF)
+        return carry
+
+    lax.fori_loop(0, total // chunk, first_norm, 0, unroll=4)
+    wait(1)
+    for c in range(parts):
+        cols = slice(c * width, (c + 1) * width)
+        tmp_s[c % 2] = jnp.dot(hlow_ref[...], wup_s[:, cols], preferred_element_type=F32)
+        for r in range(0, total, chunk):
+            x = tmp_s[c % 2, r : r + chunk, :] + row(c)
+            cdf = 0.5 + 0.5 * lax.erf(x * (0.5**0.5))
+            act_ref[r : r + chunk, cols] = (x * cdf).astype(BF)
+            slope_s[r : r + chunk, cols] = cdf + x * (jnp.exp(-0.5 * x * x) * (0.15915494309189535**0.5))
+    wait(2)
+    acc_s[...] = jnp.dot(act_ref[...], wdown_s[...], preferred_element_type=F32)
+
+    def second_norm(i, carry):
+        at = rows_at(i, chunk)
+        y = hid_s[at, :] + (acc_s[at, :] + row(5))
+        center = y - jnp.mean(y, axis=1, keepdims=True)
+        inv = lax.rsqrt(jnp.mean(center * center, axis=1, keepdims=True) + EPSILON)
+        normed = center * inv
+        result_ref[at, :] = (normed * row(8) + row(9)).astype(BF)
+        cot = cot_ref[at, :].astype(F32)
+        sum_s[2] += cot * normed
+        sum_s[3] += cot
+        scaled = cot * row(8)
+        g = inv * (
+            scaled
+            - jnp.mean(scaled, axis=1, keepdims=True)
+            - normed * jnp.mean(scaled * normed, axis=1, keepdims=True)
+        )
+        gy2_s[at, :] = g
+        gffn_ref[at, :] = g.astype(BF)
+        return carry
+
+    lax.fori_loop(0, total // chunk, second_norm, 0, unroll=2)
+    ones = jnp.ones((8, total), BF)
+    for c in range(parts):
+        cols = slice(c * width, (c + 1) * width)
+        tmp_s[c % 2] = lax.dot_general(
+            gffn_ref[...], wdown_s[cols, :], (((1,), (1,)), ((), ())), preferred_element_type=F32
+        )
+        for r in range(0, total, chunk):
+            gup_ref[r : r + chunk, cols] = (
+                tmp_s[c % 2, r : r + chunk, :] * slope_s[r : r + chunk, cols]
+            ).astype(BF)
+        small_ref[c : c + 1, :] = jnp.dot(ones, gup_ref[:, cols], preferred_element_type=F32)[:1]
+    acc_s[...] = lax.dot_general(
+        gup_ref[...], wup_s[...], (((1,), (1,)), ((), ())), preferred_element_type=F32
+    )
+
+    def first_back(i, carry):
+        at = rows_at(i, chunk)
+        g_in = gy2_s[at, :] + acc_s[at, :]
+        normed = norm_s[at, :]
+        sum_s[0] += g_in * normed
+        sum_s[1] += g_in
+        scaled = g_in * row(6)
+        g = inv_s[at, :1] * (
+            scaled
+            - jnp.mean(scaled, axis=1, keepdims=True)
+            - normed * jnp.mean(scaled * normed, axis=1, keepdims=True)
+        )
+        gy1_ref[at, :] = g
+        gattn_ref[at, :] = g.astype(BF)
+        return carry
+
+    lax.fori_loop(0, total // chunk, first_back, 0, unroll=2)
+    gmine_ref[...] = lax.dot_general(
+        gattn_ref[...], wout_s[mine_rows, :], (((1,), (1,)), ((), ())), preferred_element_type=F32
+    ).astype(BF)
+    gtheirs_ref[...] = lax.dot_general(
+        gattn_ref[...], wout_s[other_rows, :], (((1,), (1,)), ((), ())), preferred_element_type=F32
+    ).astype(BF)
+    small_ref[4:5, :] = jnp.dot(ones, gattn_ref[...], preferred_element_type=F32)[:1]
+    small_ref[5:6, :] = jnp.dot(ones, gffn_ref[...], preferred_element_type=F32)[:1]
+    for i in range(4):
+        small_ref[6 + i : 7 + i, :] = jnp.sum(sum_s[i], axis=0, keepdims=True)
+    small_ref[10:, :] = jnp.zeros((small_ref.shape[0] - 10, width), F32)
+
+
+def token_block(at, own, mine, theirs, cot, vec, out_pieces, up_pieces, down_pieces):
+    total, width = own.shape
+    span = mine.shape[1]
+    ff = up_pieces[0].shape[1]
+    vmem = pl.BlockSpec(memory_space=pltpu.VMEM)
+    pieces = [*out_pieces, *up_pieces, *down_pieces]
+    shapes = [
+        ((total, width), BF), ((total, width), F32), ((total, span), BF), ((total, span), BF),
+        ((total, ff), BF), ((total, width), BF), ((total, width), BF), ((total, ff), BF),
+        ((total, width), BF), ((16, width), F32),
+    ]
+    rows = lambda group: tuple(p.shape[0] for p in group)
+    return pl.pallas_call(
+        functools.partial(token_kernel, rows(out_pieces), rows(up_pieces), rows(down_pieces)),
+        in_specs=[pl.BlockSpec(memory_space=pltpu.SMEM)]
+        + [vmem] * 5
+        + [pl.BlockSpec(memory_space=pl.ANY)] * len(pieces),
+        out_specs=[vmem] * len(shapes),
+        out_shape=[jax.ShapeDtypeStruct(s, d) for s, d in shapes],
+        scratch_shapes=[
+            pltpu.VMEM((width, width), BF),
+            pltpu.VMEM((width, ff), BF),
+            pltpu.VMEM((ff, width), BF),
+            pltpu.VMEM((total, width), F32),
+            pltpu.VMEM((total, width), F32),
+            pltpu.VMEM((total, width), F32),
+            pltpu.VMEM((total, LANES), F32),
+            pltpu.VMEM((total, ff), F32),
+            pltpu.VMEM((total, width), F32),
+            pltpu.VMEM((2, total, width), F32),
+            pltpu.VMEM((4, 16, width), F32),
+            pltpu.SemaphoreType.DMA((len(pieces),)),
+        ],
+        compiler_params=pltpu.CompilerParams(vmem_limit_bytes=60 << 20),
+        cost_estimate=pl.CostEstimate(
+            flops=2 * total * width * (4 * ff + 2 * width),
+            bytes_accessed=4 * width * ff + 6 * total * ff,
+            transcendentals=2 * total * ff,
+        ),
+        name="token_block",
+    )(at, own, mine, theirs, cot, vec, *pieces)
+
+
+def weight_kernel(
+    at_ref, mine_ref, theirs_ref, hlow_ref, act_ref, gffn_ref, gup_ref, gattn_ref,
+    up_send, rest_send, up_keep, rest_keep, hid_t, att_t,
+):
+    total, width = hlow_ref.shape
+    span = mine_ref.shape[1]
+    ff = act_ref.shape[1]
+    core = at_ref[0]
+    n, wide = width // 4, ff // 4
+    hid_t[...] = hlow_ref[...].T
+    att_t[pl.ds(pl.multiple_of(core * span, LANES), span), :] = mine_ref[...].T
+    att_t[pl.ds(pl.multiple_of((1 - core) * span, LANES), span), :] = theirs_ref[...].T
+    for which, up_ref, rest_ref in ((1 - core, up_send, rest_send), (core, up_keep, rest_keep)):
+        for outer in range(2):
+            shard = 2 * outer + which
+            rows = pl.ds(pl.multiple_of(shard * n, 16), n)
+            left = hid_t[rows, :]
+            for i in range(8):
+                up_ref[outer, i] = jnp.dot(
+                    left, gup_ref[:, i * span : (i + 1) * span], preferred_element_type=F32
+                ).astype(BF)
+            left = act_ref[:, pl.ds(pl.multiple_of(shard * wide, LANES), wide)]
+            down = lax.dot_general(left, gffn_ref[...], (((0,), (0,)), ((), ())), preferred_element_type=F32)
+            out = jnp.dot(att_t[rows, :], gattn_ref[...], preferred_element_type=F32)
+            for i in range(8):
+                r, c = i // 2, i % 2
+                cols = slice(c * span, (c + 1) * span)
+                rest_ref[outer, i, : wide // 4, :] = down[r * wide // 4 : (r + 1) * wide // 4, cols].astype(BF)
+                rest_ref[outer, i, wide // 4 :, :] = out[r * n // 4 : (r + 1) * n // 4, cols].astype(BF)
+
+
+def weight_grads(at, mine, theirs, hlow, act, gffn, gup, gattn):
+    total, width = hlow.shape
+    span = mine.shape[1]
+    ff = act.shape[1]
+    vmem = pl.BlockSpec(memory_space=pltpu.VMEM)
+    shapes = [(2, 8, width // 4, ff // 8), (2, 8, ff // 16 + width // 16, span)] * 2
+    return pl.pallas_call(
+        weight_kernel,
+        in_specs=[pl.BlockSpec(memory_space=pltpu.SMEM)] + [vmem] * 7,
+        out_specs=[vmem] * 4,
+        out_shape=[jax.ShapeDtypeStruct(s, BF) for s in shapes],
+        scratch_shapes=[pltpu.VMEM((width, total), BF), pltpu.VMEM((width, total), BF)],
+        compiler_params=pltpu.CompilerParams(vmem_limit_bytes=60 << 20),
+        cost_estimate=pl.CostEstimate(
+            flops=2 * total * width * (2 * ff + width),
+            bytes_accessed=4 * width * ff + 6 * total * ff,
+            transcendentals=0,
+        ),
+        name="weight_grads",
+    )(at, mine, theirs, hlow, act, gffn, gup, gattn)
+
+
+def row_backward_kernel(
+    heads, hd, first_head, gmine_ref, gother_ref, keep_ref, send_ref, inv_ref, wts_ref, qcat_ref, kcat_ref,
+    vaug_ref, ent_ref, entb_ref, *refs,
+):
+    gq_ref, gkv_ref, gscore_s, low_s, gk_s, gv_s = refs[-6:]
+    step = pl.program_id(0)
+    block = gmine_ref.shape[0]
+    full = kcat_ref.shape[1]
+    scale = hd ** (-0.5)
+    lane = lax.broadcasted_iota(jnp.int32, (block, LANES - hd), 1)
+    is_ent = entb_ref[:, :1] > 0
+    early = step < pl.num_programs(0) // 2
+    g_all = jnp.where(early, gmine_ref[...], gother_ref[...])
+    att_all = jnp.where(early, keep_ref[...], send_ref[...])
+    g_word, g_ent = [], []
+    for h in range(heads):
+        cut = slice(h * hd, (h + 1) * hd)
+        g_low = (g_all[:, cut].astype(F32) * inv_ref[:, first_head + h : first_head + h + 1]).astype(BF)
+        delta = jnp.sum(g_low.astype(F32) * att_all[:, cut].astype(F32), axis=1, keepdims=True)
+        d_hi = delta.astype(BF)
+        d_lo = (delta - d_hi.astype(F32)).astype(BF)
+        extra = jnp.where(
+            lane == 0, d_hi.astype(F32), jnp.where(lane == 1, d_lo.astype(F32), 0.0)
+        ).astype(BF)
+        g_aug = jnp.concatenate([g_low, extra], axis=1)
+        gscore_s[h % 2] = lax.dot_general(
+            g_aug, vaug_ref[h], (((1,), (1,)), ((), ())), preferred_element_type=F32
+        )
+        for r in range(0, block, CHUNK):
+            low_s[h % 2, r : r + CHUNK, :] = (
+                wts_ref[h, r : r + CHUNK, :].astype(F32) * gscore_s[h % 2, r : r + CHUNK, :]
+            ).astype(BF)
+        g_q = jnp.dot(low_s[h % 2], kcat_ref[h], preferred_element_type=F32) * scale
+        g_word.append(g_q[:, :hd])
+        g_ent.append(g_q[:, hd:])
+        g_k = lax.dot_general(
+            qcat_ref[h], low_s[h % 2], (((0,), (0,)), ((), ())), preferred_element_type=F32
+        )
+        g_v = lax.dot_general(
+            g_low, wts_ref[h], (((0,), (0,)), ((), ())), preferred_element_type=F32
+        )
+
+        @pl.when(step == 0)
+        def _(h=h, g_k=g_k, g_v=g_v):
+            gk_s[h] = g_k
+            gv_s[h] = g_v
+
+        @pl.when(step > 0)
+        def _(h=h, g_k=g_k, g_v=g_v):
+            gk_s[h] += g_k
+            gv_s[h] += g_v
+
+    g_word = jnp.concatenate(g_word, axis=1)
+    g_ent = jnp.concatenate(g_ent, axis=1)
+    gq_ref[0] = jnp.where(is_ent, 0.0, g_word).astype(BF)
+    gq_ref[1] = jnp.where(is_ent, 0.0, g_ent).astype(BF)
+    gq_ref[2] = jnp.where(is_ent, g_word, 0.0).astype(BF)
+    gq_ref[3] = jnp.where(is_ent, g_ent, 0.0).astype(BF)
+
+    @pl.when(step == pl.num_programs(0) - 1)
+    def _():
+        def close(piece, carry):
+            at = pl.ds(pl.multiple_of(piece * block, block), block)
+            pick = ent_ref[at, :1] > 0
+            g_keys, g_vals = [], []
+            for h in range(heads):
+                both = gk_s[h, :, at].T
+                g_keys.append(jnp.where(pick, both[:, hd:], both[:, :hd]))
+                g_vals.append(gv_s[h, :, at].T)
+            gkv_ref[0, at, :] = jnp.concatenate(g_keys, axis=1).astype(BF)
+            gkv_ref[1, at, :] = jnp.concatenate(g_vals, axis=1).astype(BF)
+            return carry
+
+        lax.fori_loop(0, full // block, close, 0)
+
+
+def row_backward(first_head, heads, grads, gmine, gother, keep, send, inv, wts, qcat, kcat, vaug, ent, hd):
+    half, all_cols = keep.shape
+    full = 2 * half
+    block = min(256, half)
+    first = half // block
+    cols = heads * hd
+    g, c = first_head // heads, first_head * hd // cols
+    by_rows = pl.BlockSpec((block, LANES), lambda i: (i, 0))
+    by_head = lambda width: pl.BlockSpec((heads, block, width), lambda i: (g, i, 0))
+    of_head = lambda width: pl.BlockSpec((heads, full, width), lambda i: (g, 0, 0))
+    low = pl.BlockSpec((block, cols), lambda i: (jnp.minimum(i, first - 1), c))
+    high = pl.BlockSpec((block, cols), lambda i: (jnp.maximum(i - first, 0), c))
+    given = [] if grads is None else list(grads)
+    return pl.pallas_call(
+        functools.partial(row_backward_kernel, heads, hd, first_head),
+        grid=(full // block,),
+        in_specs=[
+            low, high, low, high,
+            by_rows,
+            by_head(full),
+            by_head(2 * hd),
+            of_head(2 * hd),
+            of_head(LANES),
+            pl.BlockSpec((full, LANES), lambda i: (0, 0)),
+            by_rows,
+        ]
+        + [pl.BlockSpec(memory_space=pl.ANY)] * len(given),
+        out_specs=[
+            pl.BlockSpec((4, block, cols), lambda i: (0, i, c)),
+            pl.BlockSpec((2, full, cols), lambda i: (0, 0, c)),
+        ],
+        out_shape=[
+            jax.ShapeDtypeStruct((4, full, all_cols), BF),
+            jax.ShapeDtypeStruct((2, full, all_cols), BF),
+        ],
+        scratch_shapes=[
+            pltpu.VMEM((2, block, full), F32),
+            pltpu.VMEM((2, block, full), BF),
+            pltpu.VMEM((heads, 2 * hd, full), F32),
+            pltpu.VMEM((heads, hd, full), F32),
+        ],
+        input_output_aliases={11 + i: i for i in range(len(given))},
+        compiler_params=pltpu.CompilerParams(vmem_limit_bytes=60 << 20),
+        cost_estimate=pl.CostEstimate(
+            flops=16 * heads * full * full * LANES,
+            bytes_accessed=2 * heads * full * full + 20 * full * cols,
+            transcendentals=0,
+        ),
+        name="row_backward",
+    )(gmine, gother, keep, send, inv, wts, qcat, kcat, vaug, ent, ent, *given)
+
+
+def project_back_kernel(
+    at_ref, own_ref, other_ref, gq_ref, gkv_ref, w_ref, gy1_ref,
+    send1, send2, keep1, keep2, mine_ref, away_ref, sum_ref, rows_t,
+):
+    half, width = own_ref.shape
+    span = gkv_ref.shape[2]
+    outer, near = at_ref[0], at_ref[1]
+    rows_t[:, :half] = own_ref[...].T
+    rows_t[:, half:] = other_ref[...].T
+
+    def grads(b):
+        return gq_ref.at[b] if b < 4 else gkv_ref.at[b - 4]
+
+    n = width // 16
+    for which, out_ref in ((1 - outer, send1), (outer, keep1)):
+        left = rows_t[pl.ds(pl.multiple_of(which * 8 * n, 16), 8 * n), :]
+        for b in range(3):
+            piece = jnp.dot(left, grads(b)[...], preferred_element_type=F32)
+            out_ref[:, b] = piece.reshape(8, n, span).astype(BF)
+    for which, out_ref in ((1 - near, send2), (near, keep2)):
+        for o in range(2):
+            left = rows_t[pl.ds(pl.multiple_of(o * 8 * n + which * 4 * n, 16), 4 * n), :]
+            for b in range(3):
+                piece = jnp.dot(left, grads(3 + b)[...], preferred_element_type=F32)
+                out_ref[o, :, b] = piece.reshape(4, n, span).astype(BF)
+
+    def back(at):
+        total = None
+        for b in range(6):
+            part = lax.dot_general(
+                grads(b)[at, :], w_ref[:, b * span : (b + 1) * span], (((1,), (1,)), ((), ())),
+                preferred_element_type=F32,
+            )
+            total = part if total is None else total + part
+        return total
+
+    away_ref[...] = back(slice(half, 2 * half)).astype(BF)
+    mine_ref[...] = gy1_ref[...] + back(slice(0, half))
+    ones = jnp.ones((8, 2 * half), BF)
+    for b in range(6):
+        sum_ref[b : b + 1, :] = jnp.dot(ones, grads(b)[...], preferred_element_type=F32)[:1]
+    sum_ref[6:, :] = jnp.zeros((2, span), F32)
+
+
+def project_back(at, own, other, gq, gkv, w, gy1):
+    half, width = own.shape
+    span = gkv.shape[2]
+    n = width // 16
+    vmem = pl.BlockSpec(memory_space=pltpu.VMEM)
+    one, two = ((8, 3, n, span), BF), ((2, 4, 3, n, span), BF)
+    shapes = [one, two, one, two, ((half, width), F32), ((half, width), BF), ((8, span), F32)]
+    return pl.pallas_call(
+        project_back_kernel,
+        in_specs=[pl.BlockSpec(memory_space=pltpu.SMEM)] + [vmem] * 6,
+        out_specs=[vmem] * 7,
+        out_shape=[jax.ShapeDtypeStruct(s, d) for s, d in shapes],
+        scratch_shapes=[pltpu.VMEM((width, 2 * half), BF)],
+        compiler_params=pltpu.CompilerParams(vmem_limit_bytes=60 << 20),
+        cost_estimate=pl.CostEstimate(
+            flops=8 * half * width * 6 * span, bytes_accessed=20 * half * width, transcendentals=0
+        ),
+        name="project_back",
+    )(at, own, other, gq, gkv, w, gy1)
+
+
+def row_layer(
+    inputs, query_weight, kv_weight, out_weight, up_weight, down_weight,
+    query_bias, value_bias, out_bias, up_bias, down_bias,
+    norm1_gain, norm1_shift, norm2_gain, norm2_shift, types, lengths, cotangent,
+):
+    rows_here, span, width = inputs.shape
+    hd = width // HEADS
+    full = types.shape[1]
+    heads = HEADS // 2
+    cols = heads * hd
+    row_count = lax.axis_size("row")
+    core, outer, row_id = (lax.axis_index(n) for n in ("core", "outer", "row"))
+    place = [row_id // bit % 2 for bit in (1, 2, 4)]
+    near = place[0]
+    own_count = full // 2
+    both_ways = [(0, 1), (1, 0)]
+
+    def after(values, *others):
+        return lax.optimization_barrier((values, *others))[0]
+
+    def swap(values):
+        return lax.ppermute(values, "core", both_ways)
+
+    def cross(values):
+        return lax.ppermute(values, "outer", both_ways)
+
+    def pair_up(values, bit):
+        return lax.ppermute(values, "row", [(i, i ^ bit) for i in range(row_count)])
+
+    def in_order(index, mine, other, axis=0):
+        first, second = jnp.where(index == 0, mine, other), jnp.where(index == 0, other, mine)
+        return jnp.stack([first, second], axis=axis)
+
+    def take(values, index, axis=0):
+        return lax.dynamic_index_in_dim(values, index, axis, keepdims=False)
+
+    def halves_of_rows(values):
+        pieces = values.reshape(rows_here, 2, span // 2, width)
+        other = swap(take(pieces, 1 - core, 1))
+        return in_order(core, take(pieces, core, 1), other).reshape(row_count, span // 2, width)
+
+    def over_rows(values):
+        return lax.all_to_all(values, "row", 0, 0, tiled=True)
+
+    def rows_whole(back):
+        back = back.reshape(2, rows_here, span // 2, width)
+        other = swap(take(back, 1 - core))
+        both = in_order(core, take(back, core), other)
+        return both.transpose(1, 0, 2, 3).reshape(rows_here, span, width)
+
+    shard = query_weight.shape[0]
+    wide = down_weight.shape[0]
+
+    def near_half(values):
+        return take(values.reshape(2, values.shape[0] // 2, values.shape[1]), near)
+
+    f_own, f_core = 2 * outer + core, 2 * outer + 1 - core
+    f_cross, f_both = 2 * (1 - outer) + core, 2 * (1 - outer) + 1 - core
+
+    q_got = cross(near_half(query_weight))
+    to_rows = halves_of_rows(inputs)
+    own_rows = over_rows(to_rows).reshape(own_count, width)
+    types, lengths, query_bias, cotangent, query_own, kv_own = lax.optimization_barrier(
+        (types, lengths, query_bias, cotangent, query_weight, kv_weight, to_rows)
+    )[:6]
+    q_core, kv_core = swap(query_own), swap(kv_own)
+    kv_got = cross(after(kv_weight, q_got))
+    cot_halves = halves_of_rows(cotangent)
+    q_passed = pair_up(q_got, 1)
+    q_got2, q_passed2, kv_got2 = swap(q_got), swap(q_passed), swap(kv_got)
+    other_rows = swap(own_rows)
+    query_pieces = [query_weight, q_core, q_got, q_passed, q_got2, q_passed2]
+    kv_pieces = [kv_weight, kv_core, kv_got, kv_got2]
+    part = shard // 2
+    query_at = [
+        f_own * shard, f_core * shard,
+        f_cross * shard + near * part, f_cross * shard + (1 - near) * part,
+        f_both * shard + near * part, f_both * shard + (1 - near) * part,
+    ]
+    kv_at = [f_own * shard, f_core * shard, f_cross * shard, f_both * shard]
+    at_qkv = jnp.stack([core, *query_at, *kv_at]).astype(jnp.int32)
+
+    tags = jnp.concatenate([types, lengths], axis=1)
+    tags = take(in_order(core, tags, swap(tags)).reshape(row_count, -1), row_id)
+    types_row, lengths_row = tags[:full], tags[full:]
+
+    def by_member(values):
+        two = values.reshape(row_count, 2, span // 2).transpose(1, 0, 2)
+        return jnp.concatenate([take(two, core), take(two, 1 - core)], axis=0).reshape(full)
+
+    entity = by_member(types_row) > 0
+    positions = by_member(lax.iota(jnp.int32, full))
+    docs = lengths_row.shape[0]
+    ends = [jnp.sum(lengths_row[: d + 1]) for d in range(docs)]
+    seg = sum((positions >= end).astype(jnp.int32) for end in ends)
+    lanes = lax.broadcasted_iota(jnp.int32, (full, LANES), 1)
+    same = lanes == seg[:, None]
+    qseg = jnp.where(same, 1.0, 0.0).astype(BF)
+    kseg = jnp.where(same | (lanes >= docs), 0.0, BLOCKED).astype(BF)
+    ent = jnp.broadcast_to(jnp.where(entity, 1.0, 0.0).astype(BF)[:, None], (full, LANES))
+
+    vectors = (
+        query_bias, value_bias, out_bias, up_bias, down_bias,
+        norm1_gain, norm1_shift, norm2_gain, norm2_shift,
+    )
+    packed = jnp.concatenate([v.reshape(-1, shard) for v in vectors], axis=0)
+    packed = in_order(outer, packed, cross(packed))
+    packed = in_order(core, packed, swap(packed)).transpose(1, 0, 2, 3).reshape(4, -1, shard)
+
+    def joined(first, count):
+        return packed[:, first : first + count].reshape(-1, width).astype(F32)
+
+    b_query, b_value = joined(0, 4), joined(4, 1)
+    vec = jnp.concatenate(
+        [joined(6, 4), joined(5, 1), joined(10, 1), joined(11, 1), joined(12, 1), joined(13, 1), joined(14, 1)]
+    )
+    b_six = jnp.concatenate([b_query, jnp.zeros((1, width), F32), b_value]).reshape(6, 2, cols)
+    b_sel = take(b_six, core, 1).reshape(1, 6 * cols)
+
+    qcat, kcat, vaug, w_sel = row_project(
+        at_qkv, own_rows, other_rows, b_sel, ent, query_pieces, kv_pieces, heads, hd
+    )
+
+    low_rows = down_weight[: wide // 2]
+    u_got = cross(after(near_half(up_weight), kv_got))
+    d_got = cross(after(near_half(low_rows), kv_got))
+    late_out, late_up, late_down = lax.optimization_barrier((out_weight, up_weight, down_weight, kv_got))[:3]
+    o_core, u_core, d_core = swap(late_out), swap(late_up), swap(late_down)
+    u_mid, d_mid, m_out, m_down = lax.optimization_barrier((u_got, d_got, out_weight, down_weight, kcat))[:4]
+    u_passed, d_passed = pair_up(u_mid, 1), pair_up(d_mid, 1)
+    o_got, t_got = cross(m_out), cross(m_down[wide // 2 :])
+    u_got2, d_got2 = swap(u_mid), swap(d_mid)
+    keep, send, wts, inv = row_attend(qcat, kcat, vaug, qseg, kseg, heads, hd)
+    theirs = swap(send)
+    u_passed2, d_passed2, o_got2, t_got2 = (
+        swap(v) for v in lax.optimization_barrier((u_passed, d_passed, o_got, t_got, keep))[:4]
+    )
+    out_pieces = [out_weight, o_core, o_got, o_got2]
+    out_at = [f * shard for f in (f_own, f_core, f_cross, f_both)]
+    up_pieces = [up_weight, u_core, u_got, u_passed, u_got2, u_passed2]
+    down_pieces = [down_weight, d_core, d_got, d_passed, t_got, d_got2, d_passed2, t_got2]
+    quarter = wide // 4
+    down_at = [
+        f_own * wide, f_core * wide,
+        f_cross * wide + near * quarter, f_cross * wide + (1 - near) * quarter, f_cross * wide + 2 * quarter,
+        f_both * wide + near * quarter, f_both * wide + (1 - near) * quarter, f_both * wide + 2 * quarter,
+    ]
+    at_rest = jnp.stack([core, *out_at, *query_at, *down_at]).astype(jnp.int32)
+
+    cot = over_rows(after(cot_halves, own_rows)).reshape(own_count, width)
+    (
+        result, gy1, gmine, gtheirs, act, hlow, gffn, gup, gattn, small
+    ) = token_block(at_rest, own_rows, keep, theirs, cot, vec, out_pieces, up_pieces, down_pieces)
+    gother = swap(gtheirs)
+    at_core = core.astype(jnp.int32).reshape(1)
+    up_send, rest_send, up_keep, rest_keep = weight_grads(
+        at_core, keep, theirs, hlow, act, gffn, gup, gattn
+    )
+    output_rows = over_rows(after(result, gother).reshape(row_count, span // 2, width))
+
+    def add(a, b):
+        return (a.astype(F32) + b.astype(F32)).astype(BF)
+
+    index_of = {"outer": outer, "y": place[0], "z": place[1], "far": place[2]}
+
+    def send_over(values, name):
+        return cross(values) if name == "outer" else pair_up(values, {"y": 1, "z": 2, "far": 4}[name])
+
+    bits = (2, 2, 2)
+    state, token = {}, [gother]
+
+    def begin(name, mine, other, left):
+        state[name] = (mine, other, left, None)
+
+    def reduce(name, axis):
+        mine, other, left, _ = state[name]
+        mine, other = lax.optimization_barrier((mine, other, token[0]))[:2]
+        at = left.index(axis)
+        away, mine = (
+            add(take(mine, i, at), take(other, i, at)) for i in (1 - index_of[axis], index_of[axis])
+        )
+        token[0] = away
+        state[name] = (mine, send_over(away, axis), [a for a in left if a != axis], None)
+
+    def gather(name, axis):
+        total = settle(name)
+        token[0] = total
+        have = state[name][3] or []
+        state[name] = (total, send_over(total, axis), None, [*have, axis])
+
+    def settle(name):
+        mine, other, left, have = state[name]
+        mine, other = lax.optimization_barrier((mine, other, token[0]))[:2]
+        if left is not None:
+            assert not left
+            return add(mine, other)
+        now = [a for a in ("y", "z", "far") if a in have]
+        return in_order(index_of[have[-1]], mine, other, axis=now.index(have[-1]))
+
+    every = ["outer", "y", "z", "far"]
+
+    def pieces_of(values, *lead):
+        return values.reshape(*lead, *values.shape[-2:])
+
+    begin("up", pieces_of(up_keep, 2, *bits), pieces_of(swap(up_send), 2, *bits), every)
+    begin("rest", pieces_of(rest_keep, 2, *bits), pieces_of(swap(rest_send), 2, *bits), every)
+    gq, gkv = row_backward(
+        4, 2, None, gmine, gother, keep, send, inv, wts, qcat, kcat, vaug, ent, hd
+    )
+    token[0] = gkv
+    reduce("up", "outer")
+    reduce("rest", "y")
+    gq, gkv, _ = lax.optimization_barrier((gq, gkv, token[0]))
+    gq, gkv = row_backward(
+        0, 4, (gq, gkv), gmine, gother, keep, send, inv, wts, qcat, kcat, vaug, ent, hd
+    )
+    token[0] = gkv
+    reduce("up", "y")
+    output = rows_whole(after(output_rows, gkv))
+    gq, gkv, _ = lax.optimization_barrier((gq, gkv, token[0]))
+    at_back = jnp.stack([outer, near]).astype(jnp.int32)
+    send1, send2, keep1, keep2, in_mine, in_away, six_sum = project_back(
+        at_back, own_rows, other_rows, gq, gkv, w_sel, gy1
+    )
+    n = width // 16
+    begin("one", keep1.reshape(*bits, 3 * n, cols), cross(send1).reshape(*bits, 3 * n, cols), every[1:])
+    begin(
+        "two",
+        keep2.reshape(2, *bits[1:], 3 * n, cols),
+        pair_up(send2, 1).reshape(2, *bits[1:], 3 * n, cols),
+        ["outer", "z", "far"],
+    )
+    grad_in = (in_mine + swap(in_away).astype(F32)).astype(BF)
+    token[0] = grad_in
+    input_rows = over_rows(grad_in.reshape(row_count, span // 2, width))
+    reduce("up", "z")
+    reduce("rest", "outer")
+
+    spot = lax.broadcasted_iota(jnp.int32, (1, 2, 1), 1) == core
+    wide_sum = jnp.where(spot, six_sum[:6].reshape(6, 1, cols), 0.0).reshape(6, width)
+    each = jnp.concatenate([small[4:10], wide_sum[5:]], axis=0).reshape(7, 4, shard).transpose(1, 0, 2)
+    small = jnp.concatenate(
+        [small[:4].reshape(4, 4, shard), wide_sum[:4].reshape(4, 4, shard), each, jnp.zeros_like(each[:, :1])], axis=1
+    )
+    small = jnp.broadcast_to(small[None], (row_count, 4, 16, shard)).reshape(-1, 16, shard)
+    small = lax.all_to_all(
+        after(small, token[0]), ("row", "group", "outer", "core"), 0, 0, tiled=True
+    )
+
+    reduce("one", "y")
+    reduce("two", "outer")
+    reduce("up", "far")
+    reduce("one", "z")
+    reduce("two", "z")
+    reduce("rest", "z")
+    small = jnp.sum(after(small, token[0]), axis=0)
+    gather("up", "far")
+    reduce("one", "far")
+    reduce("two", "far")
+    input_grad = rows_whole(after(input_rows, token[0]))
+    gather("up", "z")
+    gather("one", "far")
+    gather("two", "far")
+    reduce("rest", "far")
+    gather("up", "y")
+    gather("one", "z")
+    gather("two", "z")
+    gather("rest", "far")
+    gather("one", "y")
+    gather("rest", "z")
+    gather("two", "y")
+    up_total = settle("up")
+    gather("rest", "y")
+    first_total, second_total, rest_total = settle("one"), settle("two"), settle("rest")
+
+    def both_cores(total):
+        parts = total.reshape(2, 4, 3, -1, cols)
+        halves = in_order(core, take(parts, core), swap(take(parts, 1 - core)))
+        return halves.transpose(1, 3, 2, 0, 4).reshape(shard, 3 * width).astype(F32)
+
+    one, two = both_cores(first_total), both_cores(second_total)
+    g_query = jnp.concatenate([one, two[:, :width]], axis=1)
+    g_kv = two[:, width:]
+    g_up = up_total.reshape(8, shard, -1).transpose(1, 0, 2).reshape(shard, -1).astype(F32)
+    rest_total = rest_total.reshape(4, 2, -1, cols)
+    n = wide // 4
+    g_down = rest_total[:, :, :n].transpose(0, 2, 1, 3).reshape(wide, width).astype(F32)
+    g_out = rest_total[:, :, n:].transpose(0, 2, 1, 3).reshape(shard, width).astype(F32)
+
+    return (
+        output, input_grad, g_query, g_kv, g_out, g_up, g_down,
+        small[4:8].reshape(-1), small[14], small[8], small[:4].reshape(-1), *(small[i] for i in range(9, 14)),
+    )
+
+
 def solution(mesh):
     def step(*args):
         ctx, fsdp = mesh.shape["ctx"], mesh.shape["fsdp"]
@@ -492,7 +1370,9 @@
         mat, vec = P(("outer", "core"), None), P(("outer", "core"))
         in_specs = (tokens, *[mat] * 5, *[vec] * 9, mat, mat, tokens)
         out_specs = (tokens, tokens, *[mat] * 5, *[vec] * 9)
-        body = functools.partial(layer, None, per_row)
+        quarter = args[0].shape[2] // 4
+        fits = per_row == 1 and fsdp == 4 and row_count == 8 and args[0].shape[2] % (2 * LANES) == 0 and quarter % 32 == 0
+        body = row_layer if fits else functools.partial(layer, None, per_row)
         return jax.shard_map(
             body, mesh=fine, in_specs=in_specs, out_specs=out_specs, check_vma=False
         )(*args)

time: 688 us -> 420 us (0.61)
  waiting for transfers between devices: 252 us -> 110 us
  local copies, waits for them, and re-layouts: 115 us -> 36.6 us
  blocking collectives: 67.4 us -> 0 us
  matrix products: 64.4 us -> 0 us
  Pallas kernels: 69.8 us -> 129 us
  starting transfers between devices: 30.8 us -> 88.7 us
  other arithmetic: 67.7 us -> 47.5 us
  between operations: 16.2 us -> 2.32 us
    psum x1 -> x0, waiting for transfers between devices: 96.2 us -> none  [layer(): g_sel = lax.psum(g_sel.astype(BF), 'row').reshape(2, shard, 6, cols)]
    dot_general x14 -> x0, matrix products: 64.4 us -> none  [the longest x3 23.6 us: matmul(): return jnp.dot(left_mat, right_mat, preferred_element_type=F32)]
    pallas_call x2 -> x7, Pallas kernels: 69.8 us -> 129 us  [the longest x2 37.8 us: row_backward(): pl.pallas_call(functools.partial(row_backward_kernel, heads, hd, first_he...]
    psum x1 -> x0, blocking collectives: 54.7 us -> none  [layer(): total = lax.psum(jnp.concatenate(small), ('row', 'group', 'outer', 'core'))]
    ppermute x25 -> x66, starting transfers between devices: 11.6 us -> 57 us  [the longest x27 39.6 us: pair_up(): return lax.ppermute(values, 'row', [(i, i ^ bit) for i in range(row_count)])]
    all_to_all x4 -> x5, waiting for transfers between devices: 42.7 us -> 5.47 us  [the longest x4 5.47 us: over_rows(): return lax.all_to_all(values, 'row', 0, 0, tiled=True)]
    dynamic_slice x18 -> x0, local copies, waits for them, and re-layouts: 36.2 us -> none  [the longest x6 25.6 us: take(): return lax.dynamic_index_in_dim(values, index, axis, keepdims=False)]
    unnamed x163 -> x88, local copies, waits for them, and re-layouts: 35.2 us -> 9.69 us
  transfers between devices with their start and end apart: 30 -> 71, of which waited for: 10 -> 23; matrix products, arithmetic and copies ran while one was open for 24% -> 18% of each run, Pallas kernels for 10% -> 20%
where the time goes in v2:
time: 420 us; the launch traced here: 414 us
  Pallas kernels  129 us (31%)
  waiting for transfers between devices  110 us (26%)
  starting transfers between devices  88.7 us (21%)
  other arithmetic  47.5 us (11%)
  local copies, waits for them, and re-layouts  36.6 us (9%)
    ppermute x27, waiting for transfers between devices, pair_up(): return lax.ppermute(values, 'row', [(i, i ^ bit) for i in range(row_count)])  84.2 us
    ppermute x27, starting transfers between devices, pair_up(): return lax.ppermute(values, 'row', [(i, i ^ bit) for i in range(row_count)])  39.6 us
    pallas_call x2, Pallas kernels, row_backward(): pl.pallas_call(functools.partial(row_backward_kernel, heads, hd, first_he...  37.8 us
    pallas_call x1, Pallas kernels, token_block(): pl.pallas_call(functools.partial(token_kernel, rows(out_pieces), rows(up_...  32.5 us
    all_to_all x4, starting transfers between devices, over_rows(): return lax.all_to_all(values, 'row', 0, 0, tiled=True)  26.9 us
    convert_element_type x19, other arithmetic, add(): return (a.astype(F32) + b.astype(F32)).astype(BF)  21.8 us
    pallas_call x1, Pallas kernels, row_attend(): pl.pallas_call(functools.partial(attend_kernel, heads, hd), grid=(full //...  17.4 us
    pallas_call x1, Pallas kernels, project_back(): pl.pallas_call(project_back_kernel, in_specs=[pl.BlockSpec(memory_space=p...  16.5 us
  transfers between devices with their start and end apart: 71, of which 23 were waited for; matrix products, arithmetic and copies ran while one was open for 18% of the time, Pallas kernels for 20%

profile of v2, /device:TPU:0, one launch (start us, length us, event | category | flops | bytes accessed | tf_op | source)
XLA Modules:
  0.0 414.1 jit_solution(9190670305543151937)
XLA Ops:
  2.4 1.9 dynamic-slice_bitcast_fusion.1
  4.3 2.5 collective-permute-start.6
  11.2 5.8 %all-to-all-start = ((bf16[8,64,768]{2,1,0:T(8,128)(2,1)}), bf16[8,64,768]{2,1,0:T(8,128)(2,1)S(1)}, u32[]{:S(2)}, u32[]{:S(2)}) async-start(bf16[8,64,768]{2,1,0:T(8,128)(2,1)} %bitcast.22), calls=%async_computation | async-start | bytes 1572864 | tf_op jit(solution)/shard_map/all_to_all | solution.py:1108
  19.3 1.9 collective-permute-done.2
  24.7 2.6 convert_add_fusion
  27.3 1.8 collective-permute-start.11
  32.1 5.5 %all-to-all-done = bf16[8,64,768]{2,1,0:T(8,128)(2,1)S(1)} async-done(((bf16[8,64,768]{2,1,0:T(8,128)(2,1)}), bf16[8,64,768]{2,1,0:T(8,128)(2,1)S(1)}, u32[]{:S(2)}, u32[]{:S(2)}) %all-to-all-start) | async-done | bytes 786464 | tf_op jit(solution)/shard_map/all_to_all | solution.py:1108
  38.3 4.6 %collective-permute-done.11.refs_8_ = bf16[192,1536]{1,0:T(8,128)(2,1)} collective-permute-done((bf16[192,1536]{1,0:T(8,128)(2,1)}, bf16[192,1536]{1,0:T(8,128)(2,1)}, u32[]{:S(2)}, u32[]{:S(2)}) %collective-permute-start.11) | collective-permute-done | bytes 589856 | tf_op jit(solution)/shard_map/ppermute | solution.py:1090
  42.9 2.7 collective-permute-done.7.refs_3_
  48.0 1.6 collective-permute-start.17
  51.0 11.6 %row_project.1 = (bf16[6,1024,128]{2,1,0:T(8,128)(2,1)}, bf16[6,1024,128]{2,1,0:T(8,128)(2,1)}, bf16[6,1024,128]{2,1,0:T(8,128)(2,1)}, bf16[768,2304]{1,0:T(8,128)(2,1)}) custom-call(s32[11]{0:T(128)} %stack.289.at_ref, bf16[512,768]{1,0:T(8,128)(2,1)} %bitcast.311, bf16[512,768]{1,0:T(8,128)(2,1)} %collective-permute-done.1.other_ref, f32[1,2304]{1,0:T(1,128)} %bitcast.332, ...), custom_call_target="tpu_custom_call" | custom-call | flops 3623878656 | bytes 14155776 | tf_op jit(solution)/shard_map/row_project/pallas_call | solution.py:543
  62.6 6.0 %collective-permute-done.17.refs_12_ = bf16[192,768]{1,0:T(8,128)(2,1)} collective-permute-done((bf16[192,768]{1,0:T(8,128)(2,1)}, bf16[192,768]{1,0:T(8,128)(2,1)}, u32[]{:S(2)}, u32[]{:S(2)}) %collective-permute-start.17) | collective-permute-done | bytes 294944 | tf_op jit(solution)/shard_map/ppermute | solution.py:1090
  69.1 1.6 collective-permute-start.20
  71.7 5.2 %all-to-all-start.1 = ((bf16[8,64,768]{2,1,0:T(8,128)(2,1)}), bf16[8,64,768]{2,1,0:T(8,128)(2,1)S(1)}, u32[]{:S(2)}, u32[]{:S(2)}) async-start(bf16[8,64,768]{2,1,0:T(8,128)(2,1)} %bitcast.45), calls=%async_computation.1 | async-start | bytes 1572864 | tf_op jit(solution)/shard_map/all_to_all | solution.py:1108
  77.9 1.6 collective-permute-start.21
  79.5 2.0 collective-permute-start.19
  81.5 17.4 %row_attend.1 = (bf16[512,384]{1,0:T(8,128)(2,1)}, bf16[512,384]{1,0:T(8,128)(2,1)}, bf16[6,1024,1024]{2,1,0:T(8,128)(2,1)}, f32[1024,128]{1,0:T(8,128)}) custom-call(bf16[6,1024,128]{2,1,0:T(8,128)(2,1)} %get-tuple-element.145.qcat_ref, bf16[1024,128]{1,0:T(8,128)(2,1)} %get-tuple-element.352.qseg_ref, bf16[6,1024,128]{2,1,0:T(8,128)(2,1)} %get-tuple-element.146.kcat_ref, ...), custom_call_target="tpu_custom_call" | custom-call | flops 6442450944 | bytes 15728640 | tf_op jit(solution)/shard_map/row_attend/pallas_call | solution.py:608
  106.5 32.5 %token_block.1 = (bf16[512,768]{1,0:T(8,128)(2,1)}, f32[512,768]{1,0:T(8,128)}, bf16[512,384]{1,0:T(8,128)(2,1)}, bf16[512,384]{1,0:T(8,128)(2,1)}, bf16[512,307...) custom-call(s32[19]{0:T(128)} %stack.285.at_ref, ...), custom_call_target="tpu_custom_call" | custom-call | flops 10871635968 | bytes 18874368 | tf_op jit(solution)/shard_map/token_block/pallas_call | solution.py:789
  139.0 13.1 %weight_grads.1 = (bf16[2,8,192,384]{3,2,1,0:T(8,128)(2,1)}, bf16[2,8,240,384]{3,2,1,0:T(8,128)(2,1)}, bf16[2,8,192,384]{3,2,1,0:T(8,128)(2,1)}, bf16[2,8,240,384]{3,2,1,0:T(8,128)(2,1)}) custom-call(s32[1]{0:T(128)} %bitcast.at_ref, bf16[512,384]{1,0:T(8,128)(2,1)} %get-tuple-element.148.mine_ref.keep_ref, ...), custom_call_target="tpu_custom_call" | custom-call | flops 5435817984 | bytes 18874368 | tf_op jit(solution)/shard_map/weight_grads/pallas_call | solution.py:857
  155.1 6.2 %collective-permute-done.30.gother_ref = bf16[512,384]{1,0:T(8,128)(2,1)S(1)} collective-permute-done((bf16[512,384]{1,0:T(8,128)(2,1)S(1)}, bf16[512,384]{1,0:T(8,128)(2,1)S(1)}, u32[]{:S(2)}, u32[]{:S(2)}) %collective-permute-start.30) | collective-permute-done | bytes 393248 | tf_op jit(solution)/shard_map/ppermute | solution.py:1087
  161.3 6.6 %all-to-all-start.2 = ((bf16[8,64,768]{2,1,0:T(8,128)(2,1)}), bf16[8,64,768]{2,1,0:T(8,128)(2,1)S(1)}, u32[]{:S(2)}, u32[]{:S(2)}) async-start(bf16[8,64,768]{2,1,0:T(8,128)(2,1)} %bitcast.315), calls=%async_computation.2 | async-start | bytes 1572864 | tf_op jit(solution)/shard_map/all_to_all | solution.py:1108
  168.0 13.3 %row_backward.2 = (bf16[4,1024,384]{2,1,0:T(8,128)(2,1)}, bf16[2,1024,384]{2,1,0:T(8,128)(2,1)}) custom-call(bf16[512,384]{1,0:T(8,128)(2,1)} %get-tuple-element.168.gmine_ref, bf16[512,384]{1,0:T(8,128)(2,1)} %copy-done.12, bf16[512,384]{1,0:T(8,128)(2,1)} %get-tuple-element.148.mine_ref.keep_ref, bf16[512,384]{1,0:T(8,128)(2,1)} %get-tuple-element.149.send_ref, ...), custom_call_target="tpu_custom_call" | custom-call | flops 4294967296 | bytes 6815744 | tf_op jit(solution)/shard_map/row_backward/pallas_call | solution.py:962
  182.7 4.2 %fusion.3 = (bf16[2,2,2,192,384]{4,3,2,1,0:T(8,128)(2,1)S(1)}, bf16[2,2,2,192,384]{4,3,2,1,0:T(8,128)(2,1)}) fusion(bf16[2,2,2,2,192,384]{5,4,3,2,1,0:T(8,128)(2,1)} %bitcast.306, s32[]{:T(128)S(6)} %select_n.411, bf16[2,2,2,2,192,384]{5,4,3,2,1,0:T(8,128)(2,1)} %bitcast.305, s32[]{:T(128)S(6)} %select_n.407), kind=kLoop, calls=%fused_computation.14 | loop fusion | flops 4718592 | bytes 7077896 | tf_op jit(solution)/shard_map/convert_element_type | solution.py:1227
  188.4 2.8 fusion
  191.2 2.0 collective-permute-start.38
  193.2 24.6 %row_backward.3 = (bf16[4,1024,384]{2,1,0:T(8,128)(2,1)}, bf16[2,1024,384]{2,1,0:T(8,128)(2,1)}) custom-call(bf16[512,384]{1,0:T(8,128)(2,1)} %get-tuple-element.168.gmine_ref, bf16[512,384]{1,0:T(8,128)(2,1)} %copy-done.12, bf16[512,384]{1,0:T(8,128)(2,1)} %get-tuple-element.148.mine_ref.keep_ref, ...), custom_call_target="tpu_custom_call", output_to_operand_aliasing={{0}: (11, {}), {1}: (12, {})} | custom-call | flops 8589934592 | bytes 13631488 | tf_op jit(solution)/shard_map/row_backward/pallas_call | solution.py:962
  221.2 16.5 %project_back.1 = (bf16[8,3,48,384]{3,2,1,0:T(8,128)(2,1)}, bf16[2,4,3,48,384]{4,3,2,1,0:T(8,128)(2,1)}, bf16[8,3,48,384]{3,2,1,0:T(8,128)(2,1)}, bf16[2,4,3,48,...) custom-call(s32[2]{0:T(128)} %pad_add_fusion.2.at_ref, ...), custom_call_target="tpu_custom_call" | custom-call | flops 7247757312 | bytes 7864320 | tf_op jit(solution)/shard_map/project_back/pallas_call | solution.py:1052
  238.2 2.2 fusion.1
  242.0 2.0 collective-permute-start.36
  244.4 2.6 add_convert_fusion.4
  247.0 10.7 %collective-permute-done.39 = bf16[2,2,192,384]{3,2,1,0:T(8,128)(2,1)S(1)} collective-permute-done((bf16[2,2,192,384]{3,2,1,0:T(8,128)(2,1)S(1)}, bf16[2,2,192,384]{3,2,1,0:T(8,128)(2,1)S(1)}, u32[]{:S(2)}, u32[]{:S(2)}) %collective-permute-start.39) | collective-permute-done | bytes 589856 | tf_op jit(solution)/shard_map/ppermute | solution.py:1093
  260.0 2.6 fusion.5
  264.8 2.7 collective-permute-start.41
  267.5 9.2 %collective-permute-done.36 = bf16[2,4,3,48,384]{4,3,2,1,0:T(8,128)(2,1)} collective-permute-done((bf16[2,4,3,48,384]{4,3,2,1,0:T(8,128)(2,1)}, bf16[2,4,3,48,384]{4,3,2,1,0:T(8,128)(2,1)}, u32[]{:S(2)}, u32[]{:S(2)}) %collective-permute-start.36) | collective-permute-done | bytes 884768 | tf_op jit(solution)/shard_map/ppermute | solution.py:1093
  276.7 2.1 fusion.11
  280.4 4.8 %all-to-all-start.4 = ((f32[32,16,192]{2,1,0:T(8,128)}), f32[32,16,192]{2,1,0:T(8,128)S(1)}, u32[]{:S(2)}, u32[]{:S(2)}) async-start(f32[32,16,192]{2,1,0:T(8,128)} %bitcast.146), calls=%async_computation.4 | async-start | bytes 1048576 | tf_op jit(solution)/shard_map/all_to_all | solution.py:1311
  285.3 2.9 collective-permute-start.45
  289.3 1.6 collective-permute-start.44
  292.0 1.8 collective-permute-start.43
  295.5 11.1 %collective-permute-done.45 = bf16[192,384]{1,0:T(8,128)(2,1)S(1)} collective-permute-done((bf16[192,384]{1,0:T(8,128)(2,1)S(1)}, bf16[192,384]{1,0:T(8,128)(2,1)S(1)}, u32[]{:S(2)}, u32[]{:S(2)}) %collective-permute-start.45) | collective-permute-done | bytes 147488 | tf_op jit(solution)/shard_map/ppermute | solution.py:1093
  306.7 3.0 collective-permute-start.48
  309.8 2.3 collective-permute-start.53
  312.1 9.2 %all-to-all-start.3 = ((bf16[8,64,768]{2,1,0:T(8,128)(2,1)}), bf16[8,64,768]{2,1,0:T(8,128)(2,1)S(1)}, u32[]{:S(2)}, u32[]{:S(2)}) async-start(bf16[8,64,768]{2,1,0:T(8,128)(2,1)} %bitcast.69), calls=%async_computation.3 | async-start | bytes 1572864 | tf_op jit(solution)/shard_map/all_to_all | solution.py:1108
  323.4 2.1 collective-permute-start.51
  325.5 2.4 collective-permute-start.50
  328.7 2.4 collective-permute-start.55
  331.1 15.7 %collective-permute-done.51 = bf16[2,192,384]{2,1,0:T(8,128)(2,1)S(1)} collective-permute-done((bf16[2,192,384]{2,1,0:T(8,128)(2,1)S(1)}, bf16[2,192,384]{2,1,0:T(8,128)(2,1)S(1)}, u32[]{:S(2)}, u32[]{:S(2)}) %collective-permute-start.51) | collective-permute-done | bytes 294944 | tf_op jit(solution)/shard_map/ppermute | solution.py:1093
  347.0 1.5 collective-permute-start.65
  348.5 6.1 %collective-permute-done.50 = bf16[144,384]{1,0:T(8,128)(2,1)S(1)} collective-permute-done((bf16[144,384]{1,0:T(8,128)(2,1)S(1)}, bf16[144,384]{1,0:T(8,128)(2,1)S(1)}, u32[]{:S(2)}, u32[]{:S(2)}) %collective-permute-start.50) | collective-permute-done | bytes 110624 | tf_op jit(solution)/shard_map/ppermute | solution.py:1093
  354.8 2.4 collective-permute-done.56
  357.5 2.9 collective-permute-done.55
  360.8 6.1 %collective-permute-done.54 = bf16[2,144,384]{2,1,0:T(8,128)(2,1)S(1)} collective-permute-done((bf16[2,144,384]{2,1,0:T(8,128)(2,1)S(1)}, bf16[2,144,384]{2,1,0:T(8,128)(2,1)S(1)}, u32[]{:S(2)}, u32[]{:S(2)}) %collective-permute-start.54) | collective-permute-done | bytes 221216 | tf_op jit(solution)/shard_map/ppermute | solution.py:1093
  367.0 1.6 collective-permute-start.57
  368.6 2.6 collective-permute-done.58
  374.3 6.5 %collective-permute-done.59 = bf16[2,240,384]{2,1,0:T(8,128)(2,1)S(1)} collective-permute-done((bf16[2,240,384]{2,1,0:T(8,128)(2,1)S(1)}, bf16[2,240,384]{2,1,0:T(8,128)(2,1)S(1)}, u32[]{:S(2)}, u32[]{:S(2)}) %collective-permute-start.59) | collective-permute-done | bytes 368672 | tf_op jit(solution)/shard_map/ppermute | solution.py:1093
  382.3 2.6 collective-permute-done.62
  386.3 1.7 copy.86
  392.7 1.8 select_bitcast_fusion.5
  394.6 2.6 copy.75
  397.2 3.0 reshape.576
  401.4 1.7 pad_maximum_fusion
  403.1 4.2 %collective-permute-done.64 = bf16[2,2,240,384]{3,2,1,0:T(8,128)(2,1)} collective-permute-done((bf16[2,2,240,384]{3,2,1,0:T(8,128)(2,1)}, bf16[2,2,240,384]{3,2,1,0:T(8,128)(2,1)}, u32[]{:S(2)}, u32[]{:S(2)}) %collective-permute-start.64) | collective-permute-done | bytes 737312 | tf_op jit(solution)/shard_map/ppermute | solution.py:1093
  409.1 1.8 copy.89
  410.9 1.6 copy.87
  (326 shorter events, 69.8 us)
Async XLA Ops:
  1.9 8.3 %collective-permute-start = (bf16[4,64,768]{2,1,0:T(8,128)(2,1)S(1)}, bf16[4,64,768]{2,1,0:T(8,128)(2,1)S(1)}, u32[]{:S(2)}, u32[]{:S(2)}) collective-permute-start(bf16[4,64,768]{2,1,0:T(8,128)(2,1)S(1)} %dynamic-slice_bitcast_fusion.5), channel_id=1, source_target_pairs={{0,1},{1,0},{2,3},{3,2},{4,5},{5,4},{6,7},{7,6},{8,9},{9,8},{10,11... | collective-permute-start | bytes 1179656 | tf_op jit(solution)/shard_map/ppermute | solution.py:1087
  4.3 23.0 %collective-permute-start.6 = (bf16[96,3072]{1,0:T(8,128)(2,1)}, bf16[96,3072]{1,0:T(8,128)(2,1)}, u32[]{:S(2)}, u32[]{:S(2)}) collective-permute-start(bf16[96,3072]{1,0:T(8,128)(2,1)} %dynamic-slice_bitcast_fusion.1), channel_id=1, source_target_pairs={{0,2},{2,0},{1,3},{3,1},{4,6},{6,4},{5,7},{7,5},{8,10},{10,8},{9,1... | collective-permute-start | bytes 1769480 | tf_op jit(solution)/shard_map/ppermute | solution.py:1090
  11.2 26.3 %all-to-all-start = ((bf16[8,64,768]{2,1,0:T(8,128)(2,1)}), bf16[8,64,768]{2,1,0:T(8,128)(2,1)S(1)}, u32[]{:S(2)}, u32[]{:S(2)}) async-start(bf16[8,64,768]{2,1,0:T(8,128)(2,1)} %bitcast.22), calls=%async_computation | async-start | bytes 1572864 | tf_op jit(solution)/shard_map/all_to_all | solution.py:1108
  18.0 30.0 %collective-permute-start.5 = (bf16[192,3072]{1,0:T(8,128)(2,1)}, bf16[192,3072]{1,0:T(8,128)(2,1)}, u32[]{:S(2)}, u32[]{:S(2)}) collective-permute-start(bf16[192,3072]{1,0:T(8,128)(2,1)} %refs_0_.2), channel_id=1, source_target_pairs={{0,1},{1,0},{2,3},{3,2},{4,5},{5,4},{6,7},{7,6},{8,9},{9,8},{10,11... | collective-permute-start | bytes 3538952 | tf_op jit(solution)/shard_map/ppermute | solution.py:1087
  18.2 13.9 %collective-permute-start.10 = (bf16[192,1536]{1,0:T(8,128)(2,1)}, bf16[192,1536]{1,0:T(8,128)(2,1)}, u32[]{:S(2)}, u32[]{:S(2)}) collective-permute-start(bf16[192,1536]{1,0:T(8,128)(2,1)} %refs_6_.1), channel_id=1, source_target_pairs={{0,1},{1,0},{2,3},{3,2},{4,5},{5,4},{6,7},{7,6},{8,9},{9,8},{10,11... | collective-permute-start | bytes 1769480 | tf_op jit(solution)/shard_map/ppermute | solution.py:1087
  21.2 10.8 %collective-permute-start.14 = (bf16[4,64,768]{2,1,0:T(8,128)(2,1)}, bf16[4,64,768]{2,1,0:T(8,128)(2,1)}, u32[]{:S(2)}, u32[]{:S(2)}) collective-permute-start(bf16[4,64,768]{2,1,0:T(8,128)(2,1)} %dynamic-slice_bitcast_fusion.4), channel_id=1, source_target_pairs={{0,1},{1,0},{2,3},{3,2},{4,5},{5,4},{6,7},{7,6},{8,9},{9,8},{10,11... | collective-permute-start | bytes 1179656 | tf_op jit(solution)/shard_map/ppermute | solution.py:1087
  21.2 7.9 %collective-permute-start.3 = (bf16[2,15,192]{2,1,0:T(8,128)(2,1)S(1)}, bf16[2,15,192]{2,1,0:T(8,128)(2,1)S(1)}, u32[]{:S(2)}, u32[]{:S(2)}) collective-permute-start(bf16[2,15,192]{2,1,0:T(8,128)(2,1)S(1)} %pad_maximum_fusion.14), channel_id=1, source_target_pairs={{0,1},{1,0},{2,3},{3,2},{4,5},{5,4},{6,7},{7,6},{8,9},{9,8},{10,11... | collective-permute-start | bytes 34568 | tf_op jit(solution)/shard_map/ppermute | solution.py:1087
  27.3 15.6 %collective-permute-start.11 = (bf16[192,1536]{1,0:T(8,128)(2,1)}, bf16[192,1536]{1,0:T(8,128)(2,1)}, u32[]{:S(2)}, u32[]{:S(2)}) collective-permute-start(bf16[192,1536]{1,0:T(8,128)(2,1)} %refs_6_.1), channel_id=1, source_target_pairs={{0,2},{2,0},{1,3},{3,1},{4,6},{6,4},{5,7},{7,5},{8,10},{10,8},{9,1... | collective-permute-start | bytes 1769480 | tf_op jit(solution)/shard_map/ppermute | solution.py:1090
  29.1 16.5 %collective-permute-start.7 = (bf16[96,3072]{1,0:T(8,128)(2,1)}, bf16[96,3072]{1,0:T(8,128)(2,1)}, u32[]{:S(2)}, u32[]{:S(2)}) collective-permute-start(bf16[96,3072]{1,0:T(8,128)(2,1)} %collective-permute-done.6.refs_2_), channel_id=1, source_target_pairs={{0,4},{4,0},{8,12},{12,8},{16,20},{20,16},{24,28},{28,24},{1,5},{5... | collective-permute-start | bytes 1769480 | tf_op jit(solution)/shard_map/ppermute | solution.py:1093
  32.0 14.5 %collective-permute-start.8 = (bf16[96,3072]{1,0:T(8,128)(2,1)}, bf16[96,3072]{1,0:T(8,128)(2,1)}, u32[]{:S(2)}, u32[]{:S(2)}) collective-permute-start(bf16[96,3072]{1,0:T(8,128)(2,1)} %collective-permute-done.6.refs_2_), channel_id=1, source_target_pairs={{0,1},{1,0},{2,3},{3,2},{4,5},{5,4},{6,7},{7,6},{8,9},{9,8},{10,11... | collective-permute-start | bytes 1769480 | tf_op jit(solution)/shard_map/ppermute | solution.py:1087
  37.6 12.5 %collective-permute-start.1 = (bf16[512,768]{1,0:T(8,128)(2,1)S(1)}, bf16[512,768]{1,0:T(8,128)(2,1)}, u32[]{:S(2)}, u32[]{:S(2)}) collective-permute-start(bf16[512,768]{1,0:T(8,128)(2,1)S(1)} %bitcast.310), channel_id=1, source_target_pairs={{0,1},{1,0},{2,3},{3,2},{4,5},{5,4},{6,7},{7,6},{8,9},{9,8},{10,11... | collective-permute-start | bytes 2359304 | tf_op jit(solution)/shard_map/ppermute | solution.py:1087
  42.9 6.7 %collective-permute-start.12 = (bf16[192,1536]{1,0:T(8,128)(2,1)}, bf16[192,1536]{1,0:T(8,128)(2,1)}, u32[]{:S(2)}, u32[]{:S(2)}) collective-permute-start(bf16[192,1536]{1,0:T(8,128)(2,1)} %collective-permute-done.11.refs_8_), channel_id=1, source_target_pairs={{0,1},{1,0},{2,3},{3,2},{4,5},{5,4},{6,7},{7,6},{8,9},{9,8},{10,11... | collective-permute-start | bytes 1769480 | tf_op jit(solution)/shard_map/ppermute | solution.py:1087
  46.4 22.2 %collective-permute-start.16 = (bf16[96,3072]{1,0:T(8,128)(2,1)S(1)}, bf16[96,3072]{1,0:T(8,128)(2,1)}, u32[]{:S(2)}, u32[]{:S(2)}) collective-permute-start(bf16[96,3072]{1,0:T(8,128)(2,1)S(1)} %dynamic-slice_bitcast_fusion), channel_id=1, source_target_pairs={{0,2},{2,0},{1,3},{3,1},{4,6},{6,4},{5,7},{7,5},{8,10},{10,8},{9,1... | collective-permute-start | bytes 1769480 | tf_op jit(solution)/shard_map/ppermute | solution.py:1090
  48.0 20.6 %collective-permute-start.17 = (bf16[192,768]{1,0:T(8,128)(2,1)}, bf16[192,768]{1,0:T(8,128)(2,1)}, u32[]{:S(2)}, u32[]{:S(2)}) collective-permute-start(bf16[192,768]{1,0:T(8,128)(2,1)} %dynamic-slice_bitcast_fusion.6), channel_id=1, source_target_pairs={{0,2},{2,0},{1,3},{3,1},{4,6},{6,4},{5,7},{7,5},{8,10},{10,8},{9,1... | collective-permute-start | bytes 884744 | tf_op jit(solution)/shard_map/ppermute | solution.py:1090
  49.6 51.3 %collective-permute-start.23 = (bf16[192,3072]{1,0:T(8,128)(2,1)}, bf16[192,3072]{1,0:T(8,128)(2,1)}, u32[]{:S(2)}, u32[]{:S(2)}) collective-permute-start(bf16[192,3072]{1,0:T(8,128)(2,1)} %refs_4_.1), channel_id=1, source_target_pairs={{0,1},{1,0},{2,3},{3,2},{4,5},{5,4},{6,7},{7,6},{8,9},{9,8},{10,11... | collective-permute-start | bytes 3538952 | tf_op jit(solution)/shard_map/ppermute | solution.py:1087
  49.6 51.4 %collective-permute-start.26 = (bf16[768,768]{1,0:T(8,128)(2,1)S(1)}, bf16[768,768]{1,0:T(8,128)(2,1)}, u32[]{:S(2)}, u32[]{:S(2)}) collective-permute-start(bf16[768,768]{1,0:T(8,128)(2,1)S(1)} %copy-done.4), channel_id=1, source_target_pairs={{0,1},{1,0},{2,3},{3,2},{4,5},{5,4},{6,7},{7,6},{8,9},{9,8},{10,11... | collective-permute-start | bytes 3538952 | tf_op jit(solution)/shard_map/ppermute | solution.py:1087
  68.6 9.3 %collective-permute-start.18 = (bf16[192,768]{1,0:T(8,128)(2,1)}, bf16[192,768]{1,0:T(8,128)(2,1)}, u32[]{:S(2)}, u32[]{:S(2)}) collective-permute-start(bf16[192,768]{1,0:T(8,128)(2,1)} %refs_0_.3), channel_id=1, source_target_pairs={{0,2},{2,0},{1,3},{3,1},{4,6},{6,4},{5,7},{7,5},{8,10},{10,8},{9,1... | collective-permute-start | bytes 884744 | tf_op jit(solution)/shard_map/ppermute | solution.py:1090
  69.1 10.4 %collective-permute-start.20 = (bf16[192,768]{1,0:T(8,128)(2,1)}, bf16[192,768]{1,0:T(8,128)(2,1)}, u32[]{:S(2)}, u32[]{:S(2)}) collective-permute-start(bf16[192,768]{1,0:T(8,128)(2,1)} %collective-permute-done.17.refs_12_), channel_id=1, source_target_pairs={{0,4},{4,0},{8,12},{12,8},{16,20},{20,16},{24,28},{28,24},{1,5},{5... | collective-permute-start | bytes 884744 | tf_op jit(solution)/shard_map/ppermute | solution.py:1093
  71.7 33.2 %all-to-all-start.1 = ((bf16[8,64,768]{2,1,0:T(8,128)(2,1)}), bf16[8,64,768]{2,1,0:T(8,128)(2,1)S(1)}, u32[]{:S(2)}, u32[]{:S(2)}) async-start(bf16[8,64,768]{2,1,0:T(8,128)(2,1)} %bitcast.45), calls=%async_computation.1 | async-start | bytes 1572864 | tf_op jit(solution)/shard_map/all_to_all | solution.py:1108
  77.9 22.5 %collective-permute-start.15 = (bf16[192,768]{1,0:T(8,128)(2,1)}, bf16[192,768]{1,0:T(8,128)(2,1)}, u32[]{:S(2)}, u32[]{:S(2)}) collective-permute-start(bf16[192,768]{1,0:T(8,128)(2,1)} %refs_0_.3), channel_id=1, source_target_pairs={{0,1},{1,0},{2,3},{3,2},{4,5},{5,4},{6,7},{7,6},{8,9},{9,8},{10,11... | collective-permute-start | bytes 884744 | tf_op jit(solution)/shard_map/ppermute | solution.py:1087
  77.9 21.0 %collective-permute-start.21 = (bf16[384,768]{1,0:T(8,128)(2,1)S(1)}, bf16[384,768]{1,0:T(8,128)(2,1)S(1)}, u32[]{:S(2)}, u32[]{:S(2)}) collective-permute-start(bf16[384,768]{1,0:T(8,128)(2,1)S(1)} %slice.127), channel_id=1, source_target_pairs={{0,2},{2,0},{1,3},{3,1},{4,6},{6,4},{5,7},{7,5},{8,10},{10,8},{9,1... | collective-permute-start | bytes 1769480 | tf_op jit(solution)/shard_map/ppermute | solution.py:1090
  79.5 20.9 %collective-permute-start.19 = (bf16[96,3072]{1,0:T(8,128)(2,1)}, bf16[96,3072]{1,0:T(8,128)(2,1)S(1)}, u32[]{:S(2)}, u32[]{:S(2)}) collective-permute-start(bf16[96,3072]{1,0:T(8,128)(2,1)} %collective-permute-done.16.refs_6_), channel_id=1, source_target_pairs={{0,4},{4,0},{8,12},{12,8},{16,20},{20,16},{24,28},{28,24},{1,5},{5... | collective-permute-start | bytes 1769480 | tf_op jit(solution)/shard_map/ppermute | solution.py:1093
  100.4 4.5 %collective-permute-start.24 = (bf16[96,3072]{1,0:T(8,128)(2,1)}, bf16[96,3072]{1,0:T(8,128)(2,1)}, u32[]{:S(2)}, u32[]{:S(2)}) collective-permute-start(bf16[96,3072]{1,0:T(8,128)(2,1)} %collective-permute-done.16.refs_6_), channel_id=1, source_target_pairs={{0,1},{1,0},{2,3},{3,2},{4,5},{5,4},{6,7},{7,6},{8,9},{9,8},{10,11... | collective-permute-start | bytes 1769480 | tf_op jit(solution)/shard_map/ppermute | solution.py:1087
  100.9 4.7 %collective-permute-start.25 = (bf16[96,3072]{1,0:T(8,128)(2,1)S(1)}, bf16[96,3072]{1,0:T(8,128)(2,1)}, u32[]{:S(2)}, u32[]{:S(2)}) collective-permute-start(bf16[96,3072]{1,0:T(8,128)(2,1)S(1)} %collective-permute-done.19.refs_7_), channel_id=1, source_target_pairs={{0,1},{1,0},{2,3},{3,2},{4,5},{5,4},{6,7},{7,6},{8,9},{9,8},{10,11... | collective-permute-start | bytes 1769480 | tf_op jit(solution)/shard_map/ppermute | solution.py:1087
  101.0 4.6 %collective-permute-start.29 = (bf16[384,768]{1,0:T(8,128)(2,1)S(1)}, bf16[384,768]{1,0:T(8,128)(2,1)S(1)}, u32[]{:S(2)}, u32[]{:S(2)}) collective-permute-start(bf16[384,768]{1,0:T(8,128)(2,1)S(1)} %collective-permute-done.21.refs_14_), channel_id=1, source_target_pairs={{0,1},{1,0},{2,3},{3,2},{4,5},{5,4},{6,7},{7,6},{8,9},{9,8},{10,11... | collective-permute-start | bytes 1769480 | tf_op jit(solution)/shard_map/ppermute | solution.py:1087
  152.0 36.3 %collective-permute-start.31 = (bf16[2,8,240,384]{3,2,1,0:T(8,128)(2,1)}, bf16[2,8,240,384]{3,2,1,0:T(8,128)(2,1)}, u32[]{:S(2)}, u32[]{:S(2)}) collective-permute-start(bf16[2,8,240,384]{3,2,1,0:T(8,128)(2,1)} %get-tuple-element.179), channel_id=1, source_target_pairs={{0,1},{1,0},{2,3},{3,2},{4,5},{5,4},{6,7},{7,6},{8,9},{9,8},{10,11... | collective-permute-start | bytes 8847368 | tf_op jit(solution)/shard_map/ppermute | solution.py:1087
  152.1 29.1 %collective-permute-start.32 = (bf16[2,8,192,384]{3,2,1,0:T(8,128)(2,1)}, bf16[2,8,192,384]{3,2,1,0:T(8,128)(2,1)S(1)}, u32[]{:S(2)}, u32[]{:S(2)}) collective-permute-start(bf16[2,8,192,384]{3,2,1,0:T(8,128)(2,1)} %get-tuple-element.181), channel_id=1, source_target_pairs={{0,1},{1,0},{2,3},{3,2},{4,5},{5,4},{6,7},{7,6},{8,9},{9,8},{10,11... | collective-permute-start | bytes 7077896 | tf_op jit(solution)/shard_map/ppermute | solution.py:1087
  152.5 8.8 %collective-permute-start.30 = (bf16[512,384]{1,0:T(8,128)(2,1)S(1)}, bf16[512,384]{1,0:T(8,128)(2,1)S(1)}, u32[]{:S(2)}, u32[]{:S(2)}) collective-permute-start(bf16[512,384]{1,0:T(8,128)(2,1)S(1)} %copy-done.31), channel_id=1, source_target_pairs={{0,1},{1,0},{2,3},{3,2},{4,5},{5,4},{6,7},{7,6},{8,9},{9,8},{10,11... | collective-permute-start | bytes 1179656 | tf_op jit(solution)/shard_map/ppermute | solution.py:1087
  161.3 56.5 %all-to-all-start.2 = ((bf16[8,64,768]{2,1,0:T(8,128)(2,1)}), bf16[8,64,768]{2,1,0:T(8,128)(2,1)S(1)}, u32[]{:S(2)}, u32[]{:S(2)}) async-start(bf16[8,64,768]{2,1,0:T(8,128)(2,1)} %bitcast.315), calls=%async_computation.2 | async-start | bytes 1572864 | tf_op jit(solution)/shard_map/all_to_all | solution.py:1108
  186.9 31.8 %collective-permute-start.34 = (bf16[2,2,2,192,384]{4,3,2,1,0:T(8,128)(2,1)}, bf16[2,2,2,192,384]{4,3,2,1,0:T(8,128)(2,1)S(1)}, u32[]{:S(2)}, u32[]{:S(2)}) collective-permute-start(bf16[2,2,2,192,384]{4,3,2,1,0:T(8,128)(2,1)} %get-tuple-element.269), channel_id=1, source_target_pairs={{0,2},{2,0},{1,3},{3,1},{4,6},{6,4},{5,7},{7,5},{8,10},{10,8},{9,1... | collective-permute-start | bytes 3538952 | tf_op jit(solution)/shard_map/ppermute | solution.py:1090
  191.2 68.8 %collective-permute-start.38 = (bf16[2,2,2,240,384]{4,3,2,1,0:T(8,128)(2,1)}, bf16[2,2,2,240,384]{4,3,2,1,0:T(8,128)(2,1)}, u32[]{:S(2)}, u32[]{:S(2)}) collective-permute-start(bf16[2,2,2,240,384]{4,3,2,1,0:T(8,128)(2,1)} %fusion), channel_id=1, source_target_pairs={{0,4},{4,0},{8,12},{12,8},{16,20},{20,16},{24,28},{28,24},{1,5},{5... | collective-permute-start | bytes 4423688 | tf_op jit(solution)/shard_map/ppermute | solution.py:1093
  218.6 21.7 %collective-permute-start.33 = (bf16[4,64,768]{2,1,0:T(8,128)(2,1)}, bf16[4,64,768]{2,1,0:T(8,128)(2,1)S(1)}, u32[]{:S(2)}, u32[]{:S(2)}) collective-permute-start(bf16[4,64,768]{2,1,0:T(8,128)(2,1)} %dynamic-slice_bitcast_fusion.3), channel_id=1, source_target_pairs={{0,1},{1,0},{2,3},{3,2},{4,5},{5,4},{6,7},{7,6},{8,9},{9,8},{10,11... | collective-permute-start | bytes 1179656 | tf_op jit(solution)/shard_map/ppermute | solution.py:1087
  237.7 6.7 %collective-permute-start.35 = (bf16[512,768]{1,0:T(8,128)(2,1)}, bf16[512,768]{1,0:T(8,128)(2,1)}, u32[]{:S(2)}, u32[]{:S(2)}) collective-permute-start(bf16[512,768]{1,0:T(8,128)(2,1)} %get-tuple-element.198), channel_id=1, source_target_pairs={{0,1},{1,0},{2,3},{3,2},{4,5},{5,4},{6,7},{7,6},{8,9},{9,8},{10,11... | collective-permute-start | bytes 2359304 | tf_op jit(solution)/shard_map/ppermute | solution.py:1087
  241.5 16.2 %collective-permute-start.39 = (bf16[2,2,192,384]{3,2,1,0:T(8,128)(2,1)S(1)}, bf16[2,2,192,384]{3,2,1,0:T(8,128)(2,1)S(1)}, u32[]{:S(2)}, u32[]{:S(2)}) collective-permute-start(bf16[2,2,192,384]{3,2,1,0:T(8,128)(2,1)S(1)} %get-tuple-element.273), channel_id=1, source_target_pairs={{0,4},{4,0},{8,12},{12,8},{16,20},{20,16},{24,28},{28,24},{1,5},{5... | collective-permute-start | bytes 1769480 | tf_op jit(solution)/shard_map/ppermute | solution.py:1093
  241.5 21.9 %collective-permute-start.37 = (bf16[8,3,48,384]{3,2,1,0:T(8,128)(2,1)}, bf16[8,3,48,384]{3,2,1,0:T(8,128)(2,1)}, u32[]{:S(2)}, u32[]{:S(2)}) collective-permute-start(bf16[8,3,48,384]{3,2,1,0:T(8,128)(2,1)} %get-tuple-element.202), channel_id=1, source_target_pairs={{0,2},{2,0},{1,3},{3,1},{4,6},{6,4},{5,7},{7,5},{8,10},{10,8},{9,1... | collective-permute-start | bytes 2654216 | tf_op jit(solution)/shard_map/ppermute | solution.py:1090
  242.0 34.7 %collective-permute-start.36 = (bf16[2,4,3,48,384]{4,3,2,1,0:T(8,128)(2,1)}, bf16[2,4,3,48,384]{4,3,2,1,0:T(8,128)(2,1)}, u32[]{:S(2)}, u32[]{:S(2)}) collective-permute-start(bf16[2,4,3,48,384]{4,3,2,1,0:T(8,128)(2,1)} %get-tuple-element.200), channel_id=1, source_target_pairs={{0,4},{4,0},{8,12},{12,8},{16,20},{20,16},{24,28},{28,24},{1,5},{5... | collective-permute-start | bytes 2654216 | tf_op jit(solution)/shard_map/ppermute | solution.py:1093
  258.5 26.6 %collective-permute-start.42 = (bf16[2,192,384]{2,1,0:T(8,128)(2,1)}, bf16[2,192,384]{2,1,0:T(8,128)(2,1)S(1)}, u32[]{:S(2)}, u32[]{:S(2)}) collective-permute-start(bf16[2,192,384]{2,1,0:T(8,128)(2,1)} %get-tuple-element.291), channel_id=1, source_target_pairs={{0,8},{4,12},{8,0},{12,4},{16,24},{20,28},{24,16},{28,20},{1,9},{5... | collective-permute-start | bytes 884744 | tf_op jit(solution)/shard_map/ppermute | solution.py:1093
  262.5 31.3 %collective-permute-start.46 = (bf16[2,2,240,384]{3,2,1,0:T(8,128)(2,1)}, bf16[2,2,240,384]{3,2,1,0:T(8,128)(2,1)}, u32[]{:S(2)}, u32[]{:S(2)}) collective-permute-start(bf16[2,2,240,384]{3,2,1,0:T(8,128)(2,1)} %get-tuple-element.271), channel_id=1, source_target_pairs={{0,2},{2,0},{1,3},{3,1},{4,6},{6,4},{5,7},{7,5},{8,10},{10,8},{9,1... | collective-permute-start | bytes 2211848 | tf_op jit(solution)/shard_map/ppermute | solution.py:1090
  264.8 23.4 %collective-permute-start.41 = (bf16[2,2,144,384]{3,2,1,0:T(8,128)(2,1)S(1)}, bf16[2,2,144,384]{3,2,1,0:T(8,128)(2,1)}, u32[]{:S(2)}, u32[]{:S(2)}) collective-permute-start(bf16[2,2,144,384]{3,2,1,0:T(8,128)(2,1)S(1)} %get-tuple-element.275), channel_id=1, source_target_pairs={{0,4},{4,0},{8,12},{12,8},{16,20},{20,16},{24,28},{28,24},{1,5},{5... | collective-permute-start | bytes 1327112 | tf_op jit(solution)/shard_map/ppermute | solution.py:1093
  278.9 12.0 %collective-permute-start.40 = (bf16[2,2,144,384]{3,2,1,0:T(8,128)(2,1)}, bf16[2,2,144,384]{3,2,1,0:T(8,128)(2,1)}, u32[]{:S(2)}, u32[]{:S(2)}) collective-permute-start(bf16[2,2,144,384]{3,2,1,0:T(8,128)(2,1)} %get-tuple-element.276), channel_id=1, source_target_pairs={{0,2},{2,0},{1,3},{3,1},{4,6},{6,4},{5,7},{7,5},{8,10},{10,8},{9,1... | collective-permute-start | bytes 1327112 | tf_op jit(solution)/shard_map/ppermute | solution.py:1090
  280.4 31.7 %all-to-all-start.4 = ((f32[32,16,192]{2,1,0:T(8,128)}), f32[32,16,192]{2,1,0:T(8,128)S(1)}, u32[]{:S(2)}, u32[]{:S(2)}) async-start(f32[32,16,192]{2,1,0:T(8,128)} %bitcast.146), calls=%async_computation.4 | async-start | bytes 1048576 | tf_op jit(solution)/shard_map/all_to_all | solution.py:1311
  285.3 21.3 %collective-permute-start.45 = (bf16[192,384]{1,0:T(8,128)(2,1)S(1)}, bf16[192,384]{1,0:T(8,128)(2,1)S(1)}, u32[]{:S(2)}, u32[]{:S(2)}) collective-permute-start(bf16[192,384]{1,0:T(8,128)(2,1)S(1)} %get-tuple-element.313), channel_id=1, source_target_pairs={{0,16},{4,20},{8,24},{12,28},{16,0},{20,4},{24,8},{28,12},{1,17},{... | collective-permute-start | bytes 442376 | tf_op jit(solution)/shard_map/ppermute | solution.py:1093
  289.3 17.4 %collective-permute-start.44 = (bf16[2,144,384]{2,1,0:T(8,128)(2,1)S(1)}, bf16[2,144,384]{2,1,0:T(8,128)(2,1)S(1)}, u32[]{:S(2)}, u32[]{:S(2)}) collective-permute-start(bf16[2,144,384]{2,1,0:T(8,128)(2,1)S(1)} %get-tuple-element.303), channel_id=1, source_target_pairs={{0,8},{4,12},{8,0},{12,4},{16,24},{20,28},{24,16},{28,20},{1,9},{5... | collective-permute-start | bytes 663560 | tf_op jit(solution)/shard_map/ppermute | solution.py:1093
  292.0 17.7 %collective-permute-start.43 = (bf16[2,144,384]{2,1,0:T(8,128)(2,1)S(1)}, bf16[2,144,384]{2,1,0:T(8,128)(2,1)S(1)}, u32[]{:S(2)}, u32[]{:S(2)}) collective-permute-start(bf16[2,144,384]{2,1,0:T(8,128)(2,1)S(1)} %get-tuple-element.304), channel_id=1, source_target_pairs={{0,8},{4,12},{8,0},{12,4},{16,24},{20,28},{24,16},{28,20},{1,9},{5... | collective-permute-start | bytes 663560 | tf_op jit(solution)/shard_map/ppermute | solution.py:1093
  295.1 33.5 %collective-permute-start.52 = (bf16[2,240,384]{2,1,0:T(8,128)(2,1)S(1)}, bf16[2,240,384]{2,1,0:T(8,128)(2,1)S(1)}, u32[]{:S(2)}, u32[]{:S(2)}) collective-permute-start(bf16[2,240,384]{2,1,0:T(8,128)(2,1)S(1)} %get-tuple-element.281), channel_id=1, source_target_pairs={{0,8},{4,12},{8,0},{12,4},{16,24},{20,28},{24,16},{28,20},{1,9},{5... | collective-permute-start | bytes 1105928 | tf_op jit(solution)/shard_map/ppermute | solution.py:1093
  306.6 16.7 %collective-permute-start.49 = (bf16[192,384]{1,0:T(8,128)(2,1)S(1)}, bf16[192,384]{1,0:T(8,128)(2,1)S(1)}, u32[]{:S(2)}, u32[]{:S(2)}) collective-permute-start(bf16[192,384]{1,0:T(8,128)(2,1)S(1)} %add_convert_fusion.24), channel_id=1, source_target_pairs={{0,16},{4,20},{8,24},{12,28},{16,0},{20,4},{24,8},{28,12},{1,17},{... | collective-permute-start | bytes 442376 | tf_op jit(solution)/shard_map/ppermute | solution.py:1093
  306.7 18.7 %collective-permute-start.48 = (bf16[144,384]{1,0:T(8,128)(2,1)S(1)}, bf16[144,384]{1,0:T(8,128)(2,1)S(1)}, u32[]{:S(2)}, u32[]{:S(2)}) collective-permute-start(bf16[144,384]{1,0:T(8,128)(2,1)S(1)} %get-tuple-element.319), channel_id=1, source_target_pairs={{0,16},{4,20},{8,24},{12,28},{16,0},{20,4},{24,8},{28,12},{1,17},{... | collective-permute-start | bytes 331784 | tf_op jit(solution)/shard_map/ppermute | solution.py:1093
  309.8 18.2 %collective-permute-start.53 = (bf16[144,384]{1,0:T(8,128)(2,1)S(1)}, bf16[144,384]{1,0:T(8,128)(2,1)S(1)}, u32[]{:S(2)}, u32[]{:S(2)}) collective-permute-start(bf16[144,384]{1,0:T(8,128)(2,1)S(1)} %get-tuple-element.321), channel_id=1, source_target_pairs={{0,16},{4,20},{8,24},{12,28},{16,0},{20,4},{24,8},{28,12},{1,17},{... | collective-permute-start | bytes 331784 | tf_op jit(solution)/shard_map/ppermute | solution.py:1093
  312.1 45.3 %all-to-all-start.3 = ((bf16[8,64,768]{2,1,0:T(8,128)(2,1)}), bf16[8,64,768]{2,1,0:T(8,128)(2,1)S(1)}, u32[]{:S(2)}, u32[]{:S(2)}) async-start(bf16[8,64,768]{2,1,0:T(8,128)(2,1)} %bitcast.69), calls=%async_computation.3 | async-start | bytes 1572864 | tf_op jit(solution)/shard_map/all_to_all | solution.py:1108
  323.4 23.5 %collective-permute-start.51 = (bf16[2,192,384]{2,1,0:T(8,128)(2,1)S(1)}, bf16[2,192,384]{2,1,0:T(8,128)(2,1)S(1)}, u32[]{:S(2)}, u32[]{:S(2)}) collective-permute-start(bf16[2,192,384]{2,1,0:T(8,128)(2,1)S(1)} %pad_maximum_fusion.11), channel_id=1, source_target_pairs={{0,8},{4,12},{8,0},{12,4},{16,24},{20,28},{24,16},{28,20},{1,9},{5... | collective-permute-start | bytes 884744 | tf_op jit(solution)/shard_map/ppermute | solution.py:1093
  325.5 29.1 %collective-permute-start.50 = (bf16[144,384]{1,0:T(8,128)(2,1)S(1)}, bf16[144,384]{1,0:T(8,128)(2,1)S(1)}, u32[]{:S(2)}, u32[]{:S(2)}) collective-permute-start(bf16[144,384]{1,0:T(8,128)(2,1)S(1)} %add_convert_fusion.29), channel_id=1, source_target_pairs={{0,16},{4,20},{8,24},{12,28},{16,0},{20,4},{24,8},{28,12},{1,17},{... | collective-permute-start | bytes 331784 | tf_op jit(solution)/shard_map/ppermute | solution.py:1093
  328.0 29.2 %collective-permute-start.56 = (bf16[144,384]{1,0:T(8,128)(2,1)S(1)}, bf16[144,384]{1,0:T(8,128)(2,1)S(1)}, u32[]{:S(2)}, u32[]{:S(2)}) collective-permute-start(bf16[144,384]{1,0:T(8,128)(2,1)S(1)} %add_convert_fusion.27), channel_id=1, source_target_pairs={{0,16},{4,20},{8,24},{12,28},{16,0},{20,4},{24,8},{28,12},{1,17},{... | collective-permute-start | bytes 331784 | tf_op jit(solution)/shard_map/ppermute | solution.py:1093
  328.7 31.7 %collective-permute-start.55 = (bf16[240,384]{1,0:T(8,128)(2,1)S(1)}, bf16[240,384]{1,0:T(8,128)(2,1)S(1)}, u32[]{:S(2)}, u32[]{:S(2)}) collective-permute-start(bf16[240,384]{1,0:T(8,128)(2,1)S(1)} %get-tuple-element.309), channel_id=1, source_target_pairs={{0,16},{4,20},{8,24},{12,28},{16,0},{20,4},{24,8},{28,12},{1,17},{... | collective-permute-start | bytes 552968 | tf_op jit(solution)/shard_map/ppermute | solution.py:1093
  347.0 27.1 %collective-permute-start.65 = (bf16[2,2,192,384]{3,2,1,0:T(8,128)(2,1)S(1)}, bf16[2,2,192,384]{3,2,1,0:T(8,128)(2,1)S(1)}, u32[]{:S(2)}, u32[]{:S(2)}) collective-permute-start(bf16[2,2,192,384]{3,2,1,0:T(8,128)(2,1)S(1)} %pad_maximum_fusion.7), channel_id=1, source_target_pairs={{0,4},{4,0},{8,12},{12,8},{16,20},{20,16},{24,28},{28,24},{1,5},{5... | collective-permute-start | bytes 1769480 | tf_op jit(solution)/shard_map/ppermute | solution.py:1093
  354.7 12.2 %collective-permute-start.54 = (bf16[2,144,384]{2,1,0:T(8,128)(2,1)S(1)}, bf16[2,144,384]{2,1,0:T(8,128)(2,1)S(1)}, u32[]{:S(2)}, u32[]{:S(2)}) collective-permute-start(bf16[2,144,384]{2,1,0:T(8,128)(2,1)S(1)} %pad_maximum_fusion.12), channel_id=1, source_target_pairs={{0,8},{4,12},{8,0},{12,4},{16,24},{20,28},{24,16},{28,20},{1,9},{5... | collective-permute-start | bytes 663560 | tf_op jit(solution)/shard_map/ppermute | solution.py:1093
  357.3 14.1 %collective-permute-start.60 = (bf16[2,144,384]{2,1,0:T(8,128)(2,1)S(1)}, bf16[2,144,384]{2,1,0:T(8,128)(2,1)S(1)}, u32[]{:S(2)}, u32[]{:S(2)}) collective-permute-start(bf16[2,144,384]{2,1,0:T(8,128)(2,1)S(1)} %pad_maximum_fusion.13), channel_id=1, source_target_pairs={{0,8},{4,12},{8,0},{12,4},{16,24},{20,28},{24,16},{28,20},{1,9},{5... | collective-permute-start | bytes 663560 | tf_op jit(solution)/shard_map/ppermute | solution.py:1093
  357.4 15.6 %collective-permute-start.47 = (bf16[4,64,768]{2,1,0:T(8,128)(2,1)S(1)}, bf16[4,64,768]{2,1,0:T(8,128)(2,1)S(1)}, u32[]{:S(2)}, u32[]{:S(2)}) collective-permute-start(bf16[4,64,768]{2,1,0:T(8,128)(2,1)S(1)} %dynamic-slice_bitcast_fusion.2), channel_id=1, source_target_pairs={{0,1},{1,0},{2,3},{3,2},{4,5},{5,4},{6,7},{7,6},{8,9},{9,8},{10,11... | collective-permute-start | bytes 1179656 | tf_op jit(solution)/shard_map/ppermute | solution.py:1087
  360.5 10.7 %collective-permute-start.58 = (bf16[240,384]{1,0:T(8,128)(2,1)S(1)}, bf16[240,384]{1,0:T(8,128)(2,1)S(1)}, u32[]{:S(2)}, u32[]{:S(2)}) collective-permute-start(bf16[240,384]{1,0:T(8,128)(2,1)S(1)} %add_convert_fusion.21), channel_id=1, source_target_pairs={{0,16},{4,20},{8,24},{12,28},{16,0},{20,4},{24,8},{28,12},{1,17},{... | collective-permute-start | bytes 552968 | tf_op jit(solution)/shard_map/ppermute | solution.py:1093
  367.0 14.9 %collective-permute-start.57 = (bf16[2,2,144,384]{3,2,1,0:T(8,128)(2,1)S(1)}, bf16[2,2,144,384]{3,2,1,0:T(8,128)(2,1)S(1)}, u32[]{:S(2)}, u32[]{:S(2)}) collective-permute-start(bf16[2,2,144,384]{3,2,1,0:T(8,128)(2,1)S(1)} %pad_maximum_fusion.8), channel_id=1, source_target_pairs={{0,4},{4,0},{8,12},{12,8},{16,20},{20,16},{24,28},{28,24},{1,5},{5... | collective-permute-start | bytes 1327112 | tf_op jit(solution)/shard_map/ppermute | solution.py:1093
  371.3 9.6 %collective-permute-start.59 = (bf16[2,240,384]{2,1,0:T(8,128)(2,1)S(1)}, bf16[2,240,384]{2,1,0:T(8,128)(2,1)S(1)}, u32[]{:S(2)}, u32[]{:S(2)}) collective-permute-start(bf16[2,240,384]{2,1,0:T(8,128)(2,1)S(1)} %pad_maximum_fusion.10), channel_id=1, source_target_pairs={{0,8},{4,12},{8,0},{12,4},{16,24},{20,28},{24,16},{28,20},{1,9},{5... | collective-permute-start | bytes 1105928 | tf_op jit(solution)/shard_map/ppermute | solution.py:1093
  371.5 13.4 %collective-permute-start.62 = (bf16[2,2,144,384]{3,2,1,0:T(8,128)(2,1)S(1)}, bf16[2,2,144,384]{3,2,1,0:T(8,128)(2,1)S(1)}, u32[]{:S(2)}, u32[]{:S(2)}) collective-permute-start(bf16[2,2,144,384]{3,2,1,0:T(8,128)(2,1)S(1)} %pad_maximum_fusion.9), channel_id=1, source_target_pairs={{0,4},{4,0},{8,12},{12,8},{16,20},{20,16},{24,28},{28,24},{1,5},{5... | collective-permute-start | bytes 1327112 | tf_op jit(solution)/shard_map/ppermute | solution.py:1093
  382.2 7.3 %collective-permute-start.61 = (bf16[4,3,48,384]{3,2,1,0:T(8,128)(2,1)S(1)}, bf16[4,3,48,384]{3,2,1,0:T(8,128)(2,1)S(1)}, u32[]{:S(2)}, u32[]{:S(2)}) collective-permute-start(bf16[4,3,48,384]{3,2,1,0:T(8,128)(2,1)S(1)} %fusion.18), channel_id=1, source_target_pairs={{0,1},{1,0},{2,3},{3,2},{4,5},{5,4},{6,7},{7,6},{8,9},{9,8},{10,11... | collective-permute-start | bytes 1327112 | tf_op jit(solution)/shard_map/ppermute | solution.py:1087
  386.0 6.7 %collective-permute-start.63 = (bf16[4,3,48,384]{3,2,1,0:T(8,128)(2,1)}, bf16[4,3,48,384]{3,2,1,0:T(8,128)(2,1)}, u32[]{:S(2)}, u32[]{:S(2)}) collective-permute-start(bf16[4,3,48,384]{3,2,1,0:T(8,128)(2,1)} %fusion.14), channel_id=1, source_target_pairs={{0,1},{1,0},{2,3},{3,2},{4,5},{5,4},{6,7},{7,6},{8,9},{9,8},{10,11... | collective-permute-start | bytes 1327112 | tf_op jit(solution)/shard_map/ppermute | solution.py:1087
  388.0 19.2 %collective-permute-start.64 = (bf16[2,2,240,384]{3,2,1,0:T(8,128)(2,1)}, bf16[2,2,240,384]{3,2,1,0:T(8,128)(2,1)}, u32[]{:S(2)}, u32[]{:S(2)}) collective-permute-start(bf16[2,2,240,384]{3,2,1,0:T(8,128)(2,1)} %pad_maximum_fusion.6), channel_id=1, source_target_pairs={{0,4},{4,0},{8,12},{12,8},{16,20},{20,16},{24,28},{28,24},{1,5},{5... | collective-permute-start | bytes 2211848 | tf_op jit(solution)/shard_map/ppermute | solution.py:1093
  (49 other events, 342.3 us)

commit v3 on v2

--- a/solution.py
+++ b/solution.py
@@ -817,57 +817,86 @@
     )(at, own, mine, theirs, cot, vec, *pieces)
 
 
-def weight_kernel(
-    at_ref, mine_ref, theirs_ref, hlow_ref, act_ref, gffn_ref, gup_ref, gattn_ref,
-    up_send, rest_send, up_keep, rest_keep, hid_t, att_t,
+def turned(core, outer, near, z):
+    pick = lambda a, b: jnp.where(core == 0, a, b)
+    return pick(outer, near), pick(z, outer), pick(near, z)
+
+
+def up_grad_kernel(at_ref, hlow_ref, gup_ref, send_ref, keep_ref, hid_t):
+    width = hlow_ref.shape[1]
+    n, span = width // 4, gup_ref.shape[1] // 8
+    core = at_ref[0]
+    hid_t[...] = hlow_ref[...].T
+    for which, out_ref in ((1 - core, send_ref), (core, keep_ref)):
+        for outer in range(2):
+            left = hid_t[pl.ds(pl.multiple_of((2 * outer + which) * n, 16), n), :]
+            for i in range(8):
+                out_ref[(*turned(which, outer, i // 4, i // 2 % 2), i % 2)] = jnp.dot(
+                    left, gup_ref[:, i * span : (i + 1) * span], preferred_element_type=F32
+                ).astype(BF)
+
+
+def up_grad(at, hlow, gup):
+    total, width = hlow.shape
+    ff = gup.shape[1]
+    vmem = pl.BlockSpec(memory_space=pltpu.VMEM)
+    return pl.pallas_call(
+        up_grad_kernel,
+        in_specs=[pl.BlockSpec(memory_space=pltpu.SMEM), vmem, vmem],
+        out_specs=[vmem] * 2,
+        out_shape=[jax.ShapeDtypeStruct((2, 2, 2, 2, width // 4, ff // 8), BF)] * 2,
+        scratch_shapes=[pltpu.VMEM((width, total), BF)],
+        compiler_params=pltpu.CompilerParams(vmem_limit_bytes=60 << 20),
+        cost_estimate=pl.CostEstimate(
+            flops=2 * total * width * ff, bytes_accessed=2 * width * ff + 2 * total * ff, transcendentals=0
+        ),
+        name="up_grad",
+    )(at, hlow, gup)
+
+
+def rest_grad_kernel(
+    at_ref, mine_ref, theirs_ref, act_ref, gffn_ref, gattn_ref, send_ref, keep_ref, att_t
 ):
-    total, width = hlow_ref.shape
+    width = gffn_ref.shape[1]
     span = mine_ref.shape[1]
-    ff = act_ref.shape[1]
     core = at_ref[0]
-    n, wide = width // 4, ff // 4
-    hid_t[...] = hlow_ref[...].T
+    n, wide = width // 4, act_ref.shape[1] // 4
     att_t[pl.ds(pl.multiple_of(core * span, LANES), span), :] = mine_ref[...].T
     att_t[pl.ds(pl.multiple_of((1 - core) * span, LANES), span), :] = theirs_ref[...].T
-    for which, up_ref, rest_ref in ((1 - core, up_send, rest_send), (core, up_keep, rest_keep)):
+    for which, rest_ref in ((1 - core, send_ref), (core, keep_ref)):
         for outer in range(2):
             shard = 2 * outer + which
-            rows = pl.ds(pl.multiple_of(shard * n, 16), n)
-            left = hid_t[rows, :]
-            for i in range(8):
-                up_ref[outer, i] = jnp.dot(
-                    left, gup_ref[:, i * span : (i + 1) * span], preferred_element_type=F32
-                ).astype(BF)
             left = act_ref[:, pl.ds(pl.multiple_of(shard * wide, LANES), wide)]
             down = lax.dot_general(left, gffn_ref[...], (((0,), (0,)), ((), ())), preferred_element_type=F32)
+            rows = pl.ds(pl.multiple_of(shard * n, 16), n)
             out = jnp.dot(att_t[rows, :], gattn_ref[...], preferred_element_type=F32)
             for i in range(8):
                 r, c = i // 2, i % 2
                 cols = slice(c * span, (c + 1) * span)
-                rest_ref[outer, i, : wide // 4, :] = down[r * wide // 4 : (r + 1) * wide // 4, cols].astype(BF)
-                rest_ref[outer, i, wide // 4 :, :] = out[r * n // 4 : (r + 1) * n // 4, cols].astype(BF)
-
-
-def weight_grads(at, mine, theirs, hlow, act, gffn, gup, gattn):
-    total, width = hlow.shape
+                at = (*turned(which, outer, i // 4, i // 2 % 2), i % 2)
+                rest_ref[(*at, slice(0, wide // 4))] = down[r * wide // 4 : (r + 1) * wide // 4, cols].astype(BF)
+                rest_ref[(*at, slice(wide // 4, None))] = out[r * n // 4 : (r + 1) * n // 4, cols].astype(BF)
+
+
+def rest_grad(at, mine, theirs, act, gffn, gattn):
+    total, width = gffn.shape
     span = mine.shape[1]
     ff = act.shape[1]
     vmem = pl.BlockSpec(memory_space=pltpu.VMEM)
-    shapes = [(2, 8, width // 4, ff // 8), (2, 8, ff // 16 + width // 16, span)] * 2
     return pl.pallas_call(
-        weight_kernel,
-        in_specs=[pl.BlockSpec(memory_space=pltpu.SMEM)] + [vmem] * 7,
-        out_specs=[vmem] * 4,
-        out_shape=[jax.ShapeDtypeStruct(s, BF) for s in shapes],
-        scratch_shapes=[pltpu.VMEM((width, total), BF), pltpu.VMEM((width, total), BF)],
+        rest_grad_kernel,
+        in_specs=[pl.BlockSpec(memory_space=pltpu.SMEM)] + [vmem] * 5,
+        out_specs=[vmem] * 2,
+        out_shape=[jax.ShapeDtypeStruct((2, 2, 2, 2, ff // 16 + width // 16, span), BF)] * 2,
+        scratch_shapes=[pltpu.VMEM((width, total), BF)],
         compiler_params=pltpu.CompilerParams(vmem_limit_bytes=60 << 20),
         cost_estimate=pl.CostEstimate(
-            flops=2 * total * width * (2 * ff + width),
-            bytes_accessed=4 * width * ff + 6 * total * ff,
+            flops=2 * total * width * (ff + width),
+            bytes_accessed=2 * width * ff + 2 * total * ff,
             transcendentals=0,
         ),
-        name="weight_grads",
-    )(at, mine, theirs, hlow, act, gffn, gup, gattn)
+        name="rest_grad",
+    )(at, mine, theirs, act, gffn, gattn)
 
 
 def row_backward_kernel(
@@ -998,31 +1027,96 @@
     )(gmine, gother, keep, send, inv, wts, qcat, kcat, vaug, ent, ent, *given)
 
 
-def project_back_kernel(
-    at_ref, own_ref, other_ref, gq_ref, gkv_ref, w_ref, gy1_ref,
-    send1, send2, keep1, keep2, mine_ref, away_ref, sum_ref, rows_t,
-):
+def qkv_grad_kernel(at_ref, own_ref, other_ref, gq_ref, gkv_ref, send_ref, keep_ref, rows_t):
     half, width = own_ref.shape
-    span = gkv_ref.shape[2]
-    outer, near = at_ref[0], at_ref[1]
+    n = width // 16
+    span = gq_ref.shape[2]
+    core, index = at_ref[0], at_ref[1]
     rows_t[:, :half] = own_ref[...].T
     rows_t[:, half:] = other_ref[...].T
 
+    def write(out_ref, at, start, count):
+        left = rows_t[pl.ds(pl.multiple_of(start, 16), count * n), :]
+        for b in range(6):
+            right = gq_ref[b] if b < 4 else gkv_ref[b - 4]
+            piece = jnp.dot(left, right, preferred_element_type=F32).astype(BF)
+            for p in range(count):
+                out_ref[(*at(p), b)] = piece[p * n : (p + 1) * n, :]
+
+    for which, out_ref in ((1 - index, send_ref), (index, keep_ref)):
+
+        @pl.when(core == 0)
+        def _(which=which, out_ref=out_ref):
+            write(out_ref, lambda p: (p // 2 % 2, p // 4, p % 2), which * 8 * n, 8)
+
+        @pl.when(core == 1)
+        def _(which=which, out_ref=out_ref):
+            for o in range(2):
+                write(out_ref, lambda p, o=o: (o, p // 2, p % 2), o * 8 * n + which * 4 * n, 4)
+
+
+def qkv_grad(at, own, other, gq, gkv):
+    half, width = own.shape
+    span = gkv.shape[2]
+    n = width // 16
+    vmem = pl.BlockSpec(memory_space=pltpu.VMEM)
+    return pl.pallas_call(
+        qkv_grad_kernel,
+        in_specs=[pl.BlockSpec(memory_space=pltpu.SMEM)] + [vmem] * 4,
+        out_specs=[vmem] * 2,
+        out_shape=[jax.ShapeDtypeStruct((2, 2, 2, 6, n, span), BF)] * 2,
+        scratch_shapes=[pltpu.VMEM((width, 2 * half), BF)],
+        compiler_params=pltpu.CompilerParams(vmem_limit_bytes=60 << 20),
+        cost_estimate=pl.CostEstimate(
+            flops=24 * half * width * span, bytes_accessed=32 * half * span, transcendentals=0
+        ),
+        name="qkv_grad",
+    )(at, own, other, gq, gkv)
+
+
+def add_halves_kernel(at_ref, *refs):
+    del at_ref
+    away_ref, mine_ref = refs[-2:]
+    count = (len(refs) - 2) // 4
+    for out_ref, first in ((away_ref, 0), (mine_ref, 2)):
+        at = 0
+        for p in range(count):
+            a, b = refs[4 * p + first], refs[4 * p + first + 1]
+            rows = a.shape[2]
+            out_ref[0, at : at + rows, :] = (a[0, 0].astype(F32) + b[0, 0].astype(F32)).astype(BF)
+            at += rows
+
+
+def add_halves(index, pairs):
+    pieces, cols = pairs[0][0].shape[1], pairs[0][0].shape[3]
+    height = sum(a.shape[2] for a, _ in pairs)
+    specs, arrays = [], []
+    for a, b in pairs:
+        for other in (True, False):
+            pick = (lambda i, at: (1 - at[0], i, 0, 0)) if other else (lambda i, at: (at[0], i, 0, 0))
+            specs += [pl.BlockSpec((1, 1, *a.shape[2:]), pick)] * 2
+            arrays += [a, b]
+    out = pl.BlockSpec((1, height, cols), lambda i, at: (i, 0, 0))
+    return pl.pallas_call(
+        add_halves_kernel,
+        grid_spec=pltpu.PrefetchScalarGridSpec(
+            num_scalar_prefetch=1, grid=(pieces,), in_specs=specs, out_specs=[out, out]
+        ),
+        out_shape=[jax.ShapeDtypeStruct((pieces, height, cols), BF)] * 2,
+        compiler_params=pltpu.CompilerParams(vmem_limit_bytes=60 << 20),
+        cost_estimate=pl.CostEstimate(
+            flops=2 * pieces * height * cols, bytes_accessed=12 * pieces * height * cols, transcendentals=0
+        ),
+        name="add_halves",
+    )(index, *arrays)
+
+
+def input_grad_kernel(gq_ref, gkv_ref, w_ref, gy1_ref, mine_ref, away_ref, sum_ref):
+    half = gy1_ref.shape[0]
+    span = gkv_ref.shape[2]
+
     def grads(b):
         return gq_ref.at[b] if b < 4 else gkv_ref.at[b - 4]
-
-    n = width // 16
-    for which, out_ref in ((1 - outer, send1), (outer, keep1)):
-        left = rows_t[pl.ds(pl.multiple_of(which * 8 * n, 16), 8 * n), :]
-        for b in range(3):
-            piece = jnp.dot(left, grads(b)[...], preferred_element_type=F32)
-            out_ref[:, b] = piece.reshape(8, n, span).astype(BF)
-    for which, out_ref in ((1 - near, send2), (near, keep2)):
-        for o in range(2):
-            left = rows_t[pl.ds(pl.multiple_of(o * 8 * n + which * 4 * n, 16), 4 * n), :]
-            for b in range(3):
-                piece = jnp.dot(left, grads(3 + b)[...], preferred_element_type=F32)
-                out_ref[o, :, b] = piece.reshape(4, n, span).astype(BF)
 
     def back(at):
         total = None
@@ -1042,25 +1136,63 @@
     sum_ref[6:, :] = jnp.zeros((2, span), F32)
 
 
-def project_back(at, own, other, gq, gkv, w, gy1):
-    half, width = own.shape
+def row_input_grad(gq, gkv, w, gy1):
+    half, width = gy1.shape
     span = gkv.shape[2]
-    n = width // 16
     vmem = pl.BlockSpec(memory_space=pltpu.VMEM)
-    one, two = ((8, 3, n, span), BF), ((2, 4, 3, n, span), BF)
-    shapes = [one, two, one, two, ((half, width), F32), ((half, width), BF), ((8, span), F32)]
+    shapes = [((half, width), F32), ((half, width), BF), ((8, span), F32)]
     return pl.pallas_call(
-        project_back_kernel,
-        in_specs=[pl.BlockSpec(memory_space=pltpu.SMEM)] + [vmem] * 6,
-        out_specs=[vmem] * 7,
+        input_grad_kernel,
+        in_specs=[vmem] * 4,
+        out_specs=[vmem] * 3,
         out_shape=[jax.ShapeDtypeStruct(s, d) for s, d in shapes],
-        scratch_shapes=[pltpu.VMEM((width, 2 * half), BF)],
         compiler_params=pltpu.CompilerParams(vmem_limit_bytes=60 << 20),
         cost_estimate=pl.CostEstimate(
-            flops=8 * half * width * 6 * span, bytes_accessed=20 * half * width, transcendentals=0
+            flops=4 * half * width * 6 * span, bytes_accessed=20 * half * width, transcendentals=0
         ),
-        name="project_back",
-    )(at, own, other, gq, gkv, w, gy1)
+        name="row_input_grad",
+    )(gq, gkv, w, gy1)
+
+
+def lay_rest_kernel(at_ref, mine_ref, other_ref, up_ref, down_ref, out_ref):
+    span = mine_ref.shape[2]
+    k, n, m = up_ref.shape[0], down_ref.shape[0] // 4, out_ref.shape[0] // 4
+    core, index = at_ref[0], at_ref[1]
+    for a, ref in ((index, mine_ref), (1 - index, other_ref)):
+        for b in range(2):
+            pair = jnp.where(core == 0, b * 2 + a, a * 2 + b)
+            for far in range(2):
+                j = b * 2 + far
+                cols = pl.ds(pl.multiple_of((pair * 2 + far) * span, LANES), span)
+                up_ref[:, cols] = ref[j, :k, :].astype(F32)
+                cols = slice(far * span, (far + 1) * span)
+                down_ref[pl.ds(pl.multiple_of(pair * n, 8), n), cols] = ref[j, k : k + n, :].astype(F32)
+                out_ref[pl.ds(pl.multiple_of(pair * m, 8), m), cols] = ref[j, k + n :, :].astype(F32)
+
+
+def lay_qkv_kernel(at_ref, keep_ref, got_ref, query_ref, kv_ref):
+    n, span = keep_ref.shape[2:]
+    for half, src in ((at_ref[0], keep_ref), (1 - at_ref[0], got_ref)):
+        for b in range(6):
+            ref, i = (query_ref, b) if b < 4 else (kv_ref, b - 4)
+            cols = pl.ds(pl.multiple_of(i * 2 * span + half * span, LANES), span)
+            for j in range(4):
+                ref[j * n : (j + 1) * n, cols] = src[j, b].astype(F32)
+
+
+def lay(kernel, name, at, arrays, shapes):
+    vmem = pl.BlockSpec(memory_space=pltpu.VMEM)
+    return pl.pallas_call(
+        kernel,
+        in_specs=[pl.BlockSpec(memory_space=pltpu.SMEM)] + [vmem] * len(arrays),
+        out_specs=[vmem] * len(shapes),
+        out_shape=[jax.ShapeDtypeStruct(s, F32) for s in shapes],
+        compiler_params=pltpu.CompilerParams(vmem_limit_bytes=60 << 20),
+        cost_estimate=pl.CostEstimate(
+            flops=0, bytes_accessed=6 * sum(a.size for a in arrays), transcendentals=0
+        ),
+        name=name,
+    )(at, *arrays)
 
 
 def row_layer(
@@ -1107,12 +1239,6 @@
     def over_rows(values):
         return lax.all_to_all(values, "row", 0, 0, tiled=True)
 
-    def rows_whole(back):
-        back = back.reshape(2, rows_here, span // 2, width)
-        other = swap(take(back, 1 - core))
-        both = in_order(core, take(back, core), other)
-        return both.transpose(1, 0, 2, 3).reshape(rows_here, span, width)
-
     shard = query_weight.shape[0]
     wide = down_weight.shape[0]
 
@@ -1125,15 +1251,16 @@
     q_got = cross(near_half(query_weight))
     to_rows = halves_of_rows(inputs)
     own_rows = over_rows(to_rows).reshape(own_count, width)
-    types, lengths, query_bias, cotangent, query_own, kv_own = lax.optimization_barrier(
-        (types, lengths, query_bias, cotangent, query_weight, kv_weight, to_rows)
-    )[:6]
+    query_own, kv_own, types, lengths, query_bias = lax.optimization_barrier(
+        (query_weight, kv_weight, types, lengths, query_bias, to_rows)
+    )[:5]
     q_core, kv_core = swap(query_own), swap(kv_own)
-    kv_got = cross(after(kv_weight, q_got))
-    cot_halves = halves_of_rows(cotangent)
-    q_passed = pair_up(q_got, 1)
-    q_got2, q_passed2, kv_got2 = swap(q_got), swap(q_passed), swap(kv_got)
+    q_passed, kv_got = pair_up(q_got, 1), cross(after(kv_weight, q_got))
+    q_got2 = swap(after(q_got, q_core, kv_core))
+    own_rows, q_passed = lax.optimization_barrier((own_rows, q_passed))
     other_rows = swap(own_rows)
+    q_passed2, kv_got2 = swap(q_passed), swap(kv_got)
+    cot_halves = halves_of_rows(after(cotangent, own_rows))
     query_pieces = [query_weight, q_core, q_got, q_passed, q_got2, q_passed2]
     kv_pieces = [kv_weight, kv_core, kv_got, kv_got2]
     part = shard // 2
@@ -1146,7 +1273,8 @@
     at_qkv = jnp.stack([core, *query_at, *kv_at]).astype(jnp.int32)
 
     tags = jnp.concatenate([types, lengths], axis=1)
-    tags = take(in_order(core, tags, swap(tags)).reshape(row_count, -1), row_id)
+    tags_other = after(swap(tags), q_passed)
+    tags = take(in_order(core, tags, tags_other).reshape(row_count, -1), row_id)
     types_row, lengths_row = tags[:full], tags[full:]
 
     def by_member(values):
@@ -1189,12 +1317,15 @@
     low_rows = down_weight[: wide // 2]
     u_got = cross(after(near_half(up_weight), kv_got))
     d_got = cross(after(near_half(low_rows), kv_got))
-    late_out, late_up, late_down = lax.optimization_barrier((out_weight, up_weight, down_weight, kv_got))[:3]
+    late_out, late_up, late_down = lax.optimization_barrier((out_weight, up_weight, down_weight, kv_got2))[:3]
     o_core, u_core, d_core = swap(late_out), swap(late_up), swap(late_down)
-    u_mid, d_mid, m_out, m_down = lax.optimization_barrier((u_got, d_got, out_weight, down_weight, kcat))[:4]
+    u_mid, d_mid, m_out, m_down, o_core, u_core, d_core = lax.optimization_barrier(
+        (u_got, d_got, out_weight, down_weight, o_core, u_core, d_core, kcat)
+    )[:7]
     u_passed, d_passed = pair_up(u_mid, 1), pair_up(d_mid, 1)
     o_got, t_got = cross(m_out), cross(m_down[wide // 2 :])
     u_got2, d_got2 = swap(u_mid), swap(d_mid)
+    cot = over_rows(after(cot_halves, other_rows)).reshape(own_count, width)
     keep, send, wts, inv = row_attend(qcat, kcat, vaug, qseg, kseg, heads, hd)
     theirs = swap(send)
     u_passed2, d_passed2, o_got2, t_got2 = (
@@ -1212,94 +1343,91 @@
     ]
     at_rest = jnp.stack([core, *out_at, *query_at, *down_at]).astype(jnp.int32)
 
-    cot = over_rows(after(cot_halves, own_rows)).reshape(own_count, width)
     (
         result, gy1, gmine, gtheirs, act, hlow, gffn, gup, gattn, small
     ) = token_block(at_rest, own_rows, keep, theirs, cot, vec, out_pieces, up_pieces, down_pieces)
     gother = swap(gtheirs)
     at_core = core.astype(jnp.int32).reshape(1)
-    up_send, rest_send, up_keep, rest_keep = weight_grads(
-        at_core, keep, theirs, hlow, act, gffn, gup, gattn
-    )
-    output_rows = over_rows(after(result, gother).reshape(row_count, span // 2, width))
-
-    def add(a, b):
-        return (a.astype(F32) + b.astype(F32)).astype(BF)
-
-    index_of = {"outer": outer, "y": place[0], "z": place[1], "far": place[2]}
-
-    def send_over(values, name):
-        return cross(values) if name == "outer" else pair_up(values, {"y": 1, "z": 2, "far": 4}[name])
-
-    bits = (2, 2, 2)
-    state, token = {}, [gother]
-
-    def begin(name, mine, other, left):
-        state[name] = (mine, other, left, None)
-
-    def reduce(name, axis):
-        mine, other, left, _ = state[name]
-        mine, other = lax.optimization_barrier((mine, other, token[0]))[:2]
-        at = left.index(axis)
+    at_near = near.astype(jnp.int32).reshape(1)
+    rest_send, rest_keep = rest_grad(at_core, keep, theirs, act, gffn, gattn)
+    hlow, gup, gother, rest_send = lax.optimization_barrier((hlow, gup, gother, rest_send))
+    up_send, up_keep = up_grad(at_core, hlow, gup)
+
+    def add(*arrays):
+        return functools.reduce(jnp.add, [v.astype(F32) for v in arrays]).astype(BF)
+
+    def by_core(a, b):
+        return jnp.where(core == 0, a, b)
+
+    stages = {"s1": ("outer", "y"), "s2": ("z", "outer"), "s3": ("y", "z"), "far": ("far", "far"), "g1": ("z", "y")}
+    index_on = {"outer": outer, "y": near, "z": place[1], "far": place[2]}
+    index_of = {name: by_core(index_on[a], index_on[b]) for name, (a, b) in stages.items()}
+    every = ("row", "outer", "core")
+
+    def pairs_of(stage):
+        found = []
+        for r in range(row_count):
+            for o in range(2):
+                for c in range(2):
+                    axis = stages[stage][c]
+                    to = (r, 1 - o) if axis == "outer" else (r ^ {"y": 1, "z": 2, "far": 4}[axis], o)
+                    found.append(((r * 2 + o) * 2 + c, (to[0] * 2 + to[1]) * 2 + c))
+        return found
+
+    def send_over(values, stage):
+        return lax.ppermute(values, every, pairs_of(stage))
+
+    token = [gother]
+
+    def in_turn(*arrays):
+        return lax.optimization_barrier((*arrays, token[0]))[: len(arrays)]
+
+    def halve(state, axis):
+        mine, other = in_turn(*state)
         away, mine = (
-            add(take(mine, i, at), take(other, i, at)) for i in (1 - index_of[axis], index_of[axis])
+            add(take(mine, i), take(other, i)) for i in (1 - index_of[axis], index_of[axis])
         )
         token[0] = away
-        state[name] = (mine, send_over(away, axis), [a for a in left if a != axis], None)
-
-    def gather(name, axis):
-        total = settle(name)
+        return mine, send_over(away, axis)
+
+    def start_spread(state, axis):
+        total = add(*in_turn(*state))
         token[0] = total
-        have = state[name][3] or []
-        state[name] = (total, send_over(total, axis), None, [*have, axis])
-
-    def settle(name):
-        mine, other, left, have = state[name]
-        mine, other = lax.optimization_barrier((mine, other, token[0]))[:2]
-        if left is not None:
-            assert not left
-            return add(mine, other)
-        now = [a for a in ("y", "z", "far") if a in have]
-        return in_order(index_of[have[-1]], mine, other, axis=now.index(have[-1]))
-
-    every = ["outer", "y", "z", "far"]
-
-    def pieces_of(values, *lead):
-        return values.reshape(*lead, *values.shape[-2:])
-
-    begin("up", pieces_of(up_keep, 2, *bits), pieces_of(swap(up_send), 2, *bits), every)
-    begin("rest", pieces_of(rest_keep, 2, *bits), pieces_of(swap(rest_send), 2, *bits), every)
+        return total, send_over(total, axis)
+
+    def spread(state, have, axis):
+        total = in_order(index_of[have], *in_turn(*state))
+        token[0] = total
+        return total, send_over(total, axis)
+
+    state = [
+        (v.reshape(2, 8, *v.shape[4:]), swap(w).reshape(2, 8, *v.shape[4:]))
+        for v, w in ((up_keep, up_send), (rest_keep, rest_send))
+    ]
+    away, mine = add_halves(index_of["s1"].astype(jnp.int32).reshape(1), state)
+    bits = (2, 2, 2)
+    rest = (mine.reshape(*bits, *mine.shape[1:]), send_over(away, "s1").reshape(*bits, *mine.shape[1:]))
+    gmine, _ = lax.optimization_barrier((gmine, away))
     gq, gkv = row_backward(
-        4, 2, None, gmine, gother, keep, send, inv, wts, qcat, kcat, vaug, ent, hd
-    )
+        0, heads, None, gmine, gother, keep, send, inv, wts, qcat, kcat, vaug, ent, hd
+    )
+    n = width // 16
     token[0] = gkv
-    reduce("up", "outer")
-    reduce("rest", "y")
-    gq, gkv, _ = lax.optimization_barrier((gq, gkv, token[0]))
-    gq, gkv = row_backward(
-        0, 4, (gq, gkv), gmine, gother, keep, send, inv, wts, qcat, kcat, vaug, ent, hd
-    )
-    token[0] = gkv
-    reduce("up", "y")
-    output = rows_whole(after(output_rows, gkv))
-    gq, gkv, _ = lax.optimization_barrier((gq, gkv, token[0]))
-    at_back = jnp.stack([outer, near]).astype(jnp.int32)
-    send1, send2, keep1, keep2, in_mine, in_away, six_sum = project_back(
-        at_back, own_rows, other_rows, gq, gkv, w_sel, gy1
-    )
-    n = width // 16
-    begin("one", keep1.reshape(*bits, 3 * n, cols), cross(send1).reshape(*bits, 3 * n, cols), every[1:])
-    begin(
-        "two",
-        keep2.reshape(2, *bits[1:], 3 * n, cols),
-        pair_up(send2, 1).reshape(2, *bits[1:], 3 * n, cols),
-        ["outer", "z", "far"],
-    )
-    grad_in = (in_mine + swap(in_away).astype(F32)).astype(BF)
-    token[0] = grad_in
-    input_rows = over_rows(grad_in.reshape(row_count, span // 2, width))
-    reduce("up", "z")
-    reduce("rest", "outer")
+    rest = halve(rest, "s2")
+    at_first = jnp.stack([core, index_of["s1"]]).astype(jnp.int32)
+    q_send, q_keep = qkv_grad(at_first, own_rows, after(other_rows, token[0]), gq, gkv)
+    six = (q_keep.reshape(*bits, 6 * n, cols), send_over(q_send, "s1").reshape(*bits, 6 * n, cols))
+    in_mine, in_away, six_sum = row_input_grad(gq, gkv, after(w_sel, q_send), gy1)
+    in_other = swap(in_away)
+    token[0] = in_away
+    rest = halve(rest, "s3")
+    in_mine, in_other = in_turn(in_mine, in_other)
+    grad_in = (in_mine + in_other.astype(F32)).astype(BF)
+    both_out = jnp.stack([v.reshape(row_count, span // 2, width) for v in (result, grad_in)], axis=1)
+    token[0] = both_out
+    both_out = over_rows(both_out)
+    six = halve(six, "s2")
+    rest = halve(rest, "far")
 
     spot = lax.broadcasted_iota(jnp.int32, (1, 2, 1), 1) == core
     wide_sum = jnp.where(spot, six_sum[:6].reshape(6, 1, cols), 0.0).reshape(6, width)
@@ -1308,50 +1436,37 @@
         [small[:4].reshape(4, 4, shard), wide_sum[:4].reshape(4, 4, shard), each, jnp.zeros_like(each[:, :1])], axis=1
     )
     small = jnp.broadcast_to(small[None], (row_count, 4, 16, shard)).reshape(-1, 16, shard)
-    small = lax.all_to_all(
-        after(small, token[0]), ("row", "group", "outer", "core"), 0, 0, tiled=True
-    )
-
-    reduce("one", "y")
-    reduce("two", "outer")
-    reduce("up", "far")
-    reduce("one", "z")
-    reduce("two", "z")
-    reduce("rest", "z")
-    small = jnp.sum(after(small, token[0]), axis=0)
-    gather("up", "far")
-    reduce("one", "far")
-    reduce("two", "far")
-    input_grad = rows_whole(after(input_rows, token[0]))
-    gather("up", "z")
-    gather("one", "far")
-    gather("two", "far")
-    reduce("rest", "far")
-    gather("up", "y")
-    gather("one", "z")
-    gather("two", "z")
-    gather("rest", "far")
-    gather("one", "y")
-    gather("rest", "z")
-    gather("two", "y")
-    up_total = settle("up")
-    gather("rest", "y")
-    first_total, second_total, rest_total = settle("one"), settle("two"), settle("rest")
-
-    def both_cores(total):
-        parts = total.reshape(2, 4, 3, -1, cols)
-        halves = in_order(core, take(parts, core), swap(take(parts, 1 - core)))
-        return halves.transpose(1, 3, 2, 0, 4).reshape(shard, 3 * width).astype(F32)
-
-    one, two = both_cores(first_total), both_cores(second_total)
-    g_query = jnp.concatenate([one, two[:, :width]], axis=1)
-    g_kv = two[:, width:]
-    g_up = up_total.reshape(8, shard, -1).transpose(1, 0, 2).reshape(shard, -1).astype(F32)
-    rest_total = rest_total.reshape(4, 2, -1, cols)
-    n = wide // 4
-    g_down = rest_total[:, :, :n].transpose(0, 2, 1, 3).reshape(wide, width).astype(F32)
-    g_out = rest_total[:, :, n:].transpose(0, 2, 1, 3).reshape(shard, width).astype(F32)
-
+    small = lax.all_to_all(small, ("row", "group", "outer", "core"), 0, 0, tiled=True)
+
+    six = halve(six, "s3")
+    rest = start_spread(rest, "far")
+    six = halve(six, "far")
+    both_out = in_turn(both_out)[0]
+    token[0] = both_out
+    rest = spread(rest, "far", "s3")
+    six = start_spread(six, "far")
+    rest = spread(rest, "s3", "g1")
+    small = jnp.sum(in_turn(small)[0], axis=0)
+    token[0] = small
+    six = spread(six, "far", "s3")
+    both_out = both_out.reshape(2, rows_here, 2, span // 2, width)
+    halves = in_order(core, take(both_out, core), swap(take(both_out, 1 - core)))
+    output, input_grad = (
+        halves[:, :, i].transpose(1, 0, 2, 3).reshape(rows_here, span, width) for i in range(2)
+    )
+    six = spread(six, "s3", "g1")
+    at_last = jnp.stack([core, index_of["g1"]]).astype(jnp.int32)
+    g_up, g_down, g_out = lay(
+        lay_rest_kernel, "lay_rest", at_last, [v.reshape(4, *v.shape[2:]) for v in in_turn(*rest)],
+        [up_weight.shape, down_weight.shape, out_weight.shape],
+    )
+    token[0] = g_out
+    six = in_order(index_of["g1"], *in_turn(*six))
+    away, kept = by_core(six[:, 1], six[0]), by_core(six[:, 0], six[1])
+    parts = [v.reshape(4, 6, n, cols) for v in (kept, swap(away))]
+    g_query, g_kv = lay(
+        lay_qkv_kernel, "lay_qkv", at_core, parts, [query_weight.shape, kv_weight.shape]
+    )
     return (
         output, input_grad, g_query, g_kv, g_out, g_up, g_down,
         small[4:8].reshape(-1), small[14], small[8], small[:4].reshape(-1), *(small[i] for i in range(9, 14)),

time: 420 us -> 395 us (0.940)
  starting transfers between devices: 88.7 us -> 59 us
  Pallas kernels: 129 us -> 150 us
  local copies, waits for them, and re-layouts: 36.6 us -> 23 us
  other arithmetic: 47.5 us -> 34.4 us
  waiting for transfers between devices: 110 us -> 123 us
    ppermute x27 -> x3, waiting for transfers between devices: 84.2 us -> 4.08 us  [pair_up(): return lax.ppermute(values, 'row', [(i, i ^ bit) for i in range(row_count)])]
    ppermute x0 -> x14, waiting for transfers between devices: none -> 78.9 us  [send_over(): return lax.ppermute(values, every, pairs_of(stage))]
    ppermute x27 -> x3, starting transfers between devices: 39.6 us -> 4.05 us  [pair_up(): return lax.ppermute(values, 'row', [(i, i ^ bit) for i in range(row_count)])]
    pallas_call x2 -> x7, Pallas kernels: 29.5 us -> 53.6 us  [the longest x1 10.6 us: row_input_grad(): pl.pallas_call(input_grad_kernel, in_specs=[vmem] * 4, out_specs=[vmem] *...]
    all_to_all x1, waiting for transfers between devices: 0.01 us -> 17.4 us  [row_layer(): lax.all_to_all(small, ('row', 'group', 'outer', 'core'), 0, 0, tiled=True)]
    ppermute x0 -> x14, starting transfers between devices: none -> 15.2 us  [send_over(): return lax.ppermute(values, every, pairs_of(stage))]
    all_to_all x4 -> x3, starting transfers between devices: 26.9 us -> 15.5 us  [over_rows(): return lax.all_to_all(values, 'row', 0, 0, tiled=True)]
    convert_element_type x25 -> x9, other arithmetic: 25.1 us -> 14.6 us  [the longest x8 14.4 us: add(): return functools.reduce(jnp.add, [v.astype(F32) for v in arrays]).astype(BF)]
  transfers between devices with their start and end apart: 71 -> 54, of which waited for: 23 -> 19; matrix products, arithmetic and copies ran while one was open for 18% -> 12% of each run, Pallas kernels for 20% -> 27%
where the time goes in v3:
time: 395 us; the launch traced here: 391 us
  Pallas kernels  150 us (38%)
  waiting for transfers between devices  123 us (31%)
  starting transfers between devices  59 us (15%)
  other arithmetic  34.4 us (9%)
  local copies, waits for them, and re-layouts  23 us (6%)
    ppermute x14, waiting for transfers between devices, send_over(): return lax.ppermute(values, every, pairs_of(stage))  78.9 us
    pallas_call x1, Pallas kernels, row_backward(): pl.pallas_call(functools.partial(row_backward_kernel, heads, hd, first_he...  34.8 us
    pallas_call x1, Pallas kernels, token_block(): pl.pallas_call(functools.partial(token_kernel, rows(out_pieces), rows(up_...  32.4 us
    pallas_call x1, Pallas kernels, row_attend(): pl.pallas_call(functools.partial(attend_kernel, heads, hd), grid=(full //...  17.5 us
    all_to_all x1, waiting for transfers between devices, row_layer(): lax.all_to_all(small, ('row', 'group', 'outer', 'core'), 0, 0, tiled=True)  17.4 us
    ppermute x7, waiting for transfers between devices, cross(): return lax.ppermute(values, 'outer', both_ways)  16 us
    all_to_all x3, starting transfers between devices, over_rows(): return lax.all_to_all(values, 'row', 0, 0, tiled=True)  15.5 us
    ppermute x14, starting transfers between devices, send_over(): return lax.ppermute(values, every, pairs_of(stage))  15.2 us
  transfers between devices with their start and end apart: 54, of which 19 were waited for; matrix products, arithmetic and copies ran while one was open for 12% of the time, Pallas kernels for 27%

profile of v3, /device:TPU:0, one launch (start us, length us, event | category | flops | bytes accessed | tf_op | source)
XLA Modules:
  0.0 391.1 jit_solution(10718127318717556276)
XLA Ops:
  0.7 2.0 dynamic-slice_bitcast_fusion.2
  2.7 3.0 collective-permute-start.1
  5.7 1.0 dynamic-slice_bitcast_fusion.4
  8.6 1.1 dynamic-slice_bitcast_fusion.1
  9.8 0.9 pad_maximum_fusion.5
  10.8 6.0 %all-to-all-start = ((bf16[8,64,768]{2,1,0:T(8,128)(2,1)}), bf16[8,64,768]{2,1,0:T(8,128)(2,1)S(1)}, u32[]{:S(2)}, u32[]{:S(2)}) async-start(bf16[8,64,768]{2,1,0:T(8,128)(2,1)} %bitcast.22), calls=%async_computation | async-start | bytes 1572864 | tf_op jit(solution)/shard_map/all_to_all | solution.py:1240
  18.1 3.1 collective-permute-done.4
  23.1 2.0 collective-permute-start.2
  26.0 12.2 %collective-permute-done.11.refs_8_ = bf16[192,1536]{1,0:T(8,128)(2,1)} collective-permute-done((bf16[192,1536]{1,0:T(8,128)(2,1)}, bf16[192,1536]{1,0:T(8,128)(2,1)}, u32[]{:S(2)}, u32[]{:S(2)}) %collective-permute-start.11) | collective-permute-done | bytes 589856 | tf_op jit(solution)/shard_map/ppermute | solution.py:1222
  38.8 3.0 collective-permute-done.2.refs_3_
  46.7 2.6 convert_add_fusion
  49.6 1.0 select_convert_fusion
  50.6 1.1 collective-permute-start.15
  51.7 1.1 fusion.19
  52.7 0.9 pad_maximum_fusion.6
  53.7 5.4 %all-to-all-start.1 = ((bf16[8,64,768]{2,1,0:T(8,128)(2,1)}), bf16[8,64,768]{2,1,0:T(8,128)(2,1)S(1)}, u32[]{:S(2)}, u32[]{:S(2)}) async-start(bf16[8,64,768]{2,1,0:T(8,128)(2,1)} %bitcast.45), calls=%async_computation.1 | async-start | bytes 1572864 | tf_op jit(solution)/shard_map/all_to_all | solution.py:1240
  59.2 1.3 collective-permute-start.16
  61.3 11.6 %row_project.1 = (bf16[6,1024,128]{2,1,0:T(8,128)(2,1)}, bf16[6,1024,128]{2,1,0:T(8,128)(2,1)}, bf16[6,1024,128]{2,1,0:T(8,128)(2,1)}, bf16[768,2304]{1,0:T(8,128)(2,1)}) custom-call(s32[11]{0:T(128)} %stack.205.at_ref, bf16[512,768]{1,0:T(8,128)(2,1)} %bitcast.204, bf16[512,768]{1,0:T(8,128)(2,1)} %collective-permute-done.3.other_ref, f32[1,2304]{1,0:T(1,128)} %bitcast.225, ...), custom_call_target="tpu_custom_call" | custom-call | flops 3623878656 | bytes 14155776 | tf_op jit(solution)/shard_map/row_project/pallas_call | solution.py:543
  74.0 2.0 collective-permute-start.21
  76.0 1.2 collective-permute-start.20
  77.2 17.5 %row_attend.1 = (bf16[512,384]{1,0:T(8,128)(2,1)}, bf16[512,384]{1,0:T(8,128)(2,1)}, bf16[6,1024,1024]{2,1,0:T(8,128)(2,1)}, f32[1024,128]{1,0:T(8,128)}) custom-call(bf16[6,1024,128]{2,1,0:T(8,128)(2,1)} %get-tuple-element.129.qcat_ref, bf16[1024,128]{1,0:T(8,128)(2,1)} %get-tuple-element.282.qseg_ref, bf16[6,1024,128]{2,1,0:T(8,128)(2,1)} %get-tuple-element.130.kcat_ref, ...), custom_call_target="tpu_custom_call" | custom-call | flops 6442450944 | bytes 15728640 | tf_op jit(solution)/shard_map/row_attend/pallas_call | solution.py:608
  95.3 1.0 collective-permute-done.22.refs_13_
  101.9 32.4 %token_block.1 = (bf16[512,768]{1,0:T(8,128)(2,1)}, f32[512,768]{1,0:T(8,128)}, bf16[512,384]{1,0:T(8,128)(2,1)}, bf16[512,384]{1,0:T(8,128)(2,1)}, bf16[512,307...) custom-call(s32[19]{0:T(128)} %stack.201.at_ref, ...), custom_call_target="tpu_custom_call" | custom-call | flops 10871635968 | bytes 18874368 | tf_op jit(solution)/shard_map/token_block/pallas_call | solution.py:789
  134.5 8.3 %rest_grad.1 = (bf16[2,2,2,2,240,384]{5,4,3,2,1,0:T(8,128)(2,1)}, bf16[2,2,2,2,240,384]{5,4,3,2,1,0:T(8,128)(2,1)}) custom-call(s32[1]{0:T(128)} %bitcast.at_ref, bf16[512,384]{1,0:T(8,128)(2,1)} %get-tuple-element.132.mine_ref.keep_ref, bf16[512,384]{1,0:T(8,128)(2,1)} %copy-done.23, bf16[512,3072]{1,0:T(8,128)(2,1)} %get-tuple-element.157.act_ref, ...), custom_call_target="tpu_custom_call" | custom-call | flops 3019898880 | bytes 7864320 | tf_op jit(solution)/shard_map/rest_grad/pallas_call | solution.py:886
  143.1 7.9 %up_grad.1 = (bf16[2,2,2,2,192,384]{5,4,3,2,1,0:T(8,128)(2,1)}, bf16[2,2,2,2,192,384]{5,4,3,2,1,0:T(8,128)(2,1)}) custom-call(s32[1]{0:T(128)} %bitcast.at_ref, bf16[512,768]{1,0:T(8,128)(2,1)} %get-tuple-element.161.hlow_ref, bf16[512,3072]{1,0:T(8,128)(2,1)} %get-tuple-element.162.gup_ref), custom_call_target="tpu_custom_call" | custom-call | flops 2415919104 | bytes 7864320 | tf_op jit(solution)/shard_map/up_grad/pallas_call | solution.py:843
  151.2 4.7 %collective-permute-done.31 = bf16[2,2,2,2,192,384]{5,4,3,2,1,0:T(8,128)(2,1)} collective-permute-done((bf16[2,2,2,2,192,384]{5,4,3,2,1,0:T(8,128)(2,1)}, bf16[2,2,2,2,192,384]{5,4,3,2,1,0:T(8,128)(2,1)}, u32[]{:S(2)}, u32[]{:S(2)}) %collective-permute-start.31) | collective-permute-done | bytes 2359328 | tf_op jit(solution)/shard_map/ppermute | solution.py:1219
  155.9 1.6 copy-done
  157.5 8.4 %add_halves.1 = (bf16[8,432,384]{2,1,0:T(8,128)(2,1)}, bf16[8,432,384]{2,1,0:T(8,128)(2,1)}) custom-call(s32[1]{0:T(128)} %bitcast.53.at_ref, bf16[2,8,192,384]{3,2,1,0:T(8,128)(2,1)} %bitcast.192, bf16[2,8,192,384]{3,2,1,0:T(8,128)(2,1)} %bitcast.55.refs_1_.refs_3_, bf16[2,8,192,384]{3,2,1,0:T(8,128)(2,1)} %bitcast.193, ...), custom_call_target="tpu_custom_call" | custom-call | flops 2654208 | bytes 15925248 | tf_op jit(solution)/shard_map/add_halves/pallas_call | solution.py:1100
  165.9 1.2 collective-permute-start.33
  167.1 34.8 %row_backward.1 = (bf16[4,1024,384]{2,1,0:T(8,128)(2,1)}, bf16[2,1024,384]{2,1,0:T(8,128)(2,1)}) custom-call(bf16[512,384]{1,0:T(8,128)(2,1)} %get-tuple-element.168.gmine_ref, bf16[512,384]{1,0:T(8,128)(2,1)} %copy-done.24, bf16[512,384]{1,0:T(8,128)(2,1)} %get-tuple-element.132.mine_ref.keep_ref, bf16[512,384]{1,0:T(8,128)(2,1)} %get-tuple-element.133.send_ref, ...), custom_call_target="tpu_custom_call" | custom-call | flops 12884901888 | bytes 20447232 | tf_op jit(solution)/shard_map/row_backward/pallas_call | solution.py:991
  201.9 1.5 copy-done.1
  203.4 3.2 fusion.1
  206.6 2.7 collective-permute-start.35
  209.9 10.5 %qkv_grad.1 = (bf16[2,2,2,6,48,384]{5,4,3,2,1,0:T(8,128)(2,1)}, bf16[2,2,2,6,48,384]{5,4,3,2,1,0:T(8,128)(2,1)}) custom-call(s32[2]{0:T(128)} %pad_add_fusion.2.at_ref, bf16[512,768]{1,0:T(8,128)(2,1)} %bitcast.206, bf16[512,768]{1,0:T(8,128)(2,1)} %collective-permute-done.3.other_ref, bf16[4,1024,384]{2,1,0:T(8,128)(2,1)} %get-tuple-element.172.gq_ref, ...), custom_call_target="tpu_custom_call" | custom-call | flops 3623878656 | bytes 6291456 | tf_op jit(solution)/shard_map/qkv_grad/pallas_call | solution.py:1063
  220.4 10.6 %row_input_grad.1 = (f32[512,768]{1,0:T(8,128)}, bf16[512,768]{1,0:T(8,128)(2,1)}, f32[8,384]{1,0:T(8,128)}) custom-call(bf16[4,1024,384]{2,1,0:T(8,128)(2,1)} %get-tuple-element.172.gq_ref, bf16[2,1024,384]{2,1,0:T(8,128)(2,1)} %get-tuple-element.173.gkv_ref, bf16[768,2304]{1,0:T(8,128)(2,1)} %get-tuple-element.180.w_ref, f32[512,768]{1,0:T(8,128)} %get-tuple-element.181.gy1_ref), custom_call_target="tpu_custom_call" | custom-call | flops 3623878656 | bytes 7864320 | tf_op jit(solution)/shard_map/row_input_grad/pallas_call | solution.py:1144
  231.5 2.6 fusion.15
  235.3 1.3 pad_maximum_fusion
  236.6 4.1 %all-to-all-start.2 = ((bf16[8,2,64,768]{3,2,1,0:T(8,128)(2,1)}), bf16[8,2,64,768]{3,2,1,0:T(8,128)(2,1)S(1)}, u32[]{:S(2)}, u32[]{:S(2)}) async-start(bf16[8,2,64,768]{3,2,1,0:T(8,128)(2,1)} %pad_maximum_fusion), calls=%async_computation.2 | async-start | bytes 3145728 | tf_op jit(solution)/shard_map/all_to_all | solution.py:1240
  240.6 2.0 collective-permute-start.38
  242.7 11.3 %collective-permute-done.36 = bf16[2,2,2,6,48,384]{5,4,3,2,1,0:T(8,128)(2,1)} collective-permute-done((bf16[2,2,2,6,48,384]{5,4,3,2,1,0:T(8,128)(2,1)}, bf16[2,2,2,6,48,384]{5,4,3,2,1,0:T(8,128)(2,1)}, u32[]{:S(2)}, u32[]{:S(2)}) %collective-permute-start.36) | collective-permute-done | bytes 1769504 | tf_op jit(solution)/shard_map/ppermute | solution.py:1378
  253.9 3.3 fusion.3
  257.4 18.2 %collective-permute-done.38 = bf16[2,432,384]{2,1,0:T(8,128)(2,1)} collective-permute-done((bf16[2,432,384]{2,1,0:T(8,128)(2,1)}, bf16[2,432,384]{2,1,0:T(8,128)(2,1)}, u32[]{:S(2)}, u32[]{:S(2)}) %collective-permute-start.38) | collective-permute-done | bytes 663584 | tf_op jit(solution)/shard_map/ppermute | solution.py:1378
  275.6 2.0 fusion.26
  277.6 1.5 collective-permute-start.40
  280.6 8.6 %collective-permute-done.37 = bf16[2,2,288,384]{3,2,1,0:T(8,128)(2,1)} collective-permute-done((bf16[2,2,288,384]{3,2,1,0:T(8,128)(2,1)}, bf16[2,2,288,384]{3,2,1,0:T(8,128)(2,1)}, u32[]{:S(2)}, u32[]{:S(2)}) %collective-permute-start.37) | collective-permute-done | bytes 884768 | tf_op jit(solution)/shard_map/ppermute | solution.py:1378
  289.1 1.4 fusion.18
  290.5 1.4 collective-permute-start.39
  291.9 1.1 add_convert_fusion.9
  294.3 4.6 %collective-permute-done.39 = bf16[2,288,384]{2,1,0:T(8,128)(2,1)S(1)} collective-permute-done((bf16[2,288,384]{2,1,0:T(8,128)(2,1)S(1)}, bf16[2,288,384]{2,1,0:T(8,128)(2,1)S(1)}, u32[]{:S(2)}, u32[]{:S(2)}) %collective-permute-start.39) | collective-permute-done | bytes 442400 | tf_op jit(solution)/shard_map/ppermute | solution.py:1378
  299.7 9.9 %collective-permute-done.43 = bf16[432,384]{1,0:T(8,128)(2,1)S(1)} collective-permute-done((bf16[432,384]{1,0:T(8,128)(2,1)S(1)}, bf16[432,384]{1,0:T(8,128)(2,1)S(1)}, u32[]{:S(2)}, u32[]{:S(2)}) %collective-permute-start.43) | collective-permute-done | bytes 331808 | tf_op jit(solution)/shard_map/ppermute | solution.py:1378
  311.1 10.9 %all-to-all-start.3 = ((f32[32,16,192]{2,1,0:T(8,128)}), f32[32,16,192]{2,1,0:T(8,128)S(1)}, u32[]{:S(2)}, u32[]{:S(2)}) async-start(f32[32,16,192]{2,1,0:T(8,128)} %bitcast.90), calls=%async_computation.3 | async-start | bytes 1048576 | tf_op jit(solution)/shard_map/all_to_all | solution.py:1439
  322.0 2.7 collective-permute-start.44
  324.8 1.2 select_bitcast_fusion.1
  326.0 1.2 pad_maximum_fusion.1
  327.2 17.4 %all-to-all-done.3 = f32[32,16,192]{2,1,0:T(8,128)S(1)} async-done(((f32[32,16,192]{2,1,0:T(8,128)}), f32[32,16,192]{2,1,0:T(8,128)S(1)}, u32[]{:S(2)}, u32[]{:S(2)}) %all-to-all-start.3) | async-done | bytes 393248 | tf_op jit(solution)/shard_map/all_to_all | solution.py:1439
  344.7 3.6 collective-permute-done.44
  348.3 2.1 collective-permute-start.46
  350.5 11.0 %collective-permute-done.46 = bf16[2,288,384]{2,1,0:T(8,128)(2,1)S(1)} collective-permute-done((bf16[2,288,384]{2,1,0:T(8,128)(2,1)S(1)}, bf16[2,288,384]{2,1,0:T(8,128)(2,1)S(1)}, u32[]{:S(2)}, u32[]{:S(2)}) %collective-permute-start.46) | collective-permute-done | bytes 442400 | tf_op jit(solution)/shard_map/ppermute | solution.py:1378
  363.2 6.9 %collective-permute-done.48 = bf16[2,2,432,384]{3,2,1,0:T(8,128)(2,1)} collective-permute-done((bf16[2,2,432,384]{3,2,1,0:T(8,128)(2,1)}, bf16[2,2,432,384]{3,2,1,0:T(8,128)(2,1)}, u32[]{:S(2)}, u32[]{:S(2)}) %collective-permute-start.48) | collective-permute-done | bytes 1327136 | tf_op jit(solution)/shard_map/ppermute | solution.py:1378
  370.1 4.4 %lay_rest.1 = (f32[192,3072]{1,0:T(8,128)}, f32[768,768]{1,0:T(8,128)}, f32[192,768]{1,0:T(8,128)}) custom-call(s32[2]{0:T(128)} %pad_add_fusion.3.at_ref, bf16[4,432,384]{2,1,0:T(8,128)(2,1)} %bitcast.98.mine_ref, bf16[4,432,384]{2,1,0:T(8,128)(2,1)} %bitcast.99.other_ref), custom_call_target="tpu_custom_call" | custom-call | bytes 7962624 | tf_op jit(solution)/shard_map/lay_rest/pallas_call | solution.py:1185
  374.6 5.0 %collective-permute-done.47 = bf16[2,2,288,384]{3,2,1,0:T(8,128)(2,1)S(1)} collective-permute-done((bf16[2,2,288,384]{3,2,1,0:T(8,128)(2,1)S(1)}, bf16[2,2,288,384]{3,2,1,0:T(8,128)(2,1)S(1)}, u32[]{:S(2)}, u32[]{:S(2)}) %collective-permute-start.47) | collective-permute-done | bytes 884768 | tf_op jit(solution)/shard_map/ppermute | solution.py:1378
  379.7 1.5 fusion.8
  383.2 1.2 fusion.13
  387.4 3.4 lay_qkv.1
  (240 shorter events, 34.7 us)
Async XLA Ops:
  2.7 19.8 %collective-permute-start.1 = (bf16[96,3072]{1,0:T(8,128)(2,1)}, bf16[96,3072]{1,0:T(8,128)(2,1)}, u32[]{:S(2)}, u32[]{:S(2)}) collective-permute-start(bf16[96,3072]{1,0:T(8,128)(2,1)} %dynamic-slice_bitcast_fusion.2), channel_id=1, source_target_pairs={{0,2},{2,0},{1,3},{3,1},{4,6},{6,4},{5,7},{7,5},{8,10},{10,8},{9,1... | collective-permute-start | bytes 1769480 | tf_op jit(solution)/shard_map/ppermute | solution.py:1222
  6.8 2.9 collective-permute-start
  9.8 11.5 %copy-start.18 = (s32[4,4]{1,0:T(4,128)S(1)}, s32[4,4]{1,0:T(4,128)}, u32[]{:S(2)}) copy-start(s32[4,4]{1,0:T(4,128)} %param.34) | copy-start | bytes 196
  9.8 32.1 %copy-start.8 = (bf16[4,128,768]{2,1,0:T(8,128)(2,1)S(1)}, bf16[4,128,768]{2,1,0:T(8,128)(2,1)}, u32[]{:S(2)}) copy-start(bf16[4,128,768]{2,1,0:T(8,128)(2,1)} %param.35) | copy-start | bytes 2359300
  10.8 35.5 %copy-start.3 = (bf16[768,768]{1,0:T(8,128)(2,1)S(1)}, bf16[768,768]{1,0:T(8,128)(2,1)}, u32[]{:S(2)}) copy-start(bf16[768,768]{1,0:T(8,128)(2,1)} %refs_10_.1) | copy-start | bytes 3538948
  10.8 31.0 %all-to-all-start = ((bf16[8,64,768]{2,1,0:T(8,128)(2,1)}), bf16[8,64,768]{2,1,0:T(8,128)(2,1)S(1)}, u32[]{:S(2)}, u32[]{:S(2)}) async-start(bf16[8,64,768]{2,1,0:T(8,128)(2,1)} %bitcast.22), calls=%async_computation | async-start | bytes 1572864 | tf_op jit(solution)/shard_map/all_to_all | solution.py:1240
  16.7 21.5 %collective-permute-start.7 = (bf16[192,3072]{1,0:T(8,128)(2,1)}, bf16[192,3072]{1,0:T(8,128)(2,1)}, u32[]{:S(2)}, u32[]{:S(2)}) collective-permute-start(bf16[192,3072]{1,0:T(8,128)(2,1)} %refs_0_.2), channel_id=1, source_target_pairs={{0,1},{1,0},{2,3},{3,2},{4,5},{5,4},{6,7},{7,6},{8,9},{9,8},{10,11... | collective-permute-start | bytes 3538952 | tf_op jit(solution)/shard_map/ppermute | solution.py:1219
  16.9 21.3 %collective-permute-start.8 = (bf16[192,1536]{1,0:T(8,128)(2,1)}, bf16[192,1536]{1,0:T(8,128)(2,1)}, u32[]{:S(2)}, u32[]{:S(2)}) collective-permute-start(bf16[192,1536]{1,0:T(8,128)(2,1)} %refs_6_.1), channel_id=1, source_target_pairs={{0,1},{1,0},{2,3},{3,2},{4,5},{5,4},{6,7},{7,6},{8,9},{9,8},{10,11... | collective-permute-start | bytes 1769480 | tf_op jit(solution)/shard_map/ppermute | solution.py:1219
  17.5 3.7 collective-permute-start.4
  21.2 1.2 collective-permute-start.5
  21.3 20.5 %collective-permute-start.6 = (s32[4,1028]{1,0:T(4,128)S(1)}, s32[4,1028]{1,0:T(4,128)S(1)}, u32[]{:S(2)}, u32[]{:S(2)}) collective-permute-start(s32[4,1028]{1,0:T(4,128)S(1)} %constant_dynamic-update-slice_fusion), channel_id=1, source_target_pairs={{0,1},{1,0},{2,3},{3,2},{4,5},{5,4},{6,7},{7,6},{8,9},{9,8},{10,11... | collective-permute-start | bytes 49352 | tf_op jit(solution)/shard_map/ppermute | solution.py:1219
  22.5 15.8 %collective-permute-start.11 = (bf16[192,1536]{1,0:T(8,128)(2,1)}, bf16[192,1536]{1,0:T(8,128)(2,1)}, u32[]{:S(2)}, u32[]{:S(2)}) collective-permute-start(bf16[192,1536]{1,0:T(8,128)(2,1)} %refs_6_.1), channel_id=1, source_target_pairs={{0,2},{2,0},{1,3},{3,1},{4,6},{6,4},{5,7},{7,5},{8,10},{10,8},{9,1... | collective-permute-start | bytes 1769480 | tf_op jit(solution)/shard_map/ppermute | solution.py:1222
  23.1 18.7 %collective-permute-start.2 = (bf16[96,3072]{1,0:T(8,128)(2,1)}, bf16[96,3072]{1,0:T(8,128)(2,1)}, u32[]{:S(2)}, u32[]{:S(2)}) collective-permute-start(bf16[96,3072]{1,0:T(8,128)(2,1)} %collective-permute-done.1.refs_2_), channel_id=1, source_target_pairs={{0,4},{4,0},{8,12},{12,8},{16,20},{20,16},{24,28},{28,24},{1,5},{5... | collective-permute-start | bytes 1769480 | tf_op jit(solution)/shard_map/ppermute | solution.py:1225
  38.3 7.8 %collective-permute-start.12 = (bf16[192,1536]{1,0:T(8,128)(2,1)}, bf16[192,1536]{1,0:T(8,128)(2,1)}, u32[]{:S(2)}, u32[]{:S(2)}) collective-permute-start(bf16[192,1536]{1,0:T(8,128)(2,1)} %collective-permute-done.11.refs_8_), channel_id=1, source_target_pairs={{0,1},{1,0},{2,3},{3,2},{4,5},{5,4},{6,7},{7,6},{8,9},{9,8},{10,11... | collective-permute-start | bytes 1769480 | tf_op jit(solution)/shard_map/ppermute | solution.py:1219
  38.3 20.9 %collective-permute-start.9 = (bf16[96,3072]{1,0:T(8,128)(2,1)}, bf16[96,3072]{1,0:T(8,128)(2,1)}, u32[]{:S(2)}, u32[]{:S(2)}) collective-permute-start(bf16[96,3072]{1,0:T(8,128)(2,1)} %collective-permute-done.1.refs_2_), channel_id=1, source_target_pairs={{0,1},{1,0},{2,3},{3,2},{4,5},{5,4},{6,7},{7,6},{8,9},{9,8},{10,11... | collective-permute-start | bytes 1769480 | tf_op jit(solution)/shard_map/ppermute | solution.py:1219
  41.8 10.9 %copy-start.5 = (bf16[8,64,768]{2,1,0:T(8,128)(2,1)}, bf16[8,64,768]{2,1,0:T(8,128)(2,1)S(1)}, u32[]{:S(2)}) copy-start(bf16[8,64,768]{2,1,0:T(8,128)(2,1)S(1)} %all-to-all-done) | copy-start | bytes 2359300
  41.8 8.8 %collective-permute-start.3 = (bf16[512,768]{1,0:T(8,128)(2,1)S(1)}, bf16[512,768]{1,0:T(8,128)(2,1)}, u32[]{:S(2)}, u32[]{:S(2)}) collective-permute-start(bf16[512,768]{1,0:T(8,128)(2,1)S(1)} %bitcast.203), channel_id=1, source_target_pairs={{0,1},{1,0},{2,3},{3,2},{4,5},{5,4},{6,7},{7,6},{8,9},{9,8},{10,11... | collective-permute-start | bytes 2359304 | tf_op jit(solution)/shard_map/ppermute | solution.py:1219
  42.8 6.6 %collective-permute-start.14 = (bf16[4,64,768]{2,1,0:T(8,128)(2,1)}, bf16[4,64,768]{2,1,0:T(8,128)(2,1)}, u32[]{:S(2)}, u32[]{:S(2)}) collective-permute-start(bf16[4,64,768]{2,1,0:T(8,128)(2,1)} %dynamic-slice_bitcast_fusion.3), channel_id=1, source_target_pairs={{0,1},{1,0},{2,3},{3,2},{4,5},{5,4},{6,7},{7,6},{8,9},{9,8},{10,11... | collective-permute-start | bytes 1179656 | tf_op jit(solution)/shard_map/ppermute | solution.py:1219
  46.1 26.9 %collective-permute-start.18 = (bf16[192,3072]{1,0:T(8,128)(2,1)}, bf16[192,3072]{1,0:T(8,128)(2,1)}, u32[]{:S(2)}, u32[]{:S(2)}) collective-permute-start(bf16[192,3072]{1,0:T(8,128)(2,1)} %refs_4_.1), channel_id=1, source_target_pairs={{0,1},{1,0},{2,3},{3,2},{4,5},{5,4},{6,7},{7,6},{8,9},{9,8},{10,11... | collective-permute-start | bytes 3538952 | tf_op jit(solution)/shard_map/ppermute | solution.py:1219
  46.3 26.7 %collective-permute-start.19 = (bf16[768,768]{1,0:T(8,128)(2,1)S(1)}, bf16[768,768]{1,0:T(8,128)(2,1)}, u32[]{:S(2)}, u32[]{:S(2)}) collective-permute-start(bf16[768,768]{1,0:T(8,128)(2,1)S(1)} %copy-done.3), channel_id=1, source_target_pairs={{0,1},{1,0},{2,3},{3,2},{4,5},{5,4},{6,7},{7,6},{8,9},{9,8},{10,11... | collective-permute-start | bytes 3538952 | tf_op jit(solution)/shard_map/ppermute | solution.py:1219
  49.4 11.0 %collective-permute-start.10 = (bf16[96,3072]{1,0:T(8,128)(2,1)}, bf16[96,3072]{1,0:T(8,128)(2,1)}, u32[]{:S(2)}, u32[]{:S(2)}) collective-permute-start(bf16[96,3072]{1,0:T(8,128)(2,1)} %collective-permute-done.2.refs_3_), channel_id=1, source_target_pairs={{0,1},{1,0},{2,3},{3,2},{4,5},{5,4},{6,7},{7,6},{8,9},{9,8},{10,11... | collective-permute-start | bytes 1769480 | tf_op jit(solution)/shard_map/ppermute | solution.py:1219
  50.6 22.4 %collective-permute-start.15 = (bf16[96,3072]{1,0:T(8,128)(2,1)S(1)}, bf16[96,3072]{1,0:T(8,128)(2,1)}, u32[]{:S(2)}, u32[]{:S(2)}) collective-permute-start(bf16[96,3072]{1,0:T(8,128)(2,1)S(1)} %dynamic-slice_bitcast_fusion.1), channel_id=1, source_target_pairs={{0,2},{2,0},{1,3},{3,1},{4,6},{6,4},{5,7},{7,5},{8,10},{10,8},{9,1... | collective-permute-start | bytes 1769480 | tf_op jit(solution)/shard_map/ppermute | solution.py:1222
  53.7 47.1 %all-to-all-start.1 = ((bf16[8,64,768]{2,1,0:T(8,128)(2,1)}), bf16[8,64,768]{2,1,0:T(8,128)(2,1)S(1)}, u32[]{:S(2)}, u32[]{:S(2)}) async-start(bf16[8,64,768]{2,1,0:T(8,128)(2,1)} %bitcast.45), calls=%async_computation.1 | async-start | bytes 1572864 | tf_op jit(solution)/shard_map/all_to_all | solution.py:1240
  59.2 13.8 %collective-permute-start.16 = (bf16[192,768]{1,0:T(8,128)(2,1)S(1)}, bf16[192,768]{1,0:T(8,128)(2,1)}, u32[]{:S(2)}, u32[]{:S(2)}) collective-permute-start(bf16[192,768]{1,0:T(8,128)(2,1)S(1)} %copy-done.10), channel_id=1, source_target_pairs={{0,2},{2,0},{1,3},{3,1},{4,6},{6,4},{5,7},{7,5},{8,10},{10,8},{9,1... | collective-permute-start | bytes 884744 | tf_op jit(solution)/shard_map/ppermute | solution.py:1222
  60.4 12.5 %collective-permute-start.17 = (bf16[192,768]{1,0:T(8,128)(2,1)S(1)}, bf16[192,768]{1,0:T(8,128)(2,1)}, u32[]{:S(2)}, u32[]{:S(2)}) collective-permute-start(bf16[192,768]{1,0:T(8,128)(2,1)S(1)} %copy-done.25), channel_id=1, source_target_pairs={{0,1},{1,0},{2,3},{3,2},{4,5},{5,4},{6,7},{7,6},{8,9},{9,8},{10,11... | collective-permute-start | bytes 884744 | tf_op jit(solution)/shard_map/ppermute | solution.py:1219
  61.3 14.6 %copy-start.26 = (bf16[192,768]{1,0:T(8,128)(2,1)S(1)}, bf16[192,768]{1,0:T(8,128)(2,1)}, u32[]{:S(2)}) copy-start(bf16[192,768]{1,0:T(8,128)(2,1)} %refs_0_.3) | copy-start | bytes 884740
  73.1 23.3 %collective-permute-start.23 = (bf16[384,768]{1,0:T(8,128)(2,1)S(1)}, bf16[384,768]{1,0:T(8,128)(2,1)S(1)}, u32[]{:S(2)}, u32[]{:S(2)}) collective-permute-start(bf16[384,768]{1,0:T(8,128)(2,1)S(1)} %slice.127), channel_id=1, source_target_pairs={{0,2},{2,0},{1,3},{3,1},{4,6},{6,4},{5,7},{7,5},{8,10},{10,8},{9,1... | collective-permute-start | bytes 1769480 | tf_op jit(solution)/shard_map/ppermute | solution.py:1222
  74.0 22.4 %collective-permute-start.21 = (bf16[96,3072]{1,0:T(8,128)(2,1)}, bf16[96,3072]{1,0:T(8,128)(2,1)S(1)}, u32[]{:S(2)}, u32[]{:S(2)}) collective-permute-start(bf16[96,3072]{1,0:T(8,128)(2,1)} %collective-permute-done.15.refs_6_), channel_id=1, source_target_pairs={{0,4},{4,0},{8,12},{12,8},{16,20},{20,16},{24,28},{28,24},{1,5},{5... | collective-permute-start | bytes 1769480 | tf_op jit(solution)/shard_map/ppermute | solution.py:1225
  76.0 19.3 %collective-permute-start.20 = (bf16[192,768]{1,0:T(8,128)(2,1)S(1)}, bf16[192,768]{1,0:T(8,128)(2,1)}, u32[]{:S(2)}, u32[]{:S(2)}) collective-permute-start(bf16[192,768]{1,0:T(8,128)(2,1)S(1)} %copy-done.26), channel_id=1, source_target_pairs={{0,2},{2,0},{1,3},{3,1},{4,6},{6,4},{5,7},{7,5},{8,10},{10,8},{9,1... | collective-permute-start | bytes 884744 | tf_op jit(solution)/shard_map/ppermute | solution.py:1222
  77.2 19.1 %collective-permute-start.22 = (bf16[192,768]{1,0:T(8,128)(2,1)}, bf16[192,768]{1,0:T(8,128)(2,1)}, u32[]{:S(2)}, u32[]{:S(2)}) collective-permute-start(bf16[192,768]{1,0:T(8,128)(2,1)} %collective-permute-done.16.refs_12_), channel_id=1, source_target_pairs={{0,4},{4,0},{8,12},{12,8},{16,20},{20,16},{24,28},{28,24},{1,5},{5... | collective-permute-start | bytes 884744 | tf_op jit(solution)/shard_map/ppermute | solution.py:1225
  94.7 2.3 collective-permute-start.13
  95.3 5.2 %collective-permute-start.25 = (bf16[96,3072]{1,0:T(8,128)(2,1)}, bf16[96,3072]{1,0:T(8,128)(2,1)}, u32[]{:S(2)}, u32[]{:S(2)}) collective-permute-start(bf16[96,3072]{1,0:T(8,128)(2,1)} %collective-permute-done.15.refs_6_), channel_id=1, source_target_pairs={{0,1},{1,0},{2,3},{3,2},{4,5},{5,4},{6,7},{7,6},{8,9},{9,8},{10,11... | collective-permute-start | bytes 1769480 | tf_op jit(solution)/shard_map/ppermute | solution.py:1219
  96.3 1.9 collective-permute-start.27
  96.4 4.4 %collective-permute-start.26 = (bf16[96,3072]{1,0:T(8,128)(2,1)S(1)}, bf16[96,3072]{1,0:T(8,128)(2,1)S(1)}, u32[]{:S(2)}, u32[]{:S(2)}) collective-permute-start(bf16[96,3072]{1,0:T(8,128)(2,1)S(1)} %collective-permute-done.21.refs_7_), channel_id=1, source_target_pairs={{0,1},{1,0},{2,3},{3,2},{4,5},{5,4},{6,7},{7,6},{8,9},{9,8},{10,11... | collective-permute-start | bytes 1769480 | tf_op jit(solution)/shard_map/ppermute | solution.py:1219
  96.9 3.9 collective-permute-start.29
  97.0 3.4 collective-permute-start.24
  98.3 2.5 collective-permute-start.28
  134.3 8.5 %collective-permute-start.30 = (bf16[512,384]{1,0:T(8,128)(2,1)}, bf16[512,384]{1,0:T(8,128)(2,1)S(1)}, u32[]{:S(2)}, u32[]{:S(2)}) collective-permute-start(bf16[512,384]{1,0:T(8,128)(2,1)} %get-tuple-element.156), channel_id=1, source_target_pairs={{0,1},{1,0},{2,3},{3,2},{4,5},{5,4},{6,7},{7,6},{8,9},{9,8},{10,11... | collective-permute-start | bytes 1179656 | tf_op jit(solution)/shard_map/ppermute | solution.py:1219
  142.8 13.1 %collective-permute-start.32 = (bf16[2,2,2,2,240,384]{5,4,3,2,1,0:T(8,128)(2,1)}, bf16[2,2,2,2,240,384]{5,4,3,2,1,0:T(8,128)(2,1)S(1)}, u32[]{:S(2)}, u32[]{:S(2)}) collective-permute-start(bf16[2,2,2,2,240,384]{5,4,3,2,1,0:T(8,128)(2,1)} %get-tuple-element.166), channel_id=1, source_target_pairs={{0,1},{1,0},{2,3},{3,2},{4,5},{5,4},{6,7},{7,6},{8,9},{9,8},{10,11... | collective-permute-start | bytes 8847368 | tf_op jit(solution)/shard_map/ppermute | solution.py:1219
  151.0 4.9 %collective-permute-start.31 = (bf16[2,2,2,2,192,384]{5,4,3,2,1,0:T(8,128)(2,1)}, bf16[2,2,2,2,192,384]{5,4,3,2,1,0:T(8,128)(2,1)}, u32[]{:S(2)}, u32[]{:S(2)}) collective-permute-start(bf16[2,2,2,2,192,384]{5,4,3,2,1,0:T(8,128)(2,1)} %get-tuple-element.164), channel_id=1, source_target_pairs={{0,1},{1,0},{2,3},{3,2},{4,5},{5,4},{6,7},{7,6},{8,9},{9,8},{10,11... | collective-permute-start | bytes 7077896 | tf_op jit(solution)/shard_map/ppermute | solution.py:1219
  165.9 36.0 %collective-permute-start.33 = (bf16[8,432,384]{2,1,0:T(8,128)(2,1)}, bf16[8,432,384]{2,1,0:T(8,128)(2,1)S(1)}, u32[]{:S(2)}, u32[]{:S(2)}) collective-permute-start(bf16[8,432,384]{2,1,0:T(8,128)(2,1)} %get-tuple-element.167), channel_id=1, source_target_pairs={{0,2},{1,5},{2,0},{3,7},{4,6},{5,1},{6,4},{7,3},{8,10},{9,13},{10,... | collective-permute-start | bytes 7962632 | tf_op jit(solution)/shard_map/ppermute | solution.py:1378
  206.6 24.9 %collective-permute-start.35 = (bf16[2,2,432,384]{3,2,1,0:T(8,128)(2,1)S(1)}, bf16[2,2,432,384]{3,2,1,0:T(8,128)(2,1)}, u32[]{:S(2)}, u32[]{:S(2)}) collective-permute-start(bf16[2,2,432,384]{3,2,1,0:T(8,128)(2,1)S(1)} %get-tuple-element.229), channel_id=1, source_target_pairs={{0,8},{1,3},{2,10},{3,1},{4,12},{5,7},{6,14},{7,5},{8,0},{9,11},{1... | collective-permute-start | bytes 3981320 | tf_op jit(solution)/shard_map/ppermute | solution.py:1378
  231.1 3.1 collective-permute-start.34
  231.1 22.8 %collective-permute-start.36 = (bf16[2,2,2,6,48,384]{5,4,3,2,1,0:T(8,128)(2,1)}, bf16[2,2,2,6,48,384]{5,4,3,2,1,0:T(8,128)(2,1)}, u32[]{:S(2)}, u32[]{:S(2)}) collective-permute-start(bf16[2,2,2,6,48,384]{5,4,3,2,1,0:T(8,128)(2,1)} %get-tuple-element.179), channel_id=1, source_target_pairs={{0,2},{1,5},{2,0},{3,7},{4,6},{5,1},{6,4},{7,3},{8,10},{9,13},{10,... | collective-permute-start | bytes 5308424 | tf_op jit(solution)/shard_map/ppermute | solution.py:1378
  236.6 63.1 %all-to-all-start.2 = ((bf16[8,2,64,768]{3,2,1,0:T(8,128)(2,1)}), bf16[8,2,64,768]{3,2,1,0:T(8,128)(2,1)S(1)}, u32[]{:S(2)}, u32[]{:S(2)}) async-start(bf16[8,2,64,768]{3,2,1,0:T(8,128)(2,1)} %pad_maximum_fusion), calls=%async_computation.2 | async-start | bytes 3145728 | tf_op jit(solution)/shard_map/all_to_all | solution.py:1240
  240.6 35.0 %collective-permute-start.38 = (bf16[2,432,384]{2,1,0:T(8,128)(2,1)}, bf16[2,432,384]{2,1,0:T(8,128)(2,1)}, u32[]{:S(2)}, u32[]{:S(2)}) collective-permute-start(bf16[2,432,384]{2,1,0:T(8,128)(2,1)} %get-tuple-element.235), channel_id=1, source_target_pairs={{0,4},{1,9},{2,6},{3,11},{4,0},{5,13},{6,2},{7,15},{8,12},{9,1},{1... | collective-permute-start | bytes 1990664 | tf_op jit(solution)/shard_map/ppermute | solution.py:1378
  257.2 22.5 %copy-start.13 = (f32[16,768]{1,0:T(8,128)S(1)}, f32[16,768]{1,0:T(8,128)}, u32[]{:S(2)}) copy-start(f32[16,768]{1,0:T(8,128)} %get-tuple-element.204) | copy-start | bytes 147460
  257.2 31.9 %collective-permute-start.37 = (bf16[2,2,288,384]{3,2,1,0:T(8,128)(2,1)}, bf16[2,2,288,384]{3,2,1,0:T(8,128)(2,1)}, u32[]{:S(2)}, u32[]{:S(2)}) collective-permute-start(bf16[2,2,288,384]{3,2,1,0:T(8,128)(2,1)} %get-tuple-element.232), channel_id=1, source_target_pairs={{0,8},{1,3},{2,10},{3,1},{4,12},{5,7},{6,14},{7,5},{8,0},{9,11},{1... | collective-permute-start | bytes 2654216 | tf_op jit(solution)/shard_map/ppermute | solution.py:1378
  277.6 14.3 %collective-permute-start.40 = (bf16[432,384]{1,0:T(8,128)(2,1)}, bf16[432,384]{1,0:T(8,128)(2,1)}, u32[]{:S(2)}, u32[]{:S(2)}) collective-permute-start(bf16[432,384]{1,0:T(8,128)(2,1)} %get-tuple-element.247), channel_id=1, source_target_pairs={{0,16},{1,17},{2,18},{3,19},{4,20},{5,21},{6,22},{7,23},{8,24},{9,... | collective-permute-start | bytes 995336 | tf_op jit(solution)/shard_map/ppermute | solution.py:1378
  290.5 8.4 %collective-permute-start.39 = (bf16[2,288,384]{2,1,0:T(8,128)(2,1)S(1)}, bf16[2,288,384]{2,1,0:T(8,128)(2,1)S(1)}, u32[]{:S(2)}, u32[]{:S(2)}) collective-permute-start(bf16[2,288,384]{2,1,0:T(8,128)(2,1)S(1)} %get-tuple-element.240), channel_id=1, source_target_pairs={{0,4},{1,9},{2,6},{3,11},{4,0},{5,13},{6,2},{7,15},{8,12},{9,1},{1... | collective-permute-start | bytes 1327112 | tf_op jit(solution)/shard_map/ppermute | solution.py:1378
  293.0 16.6 %collective-permute-start.43 = (bf16[432,384]{1,0:T(8,128)(2,1)S(1)}, bf16[432,384]{1,0:T(8,128)(2,1)S(1)}, u32[]{:S(2)}, u32[]{:S(2)}) collective-permute-start(bf16[432,384]{1,0:T(8,128)(2,1)S(1)} %add_convert_fusion.9), channel_id=1, source_target_pairs={{0,16},{1,17},{2,18},{3,19},{4,20},{5,21},{6,22},{7,23},{8,24},{9,... | collective-permute-start | bytes 995336 | tf_op jit(solution)/shard_map/ppermute | solution.py:1378
  299.7 10.1 %slice-start.1 = ((f32[6,2,384]{2,1,0:T(2,128)}), f32[1,2,384]{2,1,0:T(2,128)S(1)}, s32[]{:S(2)}) async-start(f32[6,2,384]{2,1,0:T(2,128)} %broadcast_select_fusion.2), calls=%async_computation.5 | async-start | bytes 6144 | tf_op jit(solution)/shard_map/slice | solution.py:1434
  299.7 10.2 %slice-start.2 = ((f32[6,2,384]{2,1,0:T(2,128)}), f32[4,2,384]{2,1,0:T(2,128)S(1)}, s32[]{:S(2)}) async-start(f32[6,2,384]{2,1,0:T(2,128)} %broadcast_select_fusion.2), calls=%async_computation.6 | async-start | bytes 24576 | tf_op jit(solution)/shard_map/slice | solution.py:1436
  299.7 10.3 %copy-start.12 = (f32[6,4,192]{2,1,0:T(4,128)S(1)}, f32[6,4,192]{2,1,0:T(4,128)}, u32[]{:S(2)}) copy-start(f32[6,4,192]{2,1,0:T(4,128)} %concatenate.39) | copy-start | bytes 55300
  299.7 10.3 %copy-start.11 = (bf16[288,384]{1,0:T(8,128)(2,1)S(1)}, bf16[288,384]{1,0:T(8,128)(2,1)}, u32[]{:S(2)}) copy-start(bf16[288,384]{1,0:T(8,128)(2,1)} %get-tuple-element.255) | copy-start | bytes 663556
  309.7 15.0 %collective-permute-start.45 = (bf16[2,432,384]{2,1,0:T(8,128)(2,1)S(1)}, bf16[2,432,384]{2,1,0:T(8,128)(2,1)}, u32[]{:S(2)}, u32[]{:S(2)}) collective-permute-start(bf16[2,432,384]{2,1,0:T(8,128)(2,1)S(1)} %pad_maximum_fusion.7), channel_id=1, source_target_pairs={{0,4},{1,9},{2,6},{3,11},{4,0},{5,13},{6,2},{7,15},{8,12},{9,1},{1... | collective-permute-start | bytes 1990664 | tf_op jit(solution)/shard_map/ppermute | solution.py:1378
  310.0 11.9 %collective-permute-start.42 = (bf16[288,384]{1,0:T(8,128)(2,1)S(1)}, bf16[288,384]{1,0:T(8,128)(2,1)S(1)}, u32[]{:S(2)}, u32[]{:S(2)}) collective-permute-start(bf16[288,384]{1,0:T(8,128)(2,1)S(1)} %copy-done.11), channel_id=1, source_target_pairs={{0,16},{1,17},{2,18},{3,19},{4,20},{5,21},{6,22},{7,23},{8,24},{9,... | collective-permute-start | bytes 663560 | tf_op jit(solution)/shard_map/ppermute | solution.py:1378
  311.1 33.5 %all-to-all-start.3 = ((f32[32,16,192]{2,1,0:T(8,128)}), f32[32,16,192]{2,1,0:T(8,128)S(1)}, u32[]{:S(2)}, u32[]{:S(2)}) async-start(f32[32,16,192]{2,1,0:T(8,128)} %bitcast.90), calls=%async_computation.3 | async-start | bytes 1048576 | tf_op jit(solution)/shard_map/all_to_all | solution.py:1439
  322.0 26.2 %collective-permute-start.44 = (bf16[288,384]{1,0:T(8,128)(2,1)S(1)}, bf16[288,384]{1,0:T(8,128)(2,1)S(1)}, u32[]{:S(2)}, u32[]{:S(2)}) collective-permute-start(bf16[288,384]{1,0:T(8,128)(2,1)S(1)} %add_convert_fusion.12), channel_id=1, source_target_pairs={{0,16},{1,17},{2,18},{3,19},{4,20},{5,21},{6,22},{7,23},{8,24},{9,... | collective-permute-start | bytes 663560 | tf_op jit(solution)/shard_map/ppermute | solution.py:1378
  348.3 13.1 %collective-permute-start.46 = (bf16[2,288,384]{2,1,0:T(8,128)(2,1)S(1)}, bf16[2,288,384]{2,1,0:T(8,128)(2,1)S(1)}, u32[]{:S(2)}, u32[]{:S(2)}) collective-permute-start(bf16[2,288,384]{2,1,0:T(8,128)(2,1)S(1)} %pad_maximum_fusion.8), channel_id=1, source_target_pairs={{0,4},{1,9},{2,6},{3,11},{4,0},{5,13},{6,2},{7,15},{8,12},{9,1},{1... | collective-permute-start | bytes 1327112 | tf_op jit(solution)/shard_map/ppermute | solution.py:1378
  350.5 19.7 %collective-permute-start.48 = (bf16[2,2,432,384]{3,2,1,0:T(8,128)(2,1)}, bf16[2,2,432,384]{3,2,1,0:T(8,128)(2,1)}, u32[]{:S(2)}, u32[]{:S(2)}) collective-permute-start(bf16[2,2,432,384]{3,2,1,0:T(8,128)(2,1)} %pad_maximum_fusion.1), channel_id=1, source_target_pairs={{0,8},{1,5},{2,10},{3,7},{4,12},{5,1},{6,14},{7,3},{8,0},{9,13},{1... | collective-permute-start | bytes 3981320 | tf_op jit(solution)/shard_map/ppermute | solution.py:1378
  361.6 17.9 %collective-permute-start.47 = (bf16[2,2,288,384]{3,2,1,0:T(8,128)(2,1)S(1)}, bf16[2,2,288,384]{3,2,1,0:T(8,128)(2,1)S(1)}, u32[]{:S(2)}, u32[]{:S(2)}) collective-permute-start(bf16[2,2,288,384]{3,2,1,0:T(8,128)(2,1)S(1)} %pad_maximum_fusion.3), channel_id=1, source_target_pairs={{0,8},{1,5},{2,10},{3,7},{4,12},{5,1},{6,14},{7,3},{8,0},{9,13},{1... | collective-permute-start | bytes 2654216 | tf_op jit(solution)/shard_map/ppermute | solution.py:1378
  363.2 20.0 %collective-permute-start.41 = (bf16[4,2,64,768]{3,2,1,0:T(8,128)(2,1)}, bf16[4,2,64,768]{3,2,1,0:T(8,128)(2,1)}, u32[]{:S(2)}, u32[]{:S(2)}) collective-permute-start(bf16[4,2,64,768]{3,2,1,0:T(8,128)(2,1)} %dynamic-slice_bitcast_fusion), channel_id=1, source_target_pairs={{0,1},{1,0},{2,3},{3,2},{4,5},{5,4},{6,7},{7,6},{8,9},{9,8},{10,11... | collective-permute-start | bytes 2359304 | tf_op jit(solution)/shard_map/ppermute | solution.py:1219
  381.2 5.3 %collective-permute-start.49 = (bf16[2,2,288,384]{3,2,1,0:T(8,128)(2,1)}, bf16[2,2,288,384]{3,2,1,0:T(8,128)(2,1)S(1)}, u32[]{:S(2)}, u32[]{:S(2)}) collective-permute-start(bf16[2,2,288,384]{3,2,1,0:T(8,128)(2,1)} %get-tuple-element.230), channel_id=1, source_target_pairs={{0,1},{1,0},{2,3},{3,2},{4,5},{5,4},{6,7},{7,6},{8,9},{9,8},{10,11... | collective-permute-start | bytes 2654216 | tf_op jit(solution)/shard_map/ppermute | solution.py:1219
  (27 other events, 119.6 us)
